TPU v7x, 32 devices: a whole 2x2x4 slice. The times are simulated.
32 devices in a mesh: seq: 4 (over y, x), batch: 8 (over z, core).
Axes of the slice: x: 2, y: 2, z: 4, core: 2. Of those that a mesh axis runs over, the one named last changes fastest.
Arguments:
- layer_input: bfloat16 [8, 2048, 768], P('batch', 'seq'), may hold values from -6 to 6
- w_query: bfloat16 [768, 768], replicated, may hold values from -0.3125 to 0.3125
- b_query: bfloat16 [768], replicated, may hold values from -3 to 3
- w_key: bfloat16 [768, 768], replicated, may hold values from -0.3125 to 0.3125
- b_key: bfloat16 [768], replicated, may hold values from -3 to 3
- w_value: bfloat16 [768, 768], replicated, may hold values from -0.21875 to 0.21875
- b_value: bfloat16 [768], replicated, may hold values from -3 to 3
- w_out: bfloat16 [768, 768], replicated, may hold values from -1.75 to 1.75
- b_out: bfloat16 [768], replicated, may hold values from -3 to 3
- gain_attn: bfloat16 [768], replicated, may hold values from 0.5 to 1.5
- shift_attn: bfloat16 [768], replicated, may hold values from -1.75 to 1.75
- w_in: bfloat16 [768, 3072], replicated, may hold values from -0.21875 to 0.21875
- b_in: bfloat16 [3072], replicated, may hold values from -3 to 3
- w_down: bfloat16 [3072, 768], replicated, may hold values from -0.109375 to 0.109375
- b_down: bfloat16 [768], replicated, may hold values from -1.75 to 1.75
- gain_ffn: bfloat16 [768], replicated, may hold values from 0.5 to 1.5
- shift_ffn: bfloat16 [768], replicated, may hold values from -1.75 to 1.75
- rel_table: bfloat16 [512, 768], replicated, may hold values from -6 to 6
- segment_ids: int32 [8, 2048], P('batch'), may hold values from 0 to 3, never falling along the last dimension, each value on 1 to 1024 neighbouring positions
- cotangent: bfloat16 [8, 2048, 768], P('batch', 'seq'), may hold values from -8 to 8
Outputs:
- layer_out: bfloat16 [8, 2048, 768], P('batch', 'seq')
- input_grad: float32 [8, 2048, 768], P('batch', 'seq')
- w_query_grad: float32 [768, 768], P('batch')
- b_query_grad: float32 [768], P('batch')
- w_key_grad: float32 [768, 768], P('batch')
- b_key_grad: float32 [768], P('batch')
- w_value_grad: float32 [768, 768], P('batch')
- b_value_grad: float32 [768], P('batch')
- w_out_grad: float32 [768, 768], P('batch')
- b_out_grad: float32 [768], P('batch')
- gain_attn_grad: float32 [768], P('batch')
- shift_attn_grad: float32 [768], P('batch')
- w_in_grad: float32 [768, 3072], P('batch')
- b_in_grad: float32 [3072], P('batch')
- w_down_grad: float32 [3072, 768], P('batch')
- b_down_grad: float32 [768], P('batch')
- gain_ffn_grad: float32 [768], P('batch')
- shift_ffn_grad: float32 [768], P('batch')
- rel_table_grad: float32 [512, 768], P(('seq', 'batch'))
Inputs may be any that keep to these rules, and one draw needn't show every extreme that they name: `segment_ids`: within each row the document number never falls; each document has 1 to 1024 positions, and some document has exactly that many.
All inputs are finite; a program needn't handle non-finite values.
Results may differ from a plain program's by a relative error of at most 0.03.
Values may be sent and summed in bfloat16 or wider, within the bound.
A program may use at most 320 MiB of HBM per device.

v0:
```python
import functools
import math

import jax
import jax.numpy as jnp
from jax import lax
from jax.experimental import pallas as pl
from jax.experimental.pallas import tpu as pltpu
from jax.sharding import PartitionSpec as P

HEADS = 12
F32 = jnp.float32
BF = jnp.bfloat16
NN = (((1,), (0,)), ((), ()))
NT = (((1,), (1,)), ((), ()))
TN = (((0,), (0,)), ((), ()))


def dot(a, b, dims=NN):
    return lax.dot_general(a, b, dims, preferred_element_type=F32)


def head_lanes(x, hh):
    lane = lax.broadcasted_iota(jnp.int32, x.shape, len(x.shape) - 1)
    keep = (lane < 64) if hh == 0 else (lane >= 64)
    return jnp.where(keep, x.astype(F32), 0.0).astype(x.dtype)


def fwd_kernel(tq, span, scale, q_ref, k_ref, v_ref, rk_ref, rq_ref, qid_ref, kid_ref, ctx_ref, p_ref, bias_ref, rqm_ref):
    nq = q_ref.shape[0] // tq
    win = tq + 2 * span
    nw = win // tq
    factor = scale * math.log2(math.e)

    @pl.when(pl.program_id(0) == 0)
    def _():
        dist = (
            lax.broadcasted_iota(jnp.int32, (tq, win), 0)
            - lax.broadcasted_iota(jnp.int32, (tq, win), 1)
            + span
        )
        near = jnp.abs(dist) < span
        for qt in range(nq):
            qid = qid_ref[qt * tq : (qt + 1) * tq, :]
            kid = kid_ref[:, qt * tq : qt * tq + win]
            bias_ref[qt] = jnp.where(near & (qid == kid), 0.0, -1e30)

    for hh in range(2):
        rqm_ref[hh] = head_lanes(rq_ref[...], hh)

    def tile(qt, carry):
        row = pl.multiple_of(qt * tq, tq)
        qb = q_ref[pl.ds(row, tq), :]
        kwin = k_ref[pl.ds(row, win), :]
        vwin = v_ref[pl.ds(row, win), :]
        outs = []
        for hh in range(2):
            qm = head_lanes(qb, hh)
            logits = dot(qm, kwin, NT)
            toward = dot(qm, rk_ref[...], NT)
            logits = logits + pltpu.roll(toward, 1, 1, stride=1, stride_axis=0)
            parts = []
            for wt in range(nw):
                u = dot(
                    kwin[wt * tq : (wt + 1) * tq],
                    rqm_ref[hh, 2 * span - tq * wt : 2 * span - tq * wt + 2 * tq, :],
                    NT,
                )
                u = pltpu.roll(u, tq + 1, 1, stride=1, stride_axis=0)[:, :tq]
                parts.append(u.T)
            logits = (logits + jnp.concatenate(parts, axis=1)) * factor + bias_ref[qt]
            top = jnp.max(logits, axis=-1, keepdims=True)
            expos = jnp.exp2(logits - top)
            total = jnp.sum(expos, axis=-1, keepdims=True)
            probs = (expos * (1.0 / total)).astype(BF)
            p_ref[hh, pl.ds(row, tq), :] = probs
            outs.append(dot(probs, vwin))
        lane = lax.broadcasted_iota(jnp.int32, outs[0].shape, 1)
        ctx_ref[pl.ds(row, tq), :] = jnp.where(lane < 64, outs[0], outs[1]).astype(BF)
        return carry

    lax.fori_loop(0, nq, tile, 0)


def attn_fwd(tq, span, q, k, v, rk, rq, qid, kid):
    block, width = q.shape
    ext = k.shape[0]
    win = tq + 2 * span
    scale = (3.0 * 64) ** -0.5
    rk = jnp.pad(rk, ((0, tq), (0, 0)))
    rq = jnp.pad(rq, ((tq, tq), (0, 0)))
    col = lambda rows: pl.BlockSpec((rows, 128), lambda h: (0, h))
    whole = lambda shape: pl.BlockSpec(shape, lambda h: (0, 0))
    return pl.pallas_call(
        functools.partial(fwd_kernel, tq, span, scale),
        grid=(HEADS // 2,),
        out_shape=(
            jax.ShapeDtypeStruct((block, width), BF),
            jax.ShapeDtypeStruct((HEADS, block, win), BF),
        ),
        in_specs=[col(block), col(ext), col(ext), col(rk.shape[0]), col(rq.shape[0]), whole((block, 1)), whole((1, ext))],
        out_specs=(col(block), pl.BlockSpec((2, block, win), lambda h: (h, 0, 0))),
        scratch_shapes=[
            pltpu.VMEM((block // tq, tq, win), F32),
            pltpu.VMEM((2, rq.shape[0], 128), BF),
        ],
        compiler_params=pltpu.CompilerParams(vmem_limit_bytes=48 << 20),
        cost_estimate=pl.CostEstimate(flops=20_000_000_000, bytes_accessed=10 << 20, transcendentals=HEADS * block * win),
        name="attn_fwd",
    )(q, k, v, rk, rq, qid, kid)


def anti(n):
    r = lax.broadcasted_iota(jnp.int32, (n, n), 0)
    c = lax.broadcasted_iota(jnp.int32, (n, n), 1)
    return jnp.where(r + c == n - 1, 1.0, 0.0).astype(BF)


def bwd_kernel(tq, span, scale, q_ref, k_ref, v_ref, g_ref, rk_ref, rq_ref, p_ref,
               dq_ref, dk_ref, dv_ref, drk_ref, drq_ref,
               km_ref, vm_ref, rkm_ref, rqm_ref, kjt_ref, dk_acc, dvt_acc, drkt_acc, drqt_acc):
    nq = q_ref.shape[0] // tq
    ext = k_ref.shape[0]
    nk = ext // tq
    win = tq + 2 * span
    nw = win // tq
    flip = anti(tq)
    for hh in range(2):
        km_ref[hh] = head_lanes(k_ref[...], hh)
        rkm_ref[hh] = head_lanes(rk_ref[...], hh)
        rqm_ref[hh] = head_lanes(rq_ref[...], hh)
    for kt in range(nk):
        kjt_ref[kt] = dot(k_ref[kt * tq : (kt + 1) * tq, :], flip, TN).astype(BF)
    dk_acc[...] = jnp.zeros_like(dk_acc)
    dvt_acc[...] = jnp.zeros_like(dvt_acc)
    drkt_acc[...] = jnp.zeros_like(drkt_acc)
    drqt_acc[...] = jnp.zeros_like(drqt_acc)

    def tile(qt, carry):
        row = pl.multiple_of(qt * tq, tq)
        qb = q_ref[pl.ds(row, tq), :]
        gb = g_ref[pl.ds(row, tq), :]
        qjt = dot(qb, flip, TN).astype(BF)
        gt = gb.astype(F32).T.astype(BF)
        vwin = v_ref[pl.ds(row, win), :]
        dq_r = jnp.zeros((tq, 128), F32)
        for hh in range(2):
            lo, hi = 64 * hh, 64 * hh + 64
            qm = head_lanes(qb, hh)
            gm = head_lanes(gb, hh)
            probs = p_ref[hh, pl.ds(row, tq), :]
            gp = dot(gm, vwin, NT)
            p32 = probs.astype(F32)
            t = p32 * gp
            rows = jnp.sum(t, axis=-1, keepdims=True)
            ds = ((t - p32 * rows) * scale).astype(BF)
            dvt_acc[lo:hi, pl.ds(row, win)] += dot(gt[lo:hi], probs)
            dsj = dot(flip, ds)
            dt = pltpu.roll(dsj, win - tq, 1, stride=1, stride_axis=0).astype(BF)
            dq_r = dq_r + dot(dsj.astype(BF), km_ref[hh, pl.ds(row, win), :]) + dot(dt, rkm_ref[hh])
            drkt_acc[lo:hi, :] += dot(qjt[lo:hi], dt)
            for wt in range(nw):
                dst = dot(flip, ds[:, wt * tq : (wt + 1) * tq], NT)
                du = pltpu.roll(
                    jnp.concatenate([dst, jnp.zeros_like(dst)], axis=1), 0, 1, stride=1, stride_axis=0
                ).astype(BF)
                s0 = 2 * span - tq * wt
                dk_acc[qt + wt] += dot(dst.astype(BF), qm) + dot(du, rqm_ref[hh, s0 : s0 + 2 * tq, :])
                drqt_acc[lo:hi, s0 : s0 + 2 * tq] += dot(kjt_ref[qt + wt, lo:hi, :], du)
        dq_ref[pl.ds(row, tq), :] = dot(flip, dq_r.astype(BF)).astype(BF)
        return carry

    lax.fori_loop(0, nq, tile, 0)
    for kt in range(nk):
        dk_ref[kt * tq : (kt + 1) * tq, :] = dot(flip, dk_acc[kt].astype(BF)).astype(BF)
        dv_ref[kt * tq : (kt + 1) * tq, :] = dvt_acc[:, kt * tq : (kt + 1) * tq].T.astype(BF)
    for st in range(2 * span // 128):
        drk_ref[st * 128 : (st + 1) * 128, :] = drkt_acc[:, st * 128 : (st + 1) * 128].T.astype(BF)
        drq_ref[st * 128 : (st + 1) * 128, :] = drqt_acc[:, tq + st * 128 : tq + (st + 1) * 128].T.astype(BF)


def attn_bwd(tq, span, q, k, v, g, rk, rq, probs):
    block, width = q.shape
    ext = k.shape[0]
    win = tq + 2 * span
    scale = (3.0 * 64) ** -0.5
    rk = jnp.pad(rk, ((0, tq), (0, 0)))
    rq = jnp.pad(rq, ((tq, tq), (0, 0)))
    col = lambda rows: pl.BlockSpec((rows, 128), lambda h: (0, h))
    return pl.pallas_call(
        functools.partial(bwd_kernel, tq, span, scale),
        grid=(HEADS // 2,),
        out_shape=(
            jax.ShapeDtypeStruct((block, width), BF),
            jax.ShapeDtypeStruct((ext, width), BF),
            jax.ShapeDtypeStruct((ext, width), BF),
            jax.ShapeDtypeStruct((2 * span, width), BF),
            jax.ShapeDtypeStruct((2 * span, width), BF),
        ),
        in_specs=[col(block), col(ext), col(ext), col(block), col(rk.shape[0]), col(rq.shape[0]),
                  pl.BlockSpec((2, block, win), lambda h: (h, 0, 0))],
        out_specs=(col(block), col(ext), col(ext), col(2 * span), col(2 * span)),
        scratch_shapes=[
            pltpu.VMEM((2, ext, 128), BF),
            pltpu.VMEM((2, ext, 128), BF),
            pltpu.VMEM((2, rk.shape[0], 128), BF),
            pltpu.VMEM((2, rq.shape[0], 128), BF),
            pltpu.VMEM((ext // tq, 128, tq), BF),
            pltpu.VMEM((ext // tq, tq, 128), F32),
            pltpu.VMEM((128, ext), F32),
            pltpu.VMEM((128, rk.shape[0]), F32),
            pltpu.VMEM((128, rq.shape[0]), F32),
        ],
        compiler_params=pltpu.CompilerParams(vmem_limit_bytes=48 << 20),
        cost_estimate=pl.CostEstimate(flops=50_000_000_000, bytes_accessed=20 << 20, transcendentals=0),
        name="attn_bwd",
    )(q, k, v, g, rk, rq, probs)


NORM_EPS = 1e-07


def norm_rows(values):
    centred = values - jnp.mean(values, axis=-1, keepdims=True)
    inv_std = lax.rsqrt(jnp.mean(centred * centred, axis=-1, keepdims=True) + NORM_EPS)
    return centred * inv_std, inv_std


def norm_back(grads, normed, inv_std):
    first_mean = jnp.mean(grads, axis=-1, keepdims=True)
    second_mean = jnp.mean(grads * normed, axis=-1, keepdims=True)
    return inv_std * (grads - first_mean - normed * second_mean)


def reduced(grad):
    part = lax.psum_scatter(grad.astype(BF), "batch", scatter_dimension=0, tiled=True)
    return lax.psum(part, "seq").astype(F32)


def local(
    layer_input,
    w_query,
    b_query,
    w_key,
    b_key,
    w_value,
    b_value,
    w_out,
    b_out,
    gain_attn,
    shift_attn,
    w_in,
    b_in,
    w_down,
    b_down,
    gain_ffn,
    shift_ffn,
    rel_table,
    segment_ids,
    cotangent,
):
    rows, block, width = layer_input.shape
    span = rel_table.shape[0] // 2
    tq = span
    x = layer_input[0]
    count = lax.axis_size("seq")
    up = [(i, i + 1) for i in range(count - 1)]
    down = [(i + 1, i) for i in range(count - 1)]
    before = lax.ppermute(x[block - span :], "seq", up)
    after = lax.ppermute(x[:span], "seq", down)
    rel_flip = dot(anti(2 * span), rel_table).astype(BF)

    def project(rows_in, weight, bias):
        return (dot(rows_in, weight) + bias).astype(BF)

    q = project(x, w_query, b_query)
    rk = project(rel_flip, w_key, b_key)
    rq = project(rel_flip, w_query, b_query)
    x_ext = jnp.concatenate([before, x, after], axis=0)
    k = project(x_ext, w_key, b_key)
    v = project(x_ext, w_value, b_value)
    start = lax.axis_index("seq") * block
    padded = jnp.pad(segment_ids[0], (span, span), constant_values=-1)
    kid = lax.dynamic_slice_in_dim(padded, start, block + 2 * span, 0)
    qid = kid[span : span + block]
    context, probs = attn_fwd(tq, span, q, k, v, rk, rq, qid[:, None], kid[None])

    residual_one = x.astype(F32) + dot(context, w_out) + b_out
    normed_one, inv_one = norm_rows(residual_one)
    hidden = normed_one * gain_attn + shift_attn
    hidden_low = hidden.astype(BF)
    pre_act = dot(hidden_low, w_in) + b_in
    phi = 0.5 * (1.0 + lax.erf(pre_act * (0.5**0.5)))
    act_low = (pre_act * phi).astype(BF)
    slope = phi + pre_act * (jnp.exp(-0.5 * pre_act * pre_act) * ((2.0 * math.pi) ** -0.5))
    residual_two = hidden + dot(act_low, w_down) + b_down
    normed_two, inv_two = norm_rows(residual_two)
    output = (normed_two * gain_ffn + shift_ffn).astype(BF)

    grad_out = cotangent[0].astype(F32)
    gain_ffn_grad = jnp.sum(grad_out * normed_two, axis=0)
    shift_ffn_grad = jnp.sum(grad_out, axis=0)
    grad_two = norm_back(grad_out * gain_ffn, normed_two, inv_two)
    grad_branch = grad_two.astype(BF)
    down_grad = dot(act_low, grad_branch, TN)
    down_bias_grad = jnp.sum(grad_branch.astype(F32), axis=0)
    grad_pre = (dot(grad_branch, w_down, NT) * slope).astype(BF)
    in_grad = dot(hidden_low, grad_pre, TN)
    in_bias_grad = jnp.sum(grad_pre.astype(F32), axis=0)
    grad_hidden = grad_two + dot(grad_pre, w_in, NT)
    gain_attn_grad = jnp.sum(grad_hidden * normed_one, axis=0)
    shift_attn_grad = jnp.sum(grad_hidden, axis=0)
    grad_one = norm_back(grad_hidden * gain_attn, normed_one, inv_one)
    grad_attn = grad_one.astype(BF)
    out_grad = dot(context, grad_attn, TN)
    out_bias_grad = jnp.sum(grad_attn.astype(F32), axis=0)
    grad_context = dot(grad_attn, w_out, NT).astype(BF)

    dq, dk, dv, drk, drq = attn_bwd(tq, span, q, k, v, grad_context, rk, rq, probs)

    dx = dot(dk, w_key, NT) + dot(dv, w_value, NT)
    from_after = lax.ppermute(dx[:span].astype(BF), "seq", down)
    from_before = lax.ppermute(dx[span + block :].astype(BF), "seq", up)
    input_grad = grad_one + dx[span : span + block] + dot(dq, w_query, NT)
    edge = jnp.zeros((block - span, width), F32)
    input_grad = (
        input_grad
        + jnp.concatenate([from_before.astype(F32), edge], axis=0)
        + jnp.concatenate([edge, from_after.astype(F32)], axis=0)
    )
    query_grad = dot(x, dq, TN) + dot(rel_flip, drq, TN)
    key_grad = dot(x_ext, dk, TN) + dot(rel_flip, drk, TN)
    value_grad = dot(x_ext, dv, TN)

    def total(*parts):
        return sum(jnp.sum(part.astype(F32), axis=0) for part in parts)

    query_bias_grad = total(dq, drq)
    key_bias_grad = total(dk, drk)
    value_bias_grad = total(dv)
    rel_part = (dot(drk, w_key, NT) + dot(drq, w_query, NT)).astype(BF)
    rel_part = dot(anti(2 * span), rel_part).astype(BF)
    rel_grad = lax.psum_scatter(rel_part, ("seq", "batch"), scatter_dimension=0, tiled=True).astype(F32)
    small = [
        query_bias_grad, key_bias_grad, value_bias_grad, out_bias_grad, gain_attn_grad,
        shift_attn_grad, down_bias_grad, gain_ffn_grad, shift_ffn_grad, in_bias_grad,
    ]
    share = lax.axis_size("batch")
    packed = jnp.concatenate([vec.reshape(share, -1) for vec in small], axis=1)
    packed = reduced(packed)[0]
    cuts = []
    at = 0
    for vec in small:
        size = vec.shape[0] // share
        cuts.append(packed[at : at + size])
        at += size
    (qb, kb, vb, ob, ga, sa, db, gf, sf, ib) = cuts
    return (
        output[None],
        input_grad[None],
        reduced(query_grad),
        qb,
        reduced(key_grad),
        kb,
        reduced(value_grad),
        vb,
        reduced(out_grad),
        ob,
        ga,
        sa,
        reduced(in_grad),
        ib,
        reduced(down_grad),
        db,
        gf,
        sf,
        rel_grad,
    )


def solution(mesh):
    tokens = P("batch", "seq", None)
    in_specs = (tokens,) + (P(),) * 17 + (P("batch", None), tokens)
    matrix, vector = P("batch", None), P("batch")
    out_specs = (
        (tokens, tokens)
        + (matrix, vector) * 4
        + (vector, vector)
        + (matrix, vector) * 2
        + (vector, vector, P(("seq", "batch"), None))
    )
    return jax.shard_map(local, mesh=mesh, in_specs=in_specs, out_specs=out_specs, check_vma=False)
```

profile of v0, /device:TPU:8, one launch (start us, length us, event | category | flops | bytes accessed | tf_op | source)
XLA Modules:
  0.0 601.1 jit_solution(16177296802572976089)
XLA Ops:
  9.3 4.3 collective-permute-start
  20.5 2.5 pad.19.rq_ref
  24.9 6.9 %collective-permute-done.1 = bf16[256,768]{1,0:T(8,128)(2,1)} collective-permute-done((bf16[256,768]{1,0:T(8,128)(2,1)S(1)}, bf16[256,768]{1,0:T(8,128)(2,1)}, u32[]{:S(2)}, u32[]{:S(2)}) %collective-permute-start.1) | collective-permute-done | bytes 393248 | tf_op jit(solution)/shard_map/ppermute | solution.py:270
  31.8 2.6 add_convert_fusion.1.k_ref
  34.5 3.1 add_convert_fusion.v_ref
  37.6 39.7 %attn_fwd.1 = (bf16[512,768]{1,0:T(8,128)(2,1)S(1)}, bf16[12,512,768]{2,1,0:T(8,128)(2,1)}) custom-call(bf16[512,768]{1,0:T(8,128)(2,1)S(1)} %add_convert_fusion.7.q_ref, bf16[1024,768]{1,0:T(8,128)(2,1)S(1)} %add_convert_fusion.1.k_ref, bf16[1024,768]{1,0:T(8,128)(2,1)S(1)} %add_convert_fusion.v_ref, bf16[768,768]{1,0:T(8,128)(2,1)S(1)} %pad.18.rk_ref, ...), custom_call_target="tpu_custom_call" | custom-call | flops 20000000000 | bytes 10485760 | tf_op jit(solution)/shard_map/attn_fwd/pallas_call | solution.py:94
  78.6 6.4 %multiply_convert_fusion = (bf16[512,3072]{1,0:T(8,128)(2,1)S(1)}, f32[512,3072]{1,0:T(8,128)S(1)}) fusion(f32[3072]{0:T(1024)S(1)} %convert_element_type.186, bf16[768,3072]{1,0:T(8,128)(2,1)} %param.31, f32[512,768]{1,0:T(8,128)S(1)} %get-tuple-element.122, f32[768]{0:T(1024)S(1)} %convert_element_type.184, f32[768]{0:T(1024)S(1)} %convert_element_type.183, ...), kind=kOutput, calls=%fused_computation.7 | convolution fusion | flops 2427322368 | bytes 15751168 | tf_op jit(solution)/shard_map/dot_general | solution.py:20
  85.0 2.7 fusion.45
  88.9 2.1 fusion.13
  92.2 6.5 %fusion.47 = (bf16[3072]{0:T(1024)(128)(2,1)}, bf16[512,3072]{1,0:T(8,128)(2,1)}) fusion(f32[512,3072]{1,0:T(8,128)S(1)} %get-tuple-element.124, f32[3072]{0:T(1024)S(1)} %copy-done.22, bf16[3072,768]{1,0:T(8,128)(2,1)S(1)} %bitcast.93, f32[512,768]{1,0:T(8,128)S(1)} %get-tuple-element.104), kind=kOutput, calls=%fused_computation.112 | convolution fusion | flops 2435183616 | bytes 15747072 | tf_op jit(solution)/shard_map/dot_general | solution.py:20
  98.6 5.6 multiply_reduce_fusion
  105.9 60.8 %attn_bwd.1 = (bf16[512,768]{1,0:T(8,128)(2,1)S(1)}, bf16[1024,768]{1,0:T(8,128)(2,1)}, bf16[1024,768]{1,0:T(8,128)(2,1)}, bf16[512,768]{1,0:T(8,128)(2,1)S(1)}, bf16[512,768]{1,0:T(8,128)(2,1)S(1)}) custom-call(bf16[512,768]{1,0:T(8,128)(2,1)S(1)} %add_convert_fusion.7.q_ref, bf16[1024,768]{1,0:T(8,128)(2,1)} %copy-done.2, bf16[1024,768]{1,0:T(8,128)(2,1)} %copy-done.3, ...), custom_call_target="tpu_custom_call" | custom-call | flops 49999998976 | bytes 20971520 | tf_op jit(solution)/shard_map/attn_bwd/pallas_call | solution.py:190
  169.7 2.4 copy.48
  172.1 3.5 convolution_convert_fusion.2
  176.1 4.4 convolution_convert_fusion.3
  182.7 3.7 add_convert_fusion.2
  186.5 7.2 %convolution_convert_fusion = bf16[3072,768]{1,0:T(8,128)(2,1)} fusion(bf16[512,3072]{1,0:T(8,128)(2,1)} %copy-done.46, f32[512,768]{1,0:T(8,128)} %copy-done.15), kind=kOutput, calls=%fused_computation.9 | convolution fusion | flops 2418671616 | bytes 9437184 | tf_op jit(solution)/shard_map/dot_general | solution.py:20
  194.3 7.5 %convolution_convert_fusion.1 = bf16[768,3072]{1,0:T(8,128)(2,1)} fusion(bf16[512,3072]{1,0:T(8,128)(2,1)} %get-tuple-element.131, f32[512,768]{1,0:T(8,128)} %copy-done.7, f32[768]{0:T(1024)} %copy-done.30, f32[768]{0:T(1024)S(1)} %convert_element_type.183, f32[512]{0:T(512)S(1)} %copy-done.24, f32[512]{0:T(512)S(1)} %broadcast_multiply_fusion.5), kind=kOutput, calls=%fused_computation.10 | convolution fusion | flops 2420244480 | bytes 9447424 | tf_op jit(solution)/shard_map/dot_general | solution.py:20
  206.5 4.0 convolution_convert_fusion.5
  213.1 3.1 fusion.48
  218.0 16.8 %reduce-scatter.14.cloned.1.call-done = bf16[96,768]{1,0:T(8,128)(2,1)} async-done(((bf16[768,768]{1,0:T(8,128)(2,1)}), bf16[96,768]{1,0:T(8,128)(2,1)}) %reduce-scatter.14.cloned.1.call-update) | async-done | bytes 147472 | tf_op jit(solution)/shard_map/reduce_scatter | solution.py:236
  234.8 33.4 %reduce-scatter.12.cloned.1.call-done = bf16[96,768]{1,0:T(8,128)(2,1)} async-done(((bf16[768,768]{1,0:T(8,128)(2,1)}), bf16[96,768]{1,0:T(8,128)(2,1)}) %reduce-scatter.12.cloned.1.call-update) | async-done | bytes 147472 | tf_op jit(solution)/shard_map/reduce_scatter | solution.py:236
  268.2 33.7 %reduce-scatter.10.cloned.1.call-done = bf16[96,768]{1,0:T(8,128)(2,1)} async-done(((bf16[768,768]{1,0:T(8,128)(2,1)}), bf16[96,768]{1,0:T(8,128)(2,1)}) %reduce-scatter.10.cloned.1.call-update) | async-done | bytes 147472 | tf_op jit(solution)/shard_map/reduce_scatter | solution.py:236
  301.9 55.7 %reduce-scatter.18.cloned.1.call-done = bf16[384,768]{1,0:T(8,128)(2,1)} async-done(((bf16[3072,768]{1,0:T(8,128)(2,1)}), bf16[384,768]{1,0:T(8,128)(2,1)}) %reduce-scatter.18.cloned.1.call-update) | async-done | bytes 589840 | tf_op jit(solution)/shard_map/reduce_scatter | solution.py:236
  357.6 55.5 %reduce-scatter.16.cloned.1.call-done = bf16[96,3072]{1,0:T(8,128)(2,1)} async-done(((bf16[768,3072]{1,0:T(8,128)(2,1)}), bf16[96,3072]{1,0:T(8,128)(2,1)}) %reduce-scatter.16.cloned.1.call-update) | async-done | bytes 589840 | tf_op jit(solution)/shard_map/reduce_scatter | solution.py:236
  424.7 5.3 fusion.46
  431.0 4.6 collective-permute-start.2
  438.4 25.8 %all-reduce.5 = bf16[8,1248]{1,0:T(8,128)(2,1)} all-reduce(bf16[8,1248]{1,0:T(8,128)(2,1)} %concatenate.22), channel_id=3, replica_groups=mesh['seq'=4,'batch'=8] {'batch'}, use_global_device_ids=true, to_apply=%region_22.23.clone | all-reduce | flops 9984 | bytes 39936
  465.5 11.2 %psum.50 = bf16[1,1248]{1,0:T(2,128)(2,1)S(1)} all-reduce(bf16[1,1248]{1,0:T(2,128)(2,1)S(1)} %constant_dynamic-slice_fusion), channel_id=1, replica_groups=mesh['seq'=4,'batch'=8] {'seq'}, use_global_device_ids=true, to_apply=%region_23.24 | all-reduce | flops 1248 | bytes 4992 | tf_op jit(solution)/shard_map/psum | solution.py:237
  478.0 3.9 fusion.17
  482.0 33.3 %reduce-scatter.20.cloned.1.call-done = bf16[16,768]{1,0:T(8,128)(2,1)} async-done(((bf16[512,768]{1,0:T(8,128)(2,1)}), bf16[16,768]{1,0:T(8,128)(2,1)}) %reduce-scatter.20.cloned.1.call-update) | async-done | bytes 24592 | tf_op jit(solution)/shard_map/reduce_scatter | solution.py:343
  516.6 68.4 %all-reduce.9.cloned.1.call-done = (bf16[96,768]{0,1:T(8,128)(2,1)}, bf16[96,768]{1,0:T(8,128)(2,1)}, bf16[96,768]{1,0:T(8,128)(2,1)}, bf16[96,768]{1,0:T(8,128)...) async-done(((bf16[96,768]{0,1:T(8,128)(2,1)}, bf16[96,768]{1,0:T(8,128)(2,1)}, bf16[96,768]{1,0:T(8,128)(2,1)}, bf16[96,768]{1,0:T(8,128)(2,1)}, ...) | async-done | bytes 1769488 | tf_op jit(solution)/shard_map/psum | solution.py:237
  (195 shorter events, 59.5 us)
Async XLA Ops:
  7.2 11.1 %copy-start = (bf16[768,768]{1,0:T(8,128)(2,1)S(1)}, bf16[768,768]{1,0:T(8,128)(2,1)}, u32[]{:S(2)}) copy-start(bf16[768,768]{1,0:T(8,128)(2,1)} %param.23) | copy-start | bytes 3538948
  7.2 7.6 %copy-start.35 = (bf16[768]{0:T(1024)(128)(2,1)S(1)}, bf16[768]{0:T(1024)(128)(2,1)}, u32[]{:S(2)}) copy-start(bf16[768]{0:T(1024)(128)(2,1)} %param.22) | copy-start | bytes 4612
  7.2 7.6 %copy-start.36 = (bf16[768]{0:T(1024)(128)(2,1)S(1)}, bf16[768]{0:T(1024)(128)(2,1)}, u32[]{:S(2)}) copy-start(bf16[768]{0:T(1024)(128)(2,1)} %param.24) | copy-start | bytes 4612
  7.2 208.9 %reduce-scatter.22.cloned.1.call-start = ((), (), s32[]{:S(2)}) async-start(), calls=%async_computation.13 | async-start | bytes 1327104
  9.3 7.3 %copy-start.16 = (bf16[768,768]{1,0:T(8,128)(2,1)S(1)}, bf16[768,768]{1,0:T(8,128)(2,1)}, u32[]{:S(2)}) copy-start(bf16[768,768]{1,0:T(8,128)(2,1)} %param.21) | copy-start | bytes 3538948
  9.3 15.6 %collective-permute-start = (bf16[256,768]{1,0:T(8,128)(2,1)}, bf16[256,768]{1,0:T(8,128)(2,1)}, u32[]{:S(2)}, u32[]{:S(2)}) collective-permute-start(bf16[256,768]{1,0:T(8,128)(2,1)} %get-tuple-element.110), channel_id=1, source_target_pairs={{0,8},{8,16},{16,24},{1,9},{9,17},{17,25},{2,10},{10,18},{18,26},{... | collective-permute-start | bytes 1179656 | tf_op jit(solution)/shard_map/ppermute | solution.py:269
  13.5 18.3 %collective-permute-start.1 = (bf16[256,768]{1,0:T(8,128)(2,1)S(1)}, bf16[256,768]{1,0:T(8,128)(2,1)}, u32[]{:S(2)}, u32[]{:S(2)}) collective-permute-start(bf16[256,768]{1,0:T(8,128)(2,1)S(1)} %get-tuple-element.111), channel_id=1, source_target_pairs={{8,0},{16,8},{24,16},{9,1},{17,9},{25,17},{10,2},{18,10},{26,18},{... | collective-permute-start | bytes 1179656 | tf_op jit(solution)/shard_map/ppermute | solution.py:270
  20.2 64.8 %copy-start.30 = (f32[768]{0:T(1024)}, f32[768]{0:T(1024)S(1)}, u32[]{:S(2)}) copy-start(f32[768]{0:T(1024)S(1)} %convert_element_type.184) | copy-start | bytes 9220
  20.3 58.2 %copy-start.21 = (f32[3072]{0:T(1024)}, f32[3072]{0:T(1024)S(1)}, u32[]{:S(2)}) copy-start(f32[3072]{0:T(1024)S(1)} %convert_element_type.186) | copy-start | bytes 36868
  24.1 7.8 %copy-start.32 = (f32[768]{0:T(1024)S(1)}, f32[768]{0:T(1024)}, u32[]{:S(2)}) copy-start(f32[768]{0:T(1024)} %copy-done.31) | copy-start | bytes 9220
  37.6 39.8 %copy-start.3 = (bf16[1024,768]{1,0:T(8,128)(2,1)}, bf16[1024,768]{1,0:T(8,128)(2,1)S(1)}, u32[]{:S(2)}) copy-start(bf16[1024,768]{1,0:T(8,128)(2,1)S(1)} %add_convert_fusion.v_ref) | copy-start | bytes 4718596
  37.6 39.7 %copy-start.44 = (bf16[768,768]{1,0:T(8,128)(2,1)S(1)}, bf16[768,768]{1,0:T(8,128)(2,1)}, u32[]{:S(2)}) copy-start(bf16[768,768]{1,0:T(8,128)(2,1)} %param.27) | copy-start | bytes 3538948
  78.2 26.0 %copy-start.7 = (f32[512,768]{1,0:T(8,128)}, f32[512,768]{1,0:T(8,128)S(1)}, u32[]{:S(2)}) copy-start(f32[512,768]{1,0:T(8,128)S(1)} %get-tuple-element.122) | copy-start | bytes 4718596
  78.2 6.8 %slice-start = ((s8[4718592]{0:T(1024)(128)(4,1)}), s8[4194304]{0:T(1024)(128)(4,1)S(1)}, s32[]{:S(2)}) async-start(s8[4718592]{0:T(1024)(128)(4,1)} %bitcast.92), calls=%async_computation.15 | async-start | bytes 8388608
  78.5 25.7 %copy-start.23 = (f32[512]{0:T(512)}, f32[512]{0:T(512)S(1)}, u32[]{:S(2)}) copy-start(f32[512]{0:T(512)S(1)} %add_rsqrt_fusion.1) | copy-start | bytes 6148
  91.0 7.6 %slice-start.2 = ((s8[4718592]{0:T(1024)(128)(4,1)}), s8[4194304]{0:T(1024)(128)(4,1)S(1)}, s32[]{:S(2)}) async-start(s8[4718592]{0:T(1024)(128)(4,1)} %bitcast.94), calls=%async_computation.17 | async-start | bytes 8388608
  92.2 6.5 %copy-start.15 = (f32[512,768]{1,0:T(8,128)}, f32[512,768]{1,0:T(8,128)S(1)}, u32[]{:S(2)}) copy-start(f32[512,768]{1,0:T(8,128)S(1)} %get-tuple-element.104) | copy-start | bytes 4718596
  92.2 6.5 %slice-start.3 = ((s8[4718592]{0:T(1024)(128)(4,1)}), s8[524288]{0:T(1024)(128)(4,1)S(1)}, s32[]{:S(2)}) async-start(s8[4718592]{0:T(1024)(128)(4,1)} %bitcast.94), calls=%async_computation.18 | async-start | bytes 1048576
  172.1 62.7 %reduce-scatter.14.cloned.1.call-start = ((), (), s32[]{:S(2)}) async-start(), calls=%async_computation.9 | async-start | bytes 1327104 | tf_op jit(solution)/shard_map/reduce_scatter | solution.py:236
  175.6 92.6 %reduce-scatter.12.cloned.1.call-start = ((), (), s32[]{:S(2)}) async-start(), calls=%async_computation.8 | async-start | bytes 1327104 | tf_op jit(solution)/shard_map/reduce_scatter | solution.py:236
  180.5 121.4 %reduce-scatter.10.cloned.1.call-start = ((), (), s32[]{:S(2)}) async-start(), calls=%async_computation.7 | async-start | bytes 1327104 | tf_op jit(solution)/shard_map/reduce_scatter | solution.py:236
  186.4 171.2 %reduce-scatter.18.cloned.1.call-start = ((), (), s32[]{:S(2)}) async-start(), calls=%async_computation.11 | async-start | bytes 5308416 | tf_op jit(solution)/shard_map/reduce_scatter | solution.py:236
  193.7 219.5 %reduce-scatter.16.cloned.1.call-start = ((), (), s32[]{:S(2)}) async-start(), calls=%async_computation.10 | async-start | bytes 5308416 | tf_op jit(solution)/shard_map/reduce_scatter | solution.py:236
  201.8 313.4 %reduce-scatter.20.cloned.1.call-start = ((), (), s32[]{:S(2)}) async-start(), calls=%async_computation.12 | async-start | bytes 811008 | tf_op jit(solution)/shard_map/reduce_scatter | solution.py:343
  210.5 374.5 %all-reduce.9.cloned.1.call-start = ((), (), s32[]{:S(2)}) async-start(), calls=%async_computation.14 | async-start | bytes 3637248 | tf_op jit(solution)/shard_map/psum | solution.py:237
  216.2 197.6 %copy-start.8 = (bf16[1024,768]{1,0:T(8,128)(2,1)S(1)}, bf16[1024,768]{1,0:T(8,128)(2,1)}, u32[]{:S(2)}) copy-start(bf16[1024,768]{1,0:T(8,128)(2,1)} %get-tuple-element.29) | copy-start | bytes 4718596
  430.1 6.8 %copy-start.26 = (bf16[8,96]{1,0:T(8,128)(2,1)S(1)}, bf16[8,96]{1,0:T(8,128)(2,1)}, u32[]{:S(2)}) copy-start(bf16[8,96]{1,0:T(8,128)(2,1)} %reshape.149) | copy-start | bytes 4612
  430.1 6.8 %copy-start.27 = (bf16[8,96]{1,0:T(8,128)(2,1)S(1)}, bf16[8,96]{1,0:T(8,128)(2,1)}, u32[]{:S(2)}) copy-start(bf16[8,96]{1,0:T(8,128)(2,1)} %reshape.148) | copy-start | bytes 4612
  430.1 48.0 %copy-start.5 = (f32[512,768]{1,0:T(8,128)S(1)}, f32[512,768]{1,0:T(8,128)}, u32[]{:S(2)}) copy-start(f32[512,768]{1,0:T(8,128)} %copy-done.4) | copy-start | bytes 4718596
  431.0 47.0 %collective-permute-start.2 = (bf16[256,768]{1,0:T(8,128)(2,1)}, bf16[256,768]{1,0:T(8,128)(2,1)}, u32[]{:S(2)}, u32[]{:S(2)}) collective-permute-start(bf16[256,768]{1,0:T(8,128)(2,1)} %get-tuple-element.108), channel_id=1, source_target_pairs={{0,8},{8,16},{16,24},{1,9},{9,17},{17,25},{2,10},{10,18},{18,26},{... | collective-permute-start | bytes 1179656 | tf_op jit(solution)/shard_map/ppermute | solution.py:323
  435.6 42.4 %collective-permute-start.3 = (bf16[256,768]{1,0:T(8,128)(2,1)}, bf16[256,768]{1,0:T(8,128)(2,1)}, u32[]{:S(2)}, u32[]{:S(2)}) collective-permute-start(bf16[256,768]{1,0:T(8,128)(2,1)} %get-tuple-element.109), channel_id=1, source_target_pairs={{8,0},{16,8},{24,16},{9,1},{17,9},{25,17},{10,2},{18,10},{26,18},{... | collective-permute-start | bytes 1179656 | tf_op jit(solution)/shard_map/ppermute | solution.py:322
  585.0 6.8 %copy-start.20 = (bf16[96,3072]{1,0:T(8,128)(2,1)S(1)}, bf16[96,3072]{1,0:T(8,128)(2,1)}, u32[]{:S(2)}) copy-start(bf16[96,3072]{1,0:T(8,128)(2,1)} %get-tuple-element.101) | copy-start | bytes 1769476
  (31 other events, 68.5 us)
Sparse Core Ops, SparseCore 0:
  172.2 28.9 reduce-scatter.21
  203.5 31.2 reduce-scatter.13
  237.1 31.0 reduce-scatter.11
  270.9 30.9 reduce-scatter.9
  304.1 53.5 reduce-scatter.17
  359.8 53.3 reduce-scatter.15
  418.3 96.9 reduce-scatter.19
  519.6 65.3 all-reduce.8
where the time goes:
time: 608 us; the launch traced here: 601 us
  waiting for transfers between devices  304 us (50%)
  Pallas kernels  100 us (16%)
  matrix products  83.7 us (14%)
  blocking collectives  37 us (6%)
  local copies, waits for them, and re-layouts  31.6 us (5%)
  other arithmetic  17 us (3%)
  between operations  15.1 us (2%)
  starting transfers between devices  12.3 us (2%)
    reduce_scatter x5, waiting for transfers between devices, reduced(): lax.psum_scatter(grad.astype(BF), 'batch', scatter_dimension=0, tiled=True)  195 us
    dot_general x25, matrix products, dot(): return lax.dot_general(a, b, dims, preferred_element_type=F32)  83.7 us
    psum x1, waiting for transfers between devices, reduced(): return lax.psum(part, 'seq').astype(F32)  68.4 us
    pallas_call x1, Pallas kernels, attn_bwd(): pl.pallas_call(functools.partial(bwd_kernel, tq, span, scale), grid=(HEAD...  60.8 us
    pallas_call x1, Pallas kernels, attn_fwd(): pl.pallas_call(functools.partial(fwd_kernel, tq, span, scale), grid=(HEAD...  39.7 us
    reduce_scatter x1, waiting for transfers between devices, local(): lax.psum_scatter(rel_part, ('seq', 'batch'), scatter_dimension=0, tiled=T...  33.3 us
    unnamed x1, blocking collectives  25.8 us
    unnamed x107, local copies, waits for them, and re-layouts  12.5 us
  transfers between devices with their start and end apart: 12, of which 8 were waited for; matrix products, arithmetic and copies ran while one was open for 13% of the time, Pallas kernels for 0%

commit v1 on v0

--- a/solution.py
+++ b/solution.py
@@ -217,6 +217,253 @@
     )(q, k, v, g, rk, rq, probs)
 
 
+MESH = pl.DeviceIdType.MESH
+
+
+class Reducer:
+    def __init__(self, ns, nb, shapes, width):
+        self.ns, self.nb, self.nz, self.width = ns, nb, nb // 2, width
+        self.bits = ns.bit_length() - 1
+        self.moves = []
+        self.places = []
+        at = 0
+        for index, (share, cols) in enumerate(shapes):
+            room = -(-share // 16) * 16
+            self.places.append((at, room))
+            for part in range(cols // width):
+                self.moves.append((index, part, at, share))
+                at += room
+        unit = 16 * 2 * ns
+        self.rows = -(-at // unit) * unit
+        self.piece = self.rows // (2 * ns)
+
+    def scratch(self):
+        nz, rows, width, piece = self.nz, self.rows, self.width, self.piece
+        shapes = [pltpu.VMEM((nz, rows, width), BF), pltpu.VMEM((nz, rows, width), BF)]
+        for level in range(self.bits):
+            shapes.append(pltpu.VMEM((2, nz, rows // 4 >> level, width), BF))
+        shapes += [pltpu.VMEM((2, nz - 1, piece, width), BF), pltpu.VMEM((rows, width), BF)]
+        moves = len(self.moves)
+        dma = pltpu.SemaphoreType.DMA
+        shapes += [dma((moves,)), dma((2, moves)), dma((2, 2, self.bits)), dma((2, 2, nz - 1)), dma((2, 2, self.ns - 1))]
+        return shapes
+
+    def bind(self, sources, scratch):
+        self.sources = sources
+        self.mine, self.first = scratch[0], scratch[1]
+        self.halves = scratch[2 : 2 + self.bits]
+        self.across, self.final = scratch[2 + self.bits : 4 + self.bits]
+        self.own_sem, self.core_sem, self.seq_sem, self.z_sem, self.out_sem = scratch[4 + self.bits :]
+        self.s = lax.axis_index("seq")
+        self.b = lax.axis_index("batch")
+        self.z = self.b // 2
+        self.c = self.b % 2
+        self.base = [0, self.rows // 2]
+        self.size = self.rows // 2
+        self.started = []
+
+    def toggled(self, value, mask):
+        out = value
+        for bit in range(mask.bit_length()):
+            if mask >> bit & 1:
+                out = out + (1 - 2 * ((value // (1 << bit)) % 2)) * (1 << bit)
+        return out
+
+    def peers(self):
+        yield (self.s, self.toggled(self.b, 1))
+        for step in range(1, self.nz):
+            yield (self.s, self.toggled(self.z, step) * 2 + self.c)
+        for step in range(1, self.ns):
+            yield (self.toggled(self.s, step), self.b)
+
+    def greet(self):
+        barrier = pltpu.get_barrier_semaphore()
+        total = 0
+        for s, b in self.peers():
+            pl.semaphore_signal(barrier, inc=1, device_id={"seq": s, "batch": b}, device_id_type=MESH)
+            total += 1
+        pl.semaphore_wait(barrier, total)
+
+    def own_copies(self):
+        for n, (index, part, at, share) in enumerate(self.moves):
+            columns = pl.ds(part * self.width, self.width)
+            yield pltpu.make_async_copy(
+                self.sources[index].at[:, self.c, :, columns], self.mine.at[:, pl.ds(at, share), :], self.own_sem.at[n]
+            )
+
+    def core_copies(self):
+        for n, (index, part, at, share) in enumerate(self.moves):
+            columns = pl.ds(part * self.width, self.width)
+            yield pltpu.make_async_remote_copy(
+                src_ref=self.sources[index].at[:, 1 - self.c, :, columns],
+                dst_ref=self.first.at[:, pl.ds(at, share), :],
+                send_sem=self.core_sem.at[0, n],
+                recv_sem=self.core_sem.at[1, n],
+                device_id={"seq": self.s, "batch": self.toggled(self.b, 1)},
+                device_id_type=MESH,
+            )
+
+    def region(self, level, half):
+        base, size = half * (self.rows // 2), self.rows // 2
+        sent = base
+        for at in range(level):
+            bit = self.order(half, at)
+            size = size // 2
+            mine = (self.s // (1 << bit)) % 2
+            sent = base + (1 - mine) * size
+            base = base + mine * size
+        return base, sent, size
+
+    def order(self, half, level):
+        return (level + half) % self.bits
+
+    def rows_of(self, start, size):
+        return pl.ds(pl.multiple_of(start, 16), size)
+
+    def seq_copy(self, level, half):
+        unused, sent, size = self.region(level + 1, half)
+        return pltpu.make_async_remote_copy(
+            src_ref=self.mine.at[:, self.rows_of(sent, size), :],
+            dst_ref=self.halves[level].at[half],
+            send_sem=self.seq_sem.at[0, half, level],
+            recv_sem=self.seq_sem.at[1, half, level],
+            device_id={"seq": self.toggled(self.s, 1 << self.order(half, level)), "batch": self.b},
+            device_id_type=MESH,
+        )
+
+    def z_copies(self, half):
+        kept, unused, size = self.region(self.bits, half)
+        for step in range(1, self.nz):
+            other = self.toggled(self.z, step)
+            yield pltpu.make_async_remote_copy(
+                src_ref=self.mine.at[other, self.rows_of(kept, size), :],
+                dst_ref=self.across.at[half, step - 1],
+                send_sem=self.z_sem.at[0, half, step - 1],
+                recv_sem=self.z_sem.at[1, half, step - 1],
+                device_id={"seq": self.s, "batch": other * 2 + self.c},
+                device_id_type=MESH,
+            )
+
+    def out_copies(self, half):
+        kept, unused, size = self.region(self.bits, half)
+        for step in range(1, self.ns):
+            yield pltpu.make_async_remote_copy(
+                src_ref=self.final.at[self.rows_of(kept, size), :],
+                dst_ref=self.final.at[self.rows_of(kept, size), :],
+                send_sem=self.out_sem.at[0, half, step - 1],
+                recv_sem=self.out_sem.at[1, half, step - 1],
+                device_id={"seq": self.toggled(self.s, step), "batch": self.b},
+                device_id_type=MESH,
+            )
+
+    def start_core(self):
+        for copy in self.core_copies():
+            copy.start()
+        for copy in self.own_copies():
+            copy.start()
+
+    def add_core(self):
+        for copy in self.own_copies():
+            copy.wait()
+        for copy in self.core_copies():
+            copy.wait_recv()
+        step = self.rows // 8
+
+        def add(n, carry):
+            z, at = n // 8, pl.multiple_of((n % 8) * step, 16)
+            rows = pl.ds(at, step)
+            self.mine[z, rows, :] = (self.mine[z, rows, :].astype(F32) + self.first[z, rows, :].astype(F32)).astype(BF)
+            return carry
+
+        lax.fori_loop(0, self.nz * 8, add, 0)
+
+    def start_seq(self, level):
+        for half in range(2):
+            self.seq_copy(level, half).start()
+
+    def add_seq(self, level):
+        for half in range(2):
+            self.seq_copy(level, half).wait_recv()
+            kept, unused, size = self.region(level + 1, half)
+            rows = self.rows_of(kept, size)
+
+            def add(z, carry):
+                got = self.halves[level][half, z].astype(F32)
+                self.mine[z, rows, :] = (self.mine[z, rows, :].astype(F32) + got).astype(BF)
+                return carry
+
+            lax.fori_loop(0, self.nz, add, 0)
+
+    def start_z(self):
+        for half in range(2):
+            for copy in self.z_copies(half):
+                copy.start()
+
+    def add_z(self):
+        for half in range(2):
+            for copy in self.z_copies(half):
+                copy.wait_recv()
+            kept, unused, size = self.region(self.bits, half)
+            rows = self.rows_of(kept, size)
+            total = self.mine[self.z, rows, :].astype(F32)
+            for step in range(1, self.nz):
+                total = total + self.across[half, step - 1].astype(F32)
+            self.final[rows, :] = total.astype(BF)
+
+    def start_out(self):
+        for half in range(2):
+            for copy in self.out_copies(half):
+                copy.start()
+
+    def finish(self):
+        for half in range(2):
+            for copy in self.out_copies(half):
+                copy.wait()
+            for copy in self.z_copies(half):
+                copy.wait_send()
+            for level in range(self.bits):
+                self.seq_copy(level, half).wait_send()
+        for copy in self.core_copies():
+            copy.wait_send()
+
+    def unpack(self, packed, index, share, cols):
+        at, room = self.places[index]
+        parts = [packed[at + n * room : at + n * room + share] for n in range(cols // self.width)]
+        return parts[0] if len(parts) == 1 else jnp.concatenate(parts, axis=1)
+
+
+def reduce_kernel(reducer, count, *refs):
+    out = refs[count]
+    reducer.bind(refs[:count], refs[count + 1 :])
+    reducer.greet()
+    reducer.start_core()
+    reducer.add_core()
+    for level in range(reducer.bits):
+        reducer.start_seq(level)
+        reducer.add_seq(level)
+    reducer.start_z()
+    reducer.add_z()
+    reducer.start_out()
+    reducer.finish()
+    out[...] = reducer.final[...]
+
+
+def reduce_all(grads, width):
+    ns, nb = lax.axis_size("seq"), lax.axis_size("batch")
+    shapes = [(grad.shape[0] // nb, grad.shape[1]) for grad in grads]
+    reducer = Reducer(ns, nb, shapes, width)
+    packed = pl.pallas_call(
+        functools.partial(reduce_kernel, reducer, len(grads)),
+        out_shape=jax.ShapeDtypeStruct((reducer.rows, width), BF),
+        in_specs=[pl.BlockSpec(memory_space=pl.ANY)] * len(grads),
+        out_specs=pl.BlockSpec(memory_space=pltpu.VMEM),
+        scratch_shapes=reducer.scratch(),
+        compiler_params=pltpu.CompilerParams(collective_id=0, has_side_effects=True, vmem_limit_bytes=56 << 20),
+        name="reduce_all",
+    )(*[grad.reshape(nb // 2, 2, shape[0], shape[1]) for grad, shape in zip(grads, shapes)])
+    return [reducer.unpack(packed, n, *shape) for n, shape in enumerate(shapes)]
+
+
 NORM_EPS = 1e-07
 
 
@@ -230,11 +477,6 @@
     first_mean = jnp.mean(grads, axis=-1, keepdims=True)
     second_mean = jnp.mean(grads * normed, axis=-1, keepdims=True)
     return inv_std * (grads - first_mean - normed * second_mean)
-
-
-def reduced(grad):
-    part = lax.psum_scatter(grad.astype(BF), "batch", scatter_dimension=0, tiled=True)
-    return lax.psum(part, "seq").astype(F32)
 
 
 def local(
@@ -339,15 +581,22 @@
     key_bias_grad = total(dk, drk)
     value_bias_grad = total(dv)
     rel_part = (dot(drk, w_key, NT) + dot(drq, w_query, NT)).astype(BF)
-    rel_part = dot(anti(2 * span), rel_part).astype(BF)
-    rel_grad = lax.psum_scatter(rel_part, ("seq", "batch"), scatter_dimension=0, tiled=True).astype(F32)
+    share, lanes = lax.axis_size("batch"), lax.axis_size("seq")
+    rel_rows = 2 * span // (share * lanes)
+    order = jnp.arange(2 * span).reshape(lanes, share, rel_rows).transpose(1, 0, 2).reshape(-1)
+    picks = (2 * span - 1 - order)[:, None] == jnp.arange(2 * span)[None]
+    rel_part = dot(picks.astype(BF), rel_part).astype(BF)
     small = [
         query_bias_grad, key_bias_grad, value_bias_grad, out_bias_grad, gain_attn_grad,
         shift_attn_grad, down_bias_grad, gain_ffn_grad, shift_ffn_grad, in_bias_grad,
     ]
-    share = lax.axis_size("batch")
     packed = jnp.concatenate([vec.reshape(share, -1) for vec in small], axis=1)
-    packed = reduced(packed)[0]
+    packed = jnp.pad(packed, ((0, 0), (0, 16 * width - packed.shape[1]))).reshape(share * 16, width)
+    grads = [in_grad, down_grad, out_grad, query_grad, key_grad, value_grad, rel_part, packed]
+    sums = reduce_all([grad.astype(BF) for grad in grads], width)
+    (in_sum, down_sum, out_sum, query_sum, key_sum, value_sum, rel_sum, packed) = [part.astype(F32) for part in sums]
+    rel_sum = lax.dynamic_slice_in_dim(rel_sum, lax.axis_index("seq") * rel_rows, rel_rows, 0)
+    packed = packed.reshape(-1)
     cuts = []
     at = 0
     for vec in small:
@@ -356,25 +605,8 @@
         at += size
     (qb, kb, vb, ob, ga, sa, db, gf, sf, ib) = cuts
     return (
-        output[None],
-        input_grad[None],
-        reduced(query_grad),
-        qb,
-        reduced(key_grad),
-        kb,
-        reduced(value_grad),
-        vb,
-        reduced(out_grad),
-        ob,
-        ga,
-        sa,
-        reduced(in_grad),
-        ib,
-        reduced(down_grad),
-        db,
-        gf,
-        sf,
-        rel_grad,
+        output[None], input_grad[None], query_sum, qb, key_sum, kb, value_sum, vb, out_sum, ob,
+        ga, sa, in_sum, ib, down_sum, db, gf, sf, rel_sum,
     )
 
 

time: 608 us -> 401 us (0.66)
  waiting for transfers between devices: 304 us -> 21.2 us
  Pallas kernels: 100 us -> 254 us
  blocking collectives: 37 us -> 0 us
  between operations: 15.1 us -> 1.53 us
  matrix products: 83.7 us -> 71.7 us
  local copies, waits for them, and re-layouts: 31.6 us -> 23.5 us
    reduce_scatter x6 -> x0, waiting for transfers between devices: 228 us -> none  [the longest x5 195 us: reduced(): lax.psum_scatter(grad.astype(BF), 'batch', scatter_dimension=0, tiled=True)]
    pallas_call x0 -> x1, Pallas kernels: none -> 153 us  [reduce_all(): pl.pallas_call(functools.partial(reduce_kernel, reducer, len(grads)), out...]
    psum x1 -> x0, waiting for transfers between devices: 68.4 us -> none  [reduced(): return lax.psum(part, 'seq').astype(F32)]
    unnamed x1 -> x0, blocking collectives: 25.8 us -> none
    dot_general x25, matrix products: 83.7 us -> 71.7 us  [dot(): return lax.dot_general(a, b, dims, preferred_element_type=F32)]
    psum x1 -> x0, blocking collectives: 11.2 us -> none  [reduced(): return lax.psum(part, 'seq').astype(F32)]
    ppermute x1, waiting for transfers between devices: 0.01 us -> 10.1 us  [local(): from_after = lax.ppermute(dx[:span].astype(BF), 'seq', down)]
    unnamed x107 -> x99, local copies, waits for them, and re-layouts: 12.5 us -> 3.52 us
  transfers between devices with their start and end apart: 12 -> 4, of which waited for: 8 -> 3; matrix products, arithmetic and copies ran while one was open for 13% -> 3% of each run, Pallas kernels for 0% -> 0%
where the time goes in v1:
time: 401 us; the launch traced here: 396 us
  Pallas kernels  254 us (63%)
  matrix products  71.7 us (18%)
  local copies, waits for them, and re-layouts  23.5 us (6%)
  waiting for transfers between devices  21.2 us (5%)
  other arithmetic  13.7 us (3%)
  starting transfers between devices  10.6 us (3%)
    pallas_call x1, Pallas kernels, reduce_all(): pl.pallas_call(functools.partial(reduce_kernel, reducer, len(grads)), out...  153 us
    dot_general x25, matrix products, dot(): return lax.dot_general(a, b, dims, preferred_element_type=F32)  71.7 us
    pallas_call x1, Pallas kernels, attn_bwd(): pl.pallas_call(functools.partial(bwd_kernel, tq, span, scale), grid=(HEAD...  60.8 us
    pallas_call x1, Pallas kernels, attn_fwd(): pl.pallas_call(functools.partial(fwd_kernel, tq, span, scale), grid=(HEAD...  39.6 us
    ppermute x1, waiting for transfers between devices, local(): from_after = lax.ppermute(dx[:span].astype(BF), 'seq', down)  10.1 us
    ppermute x1, waiting for transfers between devices, local(): after = lax.ppermute(x[:span], 'seq', down)  8.08 us
  transfers between devices with their start and end apart: 4, of which 3 were waited for; matrix products, arithmetic and copies ran while one was open for 3% of the time, Pallas kernels for 0%

profile of v1, /device:TPU:8, one launch (start us, length us, event | category | flops | bytes accessed | tf_op | source)
XLA Modules:
  0.0 396.0 jit_solution(14188090547901444164)
XLA Ops:
  0.7 2.2 slice_bitcast_fusion.1
  2.9 4.3 %collective-permute-start = (bf16[256,768]{1,0:T(8,128)(2,1)}, bf16[256,768]{1,0:T(8,128)(2,1)}, u32[]{:S(2)}, u32[]{:S(2)}) collective-permute-start(bf16[256,768]{1,0:T(8,128)(2,1)} %get-tuple-element.55), channel_id=1, source_target_pairs={{0,8},{8,16},{16,24},{1,9},{9,17},{17,25},{2,10},{10,18},{18,26},{... | collective-permute-start | bytes 1179656 | tf_op jit(solution)/shard_map/ppermute | solution.py:511
  15.0 2.4 add_convert_fusion.7.q_ref
  17.4 8.1 %collective-permute-done.1 = bf16[256,768]{1,0:T(8,128)(2,1)} collective-permute-done((bf16[256,768]{1,0:T(8,128)(2,1)}, bf16[256,768]{1,0:T(8,128)(2,1)}, u32[]{:S(2)}, u32[]{:S(2)}) %collective-permute-start.1) | collective-permute-done | bytes 393248 | tf_op jit(solution)/shard_map/ppermute | solution.py:512
  25.5 2.6 add_convert_fusion.1.k_ref
  28.1 3.1 add_convert_fusion.v_ref
  31.2 39.6 %attn_fwd.1 = (bf16[512,768]{1,0:T(8,128)(2,1)S(1)}, bf16[12,512,768]{2,1,0:T(8,128)(2,1)}) custom-call(bf16[512,768]{1,0:T(8,128)(2,1)S(1)} %add_convert_fusion.7.q_ref, bf16[1024,768]{1,0:T(8,128)(2,1)S(1)} %add_convert_fusion.1.k_ref, bf16[1024,768]{1,0:T(8,128)(2,1)S(1)} %add_convert_fusion.v_ref, bf16[768,768]{1,0:T(8,128)(2,1)S(1)} %pad.23.rk_ref, ...), custom_call_target="tpu_custom_call" | custom-call | flops 20000000000 | bytes 10485760 | tf_op jit(solution)/shard_map/attn_fwd/pallas_call | solution.py:94
  72.1 5.8 %multiply_convert_fusion = (bf16[512,3072]{1,0:T(8,128)(2,1)S(1)}, f32[512,3072]{1,0:T(8,128)S(1)}) fusion(f32[3072]{0:T(1024)S(1)} %convert_element_type.188, bf16[768,3072]{1,0:T(8,128)(2,1)} %param.31, f32[512,768]{1,0:T(8,128)S(1)} %get-tuple-element.67, f32[768]{0:T(1024)S(1)} %convert_element_type.186, f32[768]{0:T(1024)S(1)} %convert_element_type.185, ...), kind=kOutput, calls=%fused_computation.7 | convolution fusion | flops 2427322368 | bytes 15751168 | tf_op jit(solution)/shard_map/dot_general | solution.py:20
  77.9 2.8 fusion.42
  81.1 2.1 fusion.13
  83.8 5.6 %fusion.44 = (bf16[3072]{0:T(1024)(128)(2,1)}, bf16[512,3072]{1,0:T(8,128)(2,1)S(1)}) fusion(f32[512,3072]{1,0:T(8,128)S(1)} %get-tuple-element.69, f32[3072]{0:T(1024)S(1)} %convert_element_type.188, bf16[3072,768]{1,0:T(8,128)(2,1)S(1)} %bitcast.92, f32[512,768]{1,0:T(8,128)S(1)} %get-tuple-element.41), kind=kOutput, calls=%fused_computation.108 | convolution fusion | flops 2435183616 | bytes 15747072 | tf_op jit(solution)/shard_map/dot_general | solution.py:20
  89.4 3.6 multiply_reduce_fusion
  95.5 60.8 %attn_bwd.1 = (bf16[512,768]{1,0:T(8,128)(2,1)S(1)}, bf16[1024,768]{1,0:T(8,128)(2,1)}, bf16[1024,768]{1,0:T(8,128)(2,1)}, bf16[512,768]{1,0:T(8,128)(2,1)S(1)}, bf16[512,768]{1,0:T(8,128)(2,1)S(1)}) custom-call(bf16[512,768]{1,0:T(8,128)(2,1)S(1)} %add_convert_fusion.7.q_ref, bf16[1024,768]{1,0:T(8,128)(2,1)} %copy-done.3, bf16[1024,768]{1,0:T(8,128)(2,1)} %copy-done.4, ...), custom_call_target="tpu_custom_call" | custom-call | flops 49999998976 | bytes 20971520 | tf_op jit(solution)/shard_map/attn_bwd/pallas_call | solution.py:190
  156.4 2.0 fusion.47
  158.4 2.2 fusion.46
  160.7 2.3 fusion.24
  162.9 4.8 %convolution_convert_fusion = bf16[3072,768]{1,0:T(8,128)(2,1)} fusion(bf16[512,3072]{1,0:T(8,128)(2,1)S(1)} %copy-done.42, f32[512,768]{1,0:T(8,128)S(1)} %get-tuple-element.41), kind=kOutput, calls=%fused_computation.9 | convolution fusion | flops 2418671616 | bytes 9437184 | tf_op jit(solution)/shard_map/dot_general | solution.py:20
  167.7 1.8 convolution_convert_fusion.3
  170.0 4.8 %convolution_convert_fusion.1 = bf16[768,3072]{1,0:T(8,128)(2,1)} fusion(bf16[512,3072]{1,0:T(8,128)(2,1)S(1)} %copy-done.44, f32[512,768]{1,0:T(8,128)S(1)} %get-tuple-element.67, f32[768]{0:T(1024)S(1)} %copy-done.27, f32[768]{0:T(1024)S(1)} %convert_element_type.185, f32[512]{0:T(512)S(1)} %add_rsqrt_fusion.1, f32[512]{0:T(512)S(1)} %broadcast_multiply_fusion.5), kind=kOutput, calls=%fused_computation.10 | convolution fusion | flops 2420244480 | bytes 9447424 | tf_op jit(solution)/shard_map/dot_general | solution.py:20
  179.1 1.7 reduce.1
  189.3 3.5 fusion.6
  192.8 4.0 %convolution_convert_fusion.6 = bf16[512,768]{1,0:T(8,128)(2,1)} fusion(f32[512,768]{1,0:T(8,128)} %fusion.47, bf16[512,768]{1,0:T(8,128)(2,1)S(1)} %get-tuple-element.31, bf16[768,768]{1,0:T(8,128)(2,1)} %param.21, s32[512]{0:T(512)S(1)} %copy-done.37), kind=kOutput, calls=%fused_computation.56 | convolution fusion | flops 1008074752 | bytes 4327424 | tf_op jit(solution)/shard_map/dot_general | solution.py:20
  196.8 4.3 %convolution_convert_fusion.2 = bf16[768,768]{1,0:T(8,128)(2,1)} fusion(bf16[1024,768]{1,0:T(8,128)(2,1)} %get-tuple-element.29, bf16[256,768]{1,0:T(8,128)(2,1)} %collective-permute-done.1, bf16[512,768]{1,0:T(8,128)(2,1)S(1)} %bitcast.82, bf16[256,768]{1,0:T(8,128)(2,1)} %collective-permute-done), kind=kOutput, calls=%fused_computation.49 | convolution fusion | flops 1213267968 | bytes 4325376 | tf_op jit(solution)/shard_map/dot_general | solution.py:20
  201.1 3.6 add_convert_fusion.2
  204.7 153.3 %reduce_all.1 = bf16[1280,768]{1,0:T(8,128)(2,1)} custom-call(bf16[4,2,96,3072]{3,2,1,0:T(8,128)(2,1)} %bitcast.79, bf16[4,2,384,768]{3,2,1,0:T(8,128)(2,1)} %bitcast.78, bf16[4,2,96,768]{3,2,1,0:T(8,128)(2,1)} %bitcast.76, bf16[4,2,96,768]{3,2,1,0:T(8,128)(2,1)} %bitcast.77, bf16[4,2,96,768]{3,2,1,0:T(8,128)(2,1)} %bitcast.85, ...), custom_call_target="tpu_custom_call" | custom-call | tf_op jit(solution)/shard_map/reduce_all/pallas_call | solution.py:455
  358.0 2.7 fusion.38
  362.4 3.1 fusion.45
  368.6 3.7 fusion.43
  372.4 3.7 collective-permute-start.2
  380.6 3.1 collective-permute-done.2
  383.7 10.1 %collective-permute-done.3 = bf16[256,768]{1,0:T(8,128)(2,1)S(1)} collective-permute-done((bf16[256,768]{1,0:T(8,128)(2,1)S(1)}, bf16[256,768]{1,0:T(8,128)(2,1)S(1)}, u32[]{:S(2)}, u32[]{:S(2)}) %collective-permute-start.3) | collective-permute-done | bytes 393248 | tf_op jit(solution)/shard_map/ppermute | solution.py:564
  393.7 2.0 fusion.17
  (166 shorter events, 35.0 us)
Async XLA Ops:
  0.7 10.8 %copy-start = (bf16[768,768]{1,0:T(8,128)(2,1)S(1)}, bf16[768,768]{1,0:T(8,128)(2,1)}, u32[]{:S(2)}) copy-start(bf16[768,768]{1,0:T(8,128)(2,1)} %param.23) | copy-start | bytes 3538948
  0.7 7.8 %copy-start.28 = (bf16[768]{0:T(1024)(128)(2,1)S(1)}, bf16[768]{0:T(1024)(128)(2,1)}, u32[]{:S(2)}) copy-start(bf16[768]{0:T(1024)(128)(2,1)} %param.24) | copy-start | bytes 4612
  0.7 7.8 %copy-start.29 = (bf16[768]{0:T(1024)(128)(2,1)S(1)}, bf16[768]{0:T(1024)(128)(2,1)}, u32[]{:S(2)}) copy-start(bf16[768]{0:T(1024)(128)(2,1)} %param.26) | copy-start | bytes 4612
  0.7 7.8 %copy-start.24 = (s32[1,2048]{1,0:T(1,128)S(1)}, s32[1,2048]{1,0:T(1,128)}, u32[]{:S(2)}) copy-start(s32[1,2048]{1,0:T(1,128)} %param.38) | copy-start | bytes 24580
  0.7 8.1 %copy-start.40 = (bf16[512,768]{1,0:T(8,128)(2,1)S(1)}, bf16[512,768]{1,0:T(8,128)(2,1)}, u32[]{:S(2)}) copy-start(bf16[512,768]{1,0:T(8,128)(2,1)} %param.37) | copy-start | bytes 2359300
  2.9 6.5 %copy-start.30 = (bf16[768]{0:T(1024)(128)(2,1)S(1)}, bf16[768]{0:T(1024)(128)(2,1)}, u32[]{:S(2)}) copy-start(bf16[768]{0:T(1024)(128)(2,1)} %param.22) | copy-start | bytes 4612
  2.9 6.5 %copy-start.17 = (bf16[768,768]{1,0:T(8,128)(2,1)S(1)}, bf16[768,768]{1,0:T(8,128)(2,1)}, u32[]{:S(2)}) copy-start(bf16[768,768]{1,0:T(8,128)(2,1)} %param.21) | copy-start | bytes 3538948
  2.9 14.5 %collective-permute-start = (bf16[256,768]{1,0:T(8,128)(2,1)}, bf16[256,768]{1,0:T(8,128)(2,1)}, u32[]{:S(2)}, u32[]{:S(2)}) collective-permute-start(bf16[256,768]{1,0:T(8,128)(2,1)} %get-tuple-element.55), channel_id=1, source_target_pairs={{0,8},{8,16},{16,24},{1,9},{9,17},{17,25},{2,10},{10,18},{18,26},{... | collective-permute-start | bytes 1179656 | tf_op jit(solution)/shard_map/ppermute | solution.py:511
  7.2 18.3 %collective-permute-start.1 = (bf16[256,768]{1,0:T(8,128)(2,1)}, bf16[256,768]{1,0:T(8,128)(2,1)}, u32[]{:S(2)}, u32[]{:S(2)}) collective-permute-start(bf16[256,768]{1,0:T(8,128)(2,1)} %get-tuple-element.56), channel_id=1, source_target_pairs={{8,0},{16,8},{24,16},{9,1},{17,9},{25,17},{10,2},{18,10},{26,18},{... | collective-permute-start | bytes 1179656 | tf_op jit(solution)/shard_map/ppermute | solution.py:512
  12.9 18.3 %copy-start.1 = (bf16[768,768]{1,0:T(8,128)(2,1)}, bf16[768,768]{1,0:T(8,128)(2,1)S(1)}, u32[]{:S(2)}) copy-start(bf16[768,768]{1,0:T(8,128)(2,1)S(1)} %pad.23.rk_ref) | copy-start | bytes 3538948
  13.0 64.9 %copy-start.26 = (f32[768]{0:T(1024)}, f32[768]{0:T(1024)S(1)}, u32[]{:S(2)}) copy-start(f32[768]{0:T(1024)S(1)} %convert_element_type.186) | copy-start | bytes 9220
  15.0 10.5 %copy-start.13 = (bf16[1,512,768]{2,1,0:T(8,128)(2,1)S(1)}, bf16[1,512,768]{2,1,0:T(8,128)(2,1)}, u32[]{:S(2)}) copy-start(bf16[1,512,768]{2,1,0:T(8,128)(2,1)} %param.20) | copy-start | bytes 2359300
  31.2 39.7 %copy-start.4 = (bf16[1024,768]{1,0:T(8,128)(2,1)}, bf16[1024,768]{1,0:T(8,128)(2,1)S(1)}, u32[]{:S(2)}) copy-start(bf16[1024,768]{1,0:T(8,128)(2,1)S(1)} %add_convert_fusion.v_ref) | copy-start | bytes 4718596
  31.2 39.7 %copy-start.38 = (bf16[768,768]{1,0:T(8,128)(2,1)S(1)}, bf16[768,768]{1,0:T(8,128)(2,1)}, u32[]{:S(2)}) copy-start(bf16[768,768]{1,0:T(8,128)(2,1)} %param.27) | copy-start | bytes 3538948
  71.7 6.2 %slice-start.1 = ((s8[4718592]{0:T(1024)(128)(4,1)}), s8[4194304]{0:T(1024)(128)(4,1)S(1)}, s32[]{:S(2)}) async-start(s8[4718592]{0:T(1024)(128)(4,1)} %bitcast.91), calls=%async_computation.1 | async-start | bytes 8388608
  72.1 5.9 %slice-start.2 = ((s8[4718592]{0:T(1024)(128)(4,1)}), s8[524288]{0:T(1024)(128)(4,1)S(1)}, s32[]{:S(2)}) async-start(s8[4718592]{0:T(1024)(128)(4,1)} %bitcast.91), calls=%async_computation.2 | async-start | bytes 1048576
  83.2 6.1 %slice-start.3 = ((s8[4718592]{0:T(1024)(128)(4,1)}), s8[4194304]{0:T(1024)(128)(4,1)S(1)}, s32[]{:S(2)}) async-start(s8[4718592]{0:T(1024)(128)(4,1)} %bitcast.93), calls=%async_computation.3 | async-start | bytes 8388608
  83.8 5.6 %slice-start.4 = ((s8[4718592]{0:T(1024)(128)(4,1)}), s8[524288]{0:T(1024)(128)(4,1)S(1)}, s32[]{:S(2)}) async-start(s8[4718592]{0:T(1024)(128)(4,1)} %bitcast.93), calls=%async_computation.4 | async-start | bytes 1048576
  93.5 74.3 %copy-start.5 = (f32[512,768]{1,0:T(8,128)}, f32[512,768]{1,0:T(8,128)S(1)}, u32[]{:S(2)}) copy-start(f32[512,768]{1,0:T(8,128)S(1)} %get-tuple-element.43) | copy-start | bytes 4718596
  170.0 4.8 %copy-start.15 = (bf16[1024,768]{1,0:T(8,128)(2,1)S(1)}, bf16[1024,768]{1,0:T(8,128)(2,1)}, u32[]{:S(2)}) copy-start(bf16[1024,768]{1,0:T(8,128)(2,1)} %get-tuple-element.28) | copy-start | bytes 4718596
  196.8 4.3 %copy-start.9 = (f32[768,768]{1,0:T(8,128)S(1)}, f32[768,768]{1,0:T(8,128)}, u32[]{:S(2)}) copy-start(f32[768,768]{1,0:T(8,128)} %fusion.46) | copy-start | bytes 7077892
  196.8 4.3 %copy-start.16 = (bf16[1024,768]{1,0:T(8,128)(2,1)S(1)}, bf16[1024,768]{1,0:T(8,128)(2,1)}, u32[]{:S(2)}) copy-start(bf16[1024,768]{1,0:T(8,128)(2,1)} %get-tuple-element.28) | copy-start | bytes 4718596
  362.4 6.2 %copy-start.10 = (bf16[1024,768]{1,0:T(8,128)(2,1)S(1)}, bf16[1024,768]{1,0:T(8,128)(2,1)}, u32[]{:S(2)}) copy-start(bf16[1024,768]{1,0:T(8,128)(2,1)} %get-tuple-element.29) | copy-start | bytes 4718596
  368.6 10.8 %copy-start.23 = (bf16[96,768]{1,0:T(8,128)(2,1)S(1)}, bf16[96,768]{1,0:T(8,128)(2,1)}, u32[]{:S(2)}) copy-start(bf16[96,768]{1,0:T(8,128)(2,1)} %get-tuple-element.47) | copy-start | bytes 442372
  372.3 5.1 %slice-start = ((bf16[1280,768]{1,0:T(8,128)(2,1)}), bf16[64,768]{1,0:T(8,128)(2,1)S(1)}, s32[]{:S(2)}) async-start(bf16[1280,768]{1,0:T(8,128)(2,1)} %reduce_all.1), calls=%async_computation | async-start | bytes 196608 | tf_op jit(solution)/shard_map/slice | solution.py:431
  372.3 7.1 %copy-start.20 = (bf16[96,768]{1,0:T(8,128)(2,1)S(1)}, bf16[96,768]{1,0:T(8,128)(2,1)}, u32[]{:S(2)}) copy-start(bf16[96,768]{1,0:T(8,128)(2,1)} %get-tuple-element.44) | copy-start | bytes 442372
  372.3 7.1 %copy-start.21 = (bf16[96,768]{1,0:T(8,128)(2,1)S(1)}, bf16[96,768]{1,0:T(8,128)(2,1)}, u32[]{:S(2)}) copy-start(bf16[96,768]{1,0:T(8,128)(2,1)} %get-tuple-element.45) | copy-start | bytes 442372
  372.4 7.1 %copy-start.22 = (bf16[96,768]{1,0:T(8,128)(2,1)S(1)}, bf16[96,768]{1,0:T(8,128)(2,1)}, u32[]{:S(2)}) copy-start(bf16[96,768]{1,0:T(8,128)(2,1)} %get-tuple-element.46) | copy-start | bytes 442372
  372.4 21.4 %copy-start.6 = (f32[512,768]{1,0:T(8,128)S(1)}, f32[512,768]{1,0:T(8,128)}, u32[]{:S(2)}) copy-start(f32[512,768]{1,0:T(8,128)} %copy-done.5) | copy-start | bytes 4718596
  372.4 21.4 %copy-start.18 = (bf16[768,768]{1,0:T(8,128)(2,1)S(1)}, bf16[768,768]{1,0:T(8,128)(2,1)}, u32[]{:S(2)}) copy-start(bf16[768,768]{1,0:T(8,128)(2,1)} %param.21) | copy-start | bytes 3538948
  372.4 11.2 %collective-permute-start.2 = (bf16[256,768]{1,0:T(8,128)(2,1)S(1)}, bf16[256,768]{1,0:T(8,128)(2,1)S(1)}, u32[]{:S(2)}, u32[]{:S(2)}) collective-permute-start(bf16[256,768]{1,0:T(8,128)(2,1)S(1)} %get-tuple-element.53), channel_id=1, source_target_pairs={{0,8},{8,16},{16,24},{1,9},{9,17},{17,25},{2,10},{10,18},{18,26},{... | collective-permute-start | bytes 1179656 | tf_op jit(solution)/shard_map/ppermute | solution.py:565
  376.2 17.6 %collective-permute-start.3 = (bf16[256,768]{1,0:T(8,128)(2,1)S(1)}, bf16[256,768]{1,0:T(8,128)(2,1)S(1)}, u32[]{:S(2)}, u32[]{:S(2)}) collective-permute-start(bf16[256,768]{1,0:T(8,128)(2,1)S(1)} %get-tuple-element.54), channel_id=1, source_target_pairs={{8,0},{16,8},{24,16},{9,1},{17,9},{25,17},{10,2},{18,10},{26,18},{... | collective-permute-start | bytes 1179656 | tf_op jit(solution)/shard_map/ppermute | solution.py:564
  (22 other events, 41.4 us)

commit v2 on v0

v2 whole, which is shorter than its diff:
```python
import functools
import math

import jax
import jax.numpy as jnp
from jax import lax
from jax.experimental import pallas as pl
from jax.experimental.pallas import tpu as pltpu
from jax.sharding import PartitionSpec as P

HEADS = 12
F32 = jnp.float32
BF = jnp.bfloat16
NN = (((1,), (0,)), ((), ()))
NT = (((1,), (1,)), ((), ()))
TN = (((0,), (0,)), ((), ()))


def dot(a, b, dims=NN):
    return lax.dot_general(a, b, dims, preferred_element_type=F32)


def head_lanes(x, hh):
    lane = lax.broadcasted_iota(jnp.int32, x.shape, len(x.shape) - 1)
    keep = (lane < 64) if hh == 0 else (lane >= 64)
    return jnp.where(keep, x.astype(F32), 0.0).astype(x.dtype)


def both_heads(first, second):
    lane = lax.broadcasted_iota(jnp.int32, first.shape, 1)
    return jnp.where(lane < 64, first, second)


def grid_of(n):
    return lax.broadcasted_iota(jnp.int32, (n, n), 0), lax.broadcasted_iota(jnp.int32, (n, n), 1)


def anti(n):
    row, lane = grid_of(n)
    return jnp.where(row + lane == n - 1, 1.0, 0.0).astype(BF)


def sheared(x, shift):
    return pltpu.roll(x, shift, 1, stride=1, stride_axis=0)


def fwd_kernel(n, scale, q_ref, k_ref, v_ref, rk_ref, rq_ref, qid_ref, kid_ref, ctx_ref, p_ref, bias_ref, mask_ref, rqm_ref):
    nq = q_ref.shape[0] // n
    factor = scale * math.log2(math.e)
    row, lane = grid_of(n)
    right = lane > row

    @pl.when(pl.program_id(0) == 0)
    def _():
        for qt in range(nq):
            qid = qid_ref[qt * n : (qt + 1) * n, :]
            first, middle, third = [kid_ref[:, (qt + m) * n : (qt + m + 1) * n] for m in range(3)]
            side = (right & (qid == first)) | ((lane < row) & (qid == third))
            bias_ref[qt, :, 0:n] = jnp.where(side, 0.0, -1e30)
            bias_ref[qt, :, n:] = jnp.where(qid == middle, 0.0, -1e30)
        mask_ref[0] = jnp.where(right, 1.0, 0.0).astype(BF)
        mask_ref[1] = jnp.where(right, 0.0, 1.0).astype(BF)

    for hh in range(2):
        rqm_ref[hh] = head_lanes(rq_ref[...], hh)

    def tile(qt, carry):
        at = lambda m: pl.ds(pl.multiple_of((qt + m) * n, n), n)
        qb = q_ref[at(0), :]
        outs = []
        for hh in range(2):
            qm = head_lanes(qb, hh)
            low, high = rqm_ref[hh, 0:n], rqm_ref[hh, n:]
            to_low = sheared(dot(qm, rk_ref[0:n], NT), 1)
            to_high = sheared(dot(qm, rk_ref[n:], NT), 1)
            side = jnp.where(right, dot(qm, k_ref[at(0), :], NT) + to_low, dot(qm, k_ref[at(2), :], NT) + to_high)
            middle = dot(qm, k_ref[at(1), :], NT) + jnp.where(right, to_high, to_low)
            upper = row + lane >= n - 1
            key_side = jnp.where(upper, dot(k_ref[at(0), :], high, NT), dot(k_ref[at(2), :], low, NT))
            key_middle = jnp.where(upper, dot(k_ref[at(1), :], low, NT), dot(k_ref[at(1), :], high, NT))
            side = (side + sheared(key_side, 1).T) * factor + bias_ref[qt, :, 0:n]
            middle = (middle + sheared(key_middle, 1).T) * factor + bias_ref[qt, :, n:]
            top = jnp.max(jnp.maximum(side, middle), axis=-1, keepdims=True)
            side, middle = jnp.exp2(side - top), jnp.exp2(middle - top)
            inverse = 1.0 / jnp.sum(side + middle, axis=-1, keepdims=True)
            side, middle = (side * inverse).astype(BF), (middle * inverse).astype(BF)
            p_ref[hh, at(0), 0:n] = side
            p_ref[hh, at(0), n:] = middle
            out = dot(side * mask_ref[0], v_ref[at(0), :]) + dot(middle, v_ref[at(1), :])
            outs.append(out + dot(side * mask_ref[1], v_ref[at(2), :]))
        ctx_ref[at(0), :] = both_heads(*outs).astype(BF)
        return carry

    lax.fori_loop(0, nq, tile, 0)


def attn_fwd(span, q, k, v, rk, rq, qid, kid):
    block, width = q.shape
    ext = k.shape[0]
    scale = (3.0 * 64) ** -0.5
    col = lambda rows: pl.BlockSpec((rows, 128), lambda h: (0, h))
    whole = lambda shape: pl.BlockSpec(shape, lambda h: (0, 0))
    return pl.pallas_call(
        functools.partial(fwd_kernel, span, scale),
        grid=(HEADS // 2,),
        out_shape=(
            jax.ShapeDtypeStruct((block, width), BF),
            jax.ShapeDtypeStruct((HEADS, block, 2 * span), BF),
        ),
        in_specs=[col(block), col(ext), col(ext), col(2 * span), col(2 * span), whole((block, 1)), whole((1, ext))],
        out_specs=(col(block), pl.BlockSpec((2, block, 2 * span), lambda h: (h, 0, 0))),
        scratch_shapes=[
            pltpu.VMEM((block // span, span, 2 * span), F32),
            pltpu.VMEM((2, span, span), BF),
            pltpu.VMEM((2, 2 * span, 128), BF),
        ],
        compiler_params=pltpu.CompilerParams(vmem_limit_bytes=48 << 20),
        cost_estimate=pl.CostEstimate(flops=20_000_000_000, bytes_accessed=10 << 20, transcendentals=HEADS * block * 2 * span),
        name="attn_fwd",
    )(q, k, v, rk, rq, qid, kid)


def bwd_tile(n, scale, qt, q_ref, k_ref, v_ref, g_ref, rk_ref, rq_ref, p_ref, mask_ref, kjt_ref, dk_acc, dvt_acc, drkt_acc, drqt_acc):
    at = lambda m: pl.ds(pl.multiple_of((qt + m) * n, n), n)
    row, lane = grid_of(n)
    flip = anti(n)
    ahead, behind, above, below = [mask_ref[m] for m in range(4)]
    qb, gb = q_ref[at(0), :], g_ref[at(0), :]
    qjt = dot(qb, flip, TN).astype(BF)
    gt = gb.astype(F32).T.astype(BF)
    dqs, dks = [], []
    for hh in range(2):
        lo, hi = 64 * hh, 64 * hh + 64
        gm = head_lanes(gb, hh)
        side, middle = p_ref[hh, at(0), 0:n], p_ref[hh, at(0), n:]
        ps, pm = side.astype(F32) * scale, middle.astype(F32) * scale
        gs = jnp.where(lane > row, dot(gm, v_ref[at(0), :], NT), dot(gm, v_ref[at(2), :], NT))
        gd = dot(gm, v_ref[at(1), :], NT)
        ts, td = ps * gs, pm * gd
        total = jnp.sum(ts + td, axis=-1, keepdims=True) * (1.0 / scale)
        ds, dm = (ts - ps * total).astype(BF), (td - pm * total).astype(BF)
        for m, part in enumerate((side * ahead, middle, side * behind)):
            dvt_acc[lo:hi, at(m)] += dot(gt[lo:hi], part)

        sj, mj = dot(flip, ds), dot(flip, dm)
        right = row + lane >= n
        to_low = sheared(jnp.where(right, sj, mj), 0).astype(BF)
        to_high = sheared(jnp.where(right, mj, sj), 0).astype(BF)
        sj, mj = sj.astype(BF), mj.astype(BF)
        dq = dot(sj * above, k_ref[at(0), :]) + dot(mj, k_ref[at(1), :]) + dot(sj * below, k_ref[at(2), :])
        dqs.append(dq + dot(to_low, rk_ref[0:n]) + dot(to_high, rk_ref[n:]))
        drkt_acc[lo:hi, 0:n] += dot(qjt[lo:hi], to_low)
        drkt_acc[lo:hi, n:] += dot(qjt[lo:hi], to_high)

        st, mt = dot(flip, ds, NT), dot(flip, dm, NT)
        us, um = sheared(st, 0).astype(BF), sheared(mt, 0).astype(BF)
        st, mt = st.astype(BF), mt.astype(BF)
        high_first, low_third = us * ahead, us * behind
        low_middle, high_middle = um * ahead, um * behind
        low, high = rq_ref[0:n], rq_ref[n:]
        dks.append((
            dot(st * below, qb) + dot(high_first, high),
            dot(mt, qb) + dot(low_middle, low) + dot(high_middle, high),
            dot(st * above, qb) + dot(low_third, low),
        ))
        kjt = [kjt_ref[qt + m, lo:hi, :] for m in range(3)]
        drqt_acc[lo:hi, 0:n] += dot(kjt[1], low_middle) + dot(kjt[2], low_third)
        drqt_acc[lo:hi, n:] += dot(kjt[0], high_first) + dot(kjt[1], high_middle)
    for m in range(3):
        dk_acc[qt + m] += both_heads(dks[0][m], dks[1][m])
    return dot(flip, both_heads(*dqs).astype(BF)).astype(BF)


def bwd_masks(n, mask_ref):
    row, lane = grid_of(n)
    for m, keep in enumerate((lane >= row, lane < row, row + lane >= n, row + lane < n)):
        mask_ref[m] = jnp.where(keep, 1.0, 0.0).astype(BF)


MESH = pl.DeviceIdType.MESH


def toggled(value, mask):
    out = value
    for bit in range(mask.bit_length()):
        if mask >> bit & 1:
            out = out + (1 - 2 * ((value // (1 << bit)) % 2)) * (1 << bit)
    return out


class Mesh:
    def __init__(self, ns, nb):
        self.ns, self.nb, self.nz = ns, nb, nb // 2
        self.bits = ns.bit_length() - 1
        self.ways = 2 if ns <= 4 else 1

    def locate(self):
        self.s = lax.axis_index("seq")
        self.b = lax.axis_index("batch")
        self.z, self.c = self.b // 2, self.b % 2

    def at(self, s, b):
        return {"seq": s, "batch": b}

    def greet(self):
        barrier = pltpu.get_barrier_semaphore()
        peers = [self.at(self.s, toggled(self.b, 1))]
        peers += [self.at(self.s, toggled(self.z, step) * 2 + self.c) for step in range(1, self.nz)]
        peers += [self.at(toggled(self.s, step), self.b) for step in range(1, self.ns)]
        for peer in peers:
            pl.semaphore_signal(barrier, inc=1, device_id=peer, device_id_type=MESH)
        pl.semaphore_wait(barrier, len(peers))


class Chunk:
    def __init__(self, mesh, rows, lanes, moves, box=None, early_z=False):
        self.mesh, self.rows, self.moves, self.box, self.early_z = mesh, rows, moves, box, early_z
        unit = 128 * mesh.ways * mesh.ns
        self.lanes = -(-lanes // unit) * unit
        self.piece = self.lanes // (mesh.ways * mesh.ns)
        self.depth = 1 if early_z else mesh.nz

    def scratch(self):
        mesh, rows, lanes = self.mesh, self.rows, self.lanes
        full = pltpu.VMEM((mesh.nz, rows, lanes), BF)
        shapes = [full] if self.box else [full, full]
        for level in range(mesh.bits):
            shapes.append(pltpu.VMEM((mesh.ways, self.depth, rows, lanes // mesh.ways // 2 >> level), BF))
        wide = lanes // mesh.ways if self.early_z else self.piece
        shapes += [pltpu.VMEM((mesh.ways, mesh.nz - 1, rows, wide), BF), pltpu.VMEM((rows, lanes), BF)]
        dma = pltpu.SemaphoreType.DMA
        moves = len(self.moves)
        shapes += [] if self.box else [dma((moves,))]
        shapes += [dma((2, moves)), dma((2, 2, mesh.bits)), dma((2, 2, mesh.nz - 1)), dma((2, 2, mesh.ns - 1))]
        return shapes

    def bind(self, refs):
        bits = self.mesh.bits
        if self.box:
            self.mine = self.box(self.mesh.c)
        else:
            self.mine, refs = refs[0], refs[1:]
        self.first = refs[0]
        self.halves = refs[1 : 1 + bits]
        self.across, self.final = refs[1 + bits : 3 + bits]
        refs = refs[3 + bits :]
        if not self.box:
            self.own_sem, refs = refs[0], refs[1:]
        self.core_sem, self.seq_sem, self.z_sem, self.out_sem = refs[:4]
        return refs[4:]

    def copy(self, src, dst, sems, index, s, b):
        return pltpu.make_async_remote_copy(
            src_ref=src,
            dst_ref=dst,
            send_sem=sems.at[(0,) + index],
            recv_sem=sems.at[(1,) + index],
            device_id=self.mesh.at(s, b),
            device_id_type=MESH,
        )

    def own_copies(self):
        for n, (source, at, size) in enumerate([] if self.box else self.moves):
            yield pltpu.make_async_copy(source(self.mesh.c), self.mine.at[:, :, pl.ds(at, size)], self.own_sem.at[n])

    def core_copies(self):
        mesh = self.mesh
        for n, (source, at, size) in enumerate(self.moves):
            yield self.copy(
                source(1 - mesh.c), self.first.at[:, :, pl.ds(at, size)], self.core_sem, (n,), mesh.s, toggled(mesh.b, 1)
            )

    def order(self, half, level):
        return (level + half) % self.mesh.bits

    def region(self, level, half):
        size = self.lanes // self.mesh.ways
        base = half * size
        sent = base
        for at in range(level):
            mine = (self.mesh.s // (1 << self.order(half, at))) % 2
            size = size // 2
            sent = base + (1 - mine) * size
            base = base + mine * size
        return base, sent, size

    def span(self, start, size):
        return pl.ds(pl.multiple_of(start, 128), size)

    def planes(self):
        return pl.ds(self.mesh.z, 1) if self.early_z else slice(None)

    def seq_copy(self, level, half):
        unused, sent, size = self.region(level + 1, half)
        return self.copy(
            self.mine.at[self.planes(), :, self.span(sent, size)],
            self.halves[level].at[half],
            self.seq_sem,
            (half, level),
            toggled(self.mesh.s, 1 << self.order(half, level)),
            self.mesh.b,
        )

    def z_region(self, half):
        kept, unused, size = self.region(0 if self.early_z else self.mesh.bits, half)
        return self.span(kept, size)

    def z_copies(self, half):
        mesh = self.mesh
        for step in range(1, mesh.nz):
            other = toggled(mesh.z, step)
            yield self.copy(
                self.mine.at[other, :, self.z_region(half)],
                self.across.at[half, step - 1],
                self.z_sem,
                (half, step - 1),
                mesh.s,
                other * 2 + mesh.c,
            )

    def out_copies(self, half):
        kept, unused, size = self.region(self.mesh.bits, half)
        for step in range(1, self.mesh.ns):
            lanes = self.span(kept, size)
            yield self.copy(
                self.final.at[:, lanes], self.final.at[:, lanes], self.out_sem, (half, step - 1), toggled(self.mesh.s, step), self.mesh.b
            )

    def start_core(self):
        for copy in self.core_copies():
            copy.start()
        for copy in self.own_copies():
            copy.start()

    def add_core(self):
        for copy in self.own_copies():
            copy.wait()
        for copy in self.core_copies():
            copy.wait_recv()
        parts = 4
        size = self.lanes // parts

        def add(n, carry):
            z, lanes = n // parts, self.span((n % parts) * size, size)
            self.mine[z, :, lanes] = (self.mine[z, :, lanes].astype(F32) + self.first[z, :, lanes].astype(F32)).astype(BF)
            return carry

        lax.fori_loop(0, self.mesh.nz * parts, add, 0)

    def start_seq(self, level):
        for half in range(self.mesh.ways):
            self.seq_copy(level, half).start()

    def add_seq(self, level):
        for half in range(self.mesh.ways):
            self.seq_copy(level, half).wait_recv()
            kept, unused, size = self.region(level + 1, half)
            lanes = self.span(kept, size)

            def add(n, carry):
                z = self.mesh.z if self.early_z else n
                got = self.halves[level][half, n].astype(F32)
                self.mine[z, :, lanes] = (self.mine[z, :, lanes].astype(F32) + got).astype(BF)
                return carry

            lax.fori_loop(0, self.depth, add, 0)
            if self.early_z and level == self.mesh.bits - 1:
                self.final[:, lanes] = self.mine[self.mesh.z, :, lanes]

    def end_seq(self):
        self.add_seq(1)
        for level in range(2, self.mesh.bits):
            self.start_seq(level)
            self.add_seq(level)

    def start_z(self):
        for half in range(self.mesh.ways):
            for copy in self.z_copies(half):
                copy.start()

    def add_z(self):
        z = self.mesh.z
        for half in range(self.mesh.ways):
            for copy in self.z_copies(half):
                copy.wait_recv()
            lanes = self.z_region(half)
            total = self.mine[z, :, lanes].astype(F32)
            for step in range(1, self.mesh.nz):
                total = total + self.across[half, step - 1].astype(F32)
            if self.early_z:
                self.mine[z, :, lanes] = total.astype(BF)
            else:
                self.final[:, lanes] = total.astype(BF)

    def start_out(self):
        for half in range(self.mesh.ways):
            for copy in self.out_copies(half):
                copy.start()

    def core(self):
        self.start_core()

    def s0(self):
        if self.early_z:
            self.add_z()
        else:
            self.add_core()
        self.start_seq(0)

    def s1(self):
        self.add_seq(0)
        self.start_seq(1)

    def z(self):
        if self.early_z:
            self.add_core()
        else:
            self.end_seq()
        self.start_z()

    def out(self):
        if self.early_z:
            self.end_seq()
        else:
            self.add_z()
        self.start_out()

    def finish(self):
        for half in range(self.mesh.ways):
            for copy in self.out_copies(half):
                copy.wait()
            for copy in self.z_copies(half):
                copy.wait_send()
            for level in range(self.mesh.bits):
                self.seq_copy(level, half).wait_send()
        for copy in self.core_copies():
            copy.wait_send()


class Layout:
    def __init__(self, ns, nb, width, hidden, table):
        self.mesh = mesh = Mesh(ns, nb)
        self.width, self.hidden = width, hidden
        self.rows = rows = width // nb
        self.fold = hidden // nb // rows
        self.rel_rows = table // nb
        self.pairs = width // 128
        self.third = width // 3
        self.rel_at = 384
        self.small_at = 384 + 512
        self.stack = rows // 16
        small_lanes = -(-self.pairs // self.stack) * 128
        down = [
            (lambda c, n=n: self.down_ref.at[:, c, pl.ds(n * rows, rows), :], n * width, width) for n in range(self.fold)
        ]
        into = [(lambda c: self.in_ref.at[:, c], 0, hidden)]
        self.down = Chunk(mesh, rows, self.fold * width, down)
        self.into = Chunk(mesh, rows, hidden, into)
        lanes = Chunk(mesh, rows, 768 + self.third, []).lanes
        self.near = []
        for n in range(3):
            box = lambda c, n=n: self.near_ref.at[n, :, c]
            self.near.append(Chunk(mesh, rows, lanes, [(box, 0, lanes)], box, early_z=n < 0))
        lanes = Chunk(mesh, rows, self.small_at + small_lanes, []).lanes
        far = lambda c: self.far_ref.at[:, c]
        self.far = Chunk(mesh, rows, lanes, [(far, 0, lanes)], far)
        self.chunks = [self.down, self.into, *self.near, self.far]

    def scratch(self):
        mesh = self.mesh
        shapes = [
            pltpu.VMEM((3, mesh.nz, 2, self.rows, self.near[0].lanes), BF),
            pltpu.VMEM((mesh.nz, 2, self.rows, self.far.lanes), BF),
            pltpu.SemaphoreType.DMA((3,)),
        ]
        for chunk in self.chunks:
            shapes += chunk.scratch()
        return shapes

    def bind(self, down_ref, in_ref, out_ref, refs):
        self.mesh.locate()
        self.down_ref, self.in_ref, self.out_ref = down_ref, in_ref, out_ref
        self.near_ref, self.far_ref, self.out_sem = refs[:3]
        refs = refs[3:]
        for chunk in self.chunks:
            refs = chunk.bind(refs)
        return refs

    def out_copies(self):
        for n in range(3):
            yield pltpu.make_async_copy(
                self.out_ref.at[:, :, :, pl.ds(n * self.third, self.third)],
                self.near_ref.at[n, :, :, :, pl.ds(768, self.third)],
                self.out_sem.at[n],
            )

    def store_pair(self, pair, grads):
        rows = self.rows
        box = pair // 2
        lanes = pl.ds(pl.multiple_of((pair % 2) * 384, 128), 384)

        @pl.when(pair < self.pairs - 1)
        def _():
            for b in range(self.mesh.nb):
                self.near_ref[box, b // 2, b % 2, :, lanes] = grads[b * rows : (b + 1) * rows]

        @pl.when(pair == self.pairs - 1)
        def _():
            for b in range(self.mesh.nb):
                self.far_ref[b // 2, b % 2, :, 0:384] = grads[b * rows : (b + 1) * rows]

    def store_rest(self, rel, vectors):
        take, at, half = self.rel_rows, self.rel_at, self.rel_rows // 2
        for b in range(self.mesh.nb):
            part = rel[b * take : (b + 1) * take]
            put = self.far_ref.at[b // 2, b % 2]
            put[0:take, at : at + 512] = part[:, 0:512]
            put[take : take + half, at : at + 256] = part[0:half, 512:768]
            put[take : take + half, at + 256 : at + 512] = part[half:, 512:768]
            for n in range(self.pairs):
                row, lane = (n % self.stack) * 16, self.small_at + (n // self.stack) * 128
                put[row : row + 16, lane : lane + 128] = vectors[:, n * 128 : (n + 1) * 128]

    def rel_of(self, far):
        take, at, half = self.rel_rows, self.rel_at, self.rel_rows // 2
        low = [far[take : take + half, at : at + 256], far[take : take + half, at + 256 : at + 512]]
        return jnp.concatenate([far[0:take, at : at + 512], jnp.concatenate(low, axis=0)], axis=1)

    def vectors_of(self, far):
        parts = []
        for n in range(self.pairs):
            row, lane = (n % self.stack) * 16, self.small_at + (n // self.stack) * 128
            parts.append(far[row : row + 16, lane : lane + 128])
        return jnp.concatenate(parts, axis=1)

    def pairs_of(self, near, far, n):
        blocks = [side[:, m * 384 + n * 128 : m * 384 + (n + 1) * 128] for side in near for m in range(2)][: self.pairs - 1]
        return jnp.concatenate(blocks + [far[:, n * 128 : (n + 1) * 128]], axis=1)

    def schedule(self, edges):
        down, into, one, two, three, far = self.chunks

        def open_all():
            self.mesh.greet()
            for copy in self.out_copies():
                copy.start()
            down.core()
            into.core()

        def open_near():
            for copy in self.out_copies():
                copy.wait()
            one.core()

        steps = {
            0: [open_all],
            1: [down.s0],
            2: [into.s0],
            4: [down.s1, open_near],
            5: [one.s0],
            6: [into.s1],
            7: [down.z],
            8: [one.s1, two.core],
            9: [into.z, two.s0],
            10: [down.out, three.core, one.z],
            11: [three.s0, two.s1],
        }
        last = [far.core, into.out, one.out, two.z, three.s1, far.s0, edges.start, two.out, three.z, far.s1, three.out, far.z, far.out]
        last += [chunk.finish for chunk in self.chunks]
        return steps, last


class Edges:
    def __init__(self, mesh, refs):
        self.mesh = mesh
        self.sent, self.got, self.sems = refs

    def copy(self, side):
        other = self.mesh.s + (2 * side - 1)
        return pltpu.make_async_remote_copy(
            src_ref=self.sent.at[side],
            dst_ref=self.got.at[1 - side],
            send_sem=self.sems.at[0, side],
            recv_sem=self.sems.at[1, 1 - side],
            device_id=self.mesh.at(other, self.mesh.b),
            device_id_type=MESH,
        )

    def has(self, side):
        return self.mesh.s > 0 if side == 0 else self.mesh.s < self.mesh.ns - 1

    def start(self):
        for side in range(2):
            pl.when(self.has(side))(lambda side=side: self.copy(side).start())

    def finish(self, add):
        for side in range(2):

            @pl.when(self.has(side))
            def _(side=side):
                self.copy(side).wait_send()
                self.copy(1 - side).wait_recv()
                add(side, self.got[side])


def bwd_kernel(tq, scale, layout, q_ref, k_ref, v_ref, g_ref, rk_ref, rq_ref, p_ref, wk_ref, wq_ref, wv_ref,
               g_one_ref, x_ref, rel_ref, picks_ref, small_ref, down_ref, in_ref, out_ref,
               dx_ref, down_out, in_out, near0_out, near1_out, near2_out, far_out,
               mask_ref, kjt_ref, dk_acc, dvt_acc, drkt_acc, drqt_acc,
               xt_ref, d_ref, rel_acc, vec_ref, dx_acc, sent_ref, got_ref, edge_sem, *refs):
    block = q_ref.shape[0]
    nq = block // tq
    ext = k_ref.shape[0]
    nk = ext // tq
    span = tq
    table = 2 * span
    pair = pl.program_id(0)
    pairs = layout.pairs
    flip = anti(tq)
    layout.bind(down_ref, in_ref, out_ref, refs)
    edges = Edges(layout.mesh, (sent_ref, got_ref, edge_sem))
    steps, last = layout.schedule(edges)

    def run(actions):
        def all_of():
            for action in actions:
                action()
        return all_of

    @pl.when(pair == 0)
    def _():
        run(steps[0])()
        bwd_masks(tq, mask_ref)
        for n in range(ext // 128):
            xt_ref[:, n * 128 : (n + 1) * 128] = x_ref[n * 128 : (n + 1) * 128, :].astype(F32).T.astype(BF)
        for n in range(table // 128):
            xt_ref[:, ext + n * 128 : ext + (n + 1) * 128] = rel_ref[n * 128 : (n + 1) * 128, :].astype(F32).T.astype(BF)
        d_ref[...] = jnp.zeros_like(d_ref)
        rel_acc[...] = jnp.zeros_like(rel_acc)
        dx_acc[...] = jnp.zeros_like(dx_acc)
        vec_ref[...] = small_ref[...].astype(F32)

    for kt in range(nk):
        kjt_ref[kt] = dot(k_ref[kt * tq : (kt + 1) * tq, :], flip, TN).astype(BF)
    dk_acc[...] = jnp.zeros_like(dk_acc)
    dvt_acc[...] = jnp.zeros_like(dvt_acc)
    drkt_acc[...] = jnp.zeros_like(drkt_acc)
    drqt_acc[...] = jnp.zeros_like(drqt_acc)

    def tile(qt, carry):
        for step, actions in steps.items():
            if step:
                pl.when(pair * nq + qt == step * pairs * nq // 12)(run(actions))
        row = pl.multiple_of(qt * tq, tq)
        dq = bwd_tile(
            tq, scale, qt, q_ref, k_ref, v_ref, g_ref, rk_ref, rq_ref, p_ref, mask_ref, kjt_ref, dk_acc, dvt_acc, drkt_acc, drqt_acc
        )
        d_ref[pl.ds(span + row, tq), 0:128] = dq
        return carry

    lax.fori_loop(0, nq, tile, 0)
    for kt in range(nk):
        here = slice(kt * tq, (kt + 1) * tq)
        dk = dot(flip, dk_acc[kt].astype(BF)).astype(BF)
        dv = dvt_acc[:, here].T.astype(BF)
        d_ref[here, 128:256] = dk
        d_ref[here, 256:384] = dv
    for st in range(table // 128):
        here = slice(ext + st * 128, ext + (st + 1) * 128)
        d_ref[here, 0:128] = drqt_acc[:, st * 128 : (st + 1) * 128].T.astype(BF)
        d_ref[here, 128:256] = drkt_acc[:, st * 128 : (st + 1) * 128].T.astype(BF)

    grads = dot(xt_ref[...], d_ref[...]).astype(BF)
    layout.store_pair(pair, grads)
    weights = jnp.concatenate([wq_ref[...], wk_ref[...], wv_ref[...]], axis=1)
    dx_acc[...] += dot(d_ref[0:ext], weights, NT)
    rel_acc[...] += dot(d_ref[ext:, 0:128], wq_ref[...], NT) + dot(d_ref[ext:, 128:256], wk_ref[...], NT)
    sums = dot(jnp.ones((8, ext + table), BF), d_ref[...])[0:1]
    for n in range(3):
        vec_ref[10 + n : 11 + n, pl.ds(pl.multiple_of(pair * 128, 128), 128)] = sums[:, n * 128 : (n + 1) * 128]

    @pl.when(pair == pairs - 1)
    def _():
        rel = dot(picks_ref[...], rel_acc[...].astype(BF)).astype(BF)
        layout.store_rest(rel, vec_ref[...].astype(BF))
        sent_ref[0] = dx_acc[0:span].astype(BF)
        sent_ref[1] = dx_acc[ext - span :].astype(BF)
        run(last[:1])()
        dx_ref[...] = g_one_ref[...] + dx_acc[span : span + block]
        run(last[1:])()

        def take(side, rows):
            here = slice(0, span) if side == 0 else slice(block - span, block)
            dx_ref[here] += rows.astype(F32)

        edges.finish(take)
        outs = (down_out, in_out, near0_out, near1_out, near2_out, far_out)
        for out, chunk in zip(outs, layout.chunks):
            out[...] = chunk.final[...]


def attn_bwd(span, q, k, v, g, rk, rq, probs, w_key, w_query, w_value, grad_one, x_ext, rel_flip, picks, small, down_grad, in_grad, out_grad):
    block, width = q.shape
    ext = k.shape[0]
    table = 2 * span
    scale = (3.0 * 64) ** -0.5
    ns, nb = lax.axis_size("seq"), lax.axis_size("batch")
    layout = Layout(ns, nb, width, in_grad.shape[1], table)
    col = lambda rows: pl.BlockSpec((rows, 128), lambda h: (0, h))
    whole = lambda shape: pl.BlockSpec(shape, lambda h: (0, 0), pipeline_mode=pl.Buffered(1))
    any_spec = pl.BlockSpec(memory_space=pl.ANY)
    by_share = lambda grad: grad.reshape(nb // 2, 2, grad.shape[0] // nb, grad.shape[1])
    packed = [jax.ShapeDtypeStruct((layout.rows, chunk.lanes), BF) for chunk in layout.chunks]
    outs = pl.pallas_call(
        functools.partial(bwd_kernel, span, scale, layout),
        grid=(width // 128,),
        out_shape=(
            jax.ShapeDtypeStruct((block, width), F32),
            *packed,
        ),
        in_specs=[col(block), col(ext), col(ext), col(block), col(rk.shape[0]), col(rq.shape[0]),
                  pl.BlockSpec((2, block, table), lambda h: (h, 0, 0)), col(width), col(width), col(width),
                  whole(grad_one.shape), whole(x_ext.shape), whole(rel_flip.shape), whole(picks.shape), whole(small.shape),
                  any_spec, any_spec, any_spec],
        out_specs=(whole((block, width)),) + tuple(whole(part.shape) for part in packed),
        scratch_shapes=[
            pltpu.VMEM((4, span, span), BF),
            pltpu.VMEM((ext // span, 128, span), BF),
            pltpu.VMEM((ext // span, span, 128), F32),
            pltpu.VMEM((128, ext), F32),
            pltpu.VMEM((128, table), F32),
            pltpu.VMEM((128, table), F32),
            pltpu.VMEM((width, ext + table), BF),
            pltpu.VMEM((ext + table, 384), BF),
            pltpu.VMEM((table, width), F32),
            pltpu.VMEM((16, width), F32),
            pltpu.VMEM((ext, width), F32),
            pltpu.VMEM((2, span, width), BF),
            pltpu.VMEM((2, span, width), BF),
            pltpu.SemaphoreType.DMA((2, 2)),
        ] + layout.scratch(),
        compiler_params=pltpu.CompilerParams(collective_id=0, has_side_effects=True, vmem_limit_bytes=60 << 20),
        cost_estimate=pl.CostEstimate(flops=50_000_000_000, bytes_accessed=20 << 20, transcendentals=0),
        name="attn_bwd_reduce",
    )(q, k, v, g, rk, rq, probs, w_key, w_query, w_value, grad_one, x_ext, rel_flip, picks, small,
      by_share(down_grad), by_share(in_grad), by_share(out_grad))
    return layout, outs


NORM_EPS = 1e-07


def norm_rows(values):
    centred = values - jnp.mean(values, axis=-1, keepdims=True)
    inv_std = lax.rsqrt(jnp.mean(centred * centred, axis=-1, keepdims=True) + NORM_EPS)
    return centred * inv_std, inv_std


def norm_back(grads, normed, inv_std):
    first_mean = jnp.mean(grads, axis=-1, keepdims=True)
    second_mean = jnp.mean(grads * normed, axis=-1, keepdims=True)
    return inv_std * (grads - first_mean - normed * second_mean)


def local(
    layer_input,
    w_query,
    b_query,
    w_key,
    b_key,
    w_value,
    b_value,
    w_out,
    b_out,
    gain_attn,
    shift_attn,
    w_in,
    b_in,
    w_down,
    b_down,
    gain_ffn,
    shift_ffn,
    rel_table,
    segment_ids,
    cotangent,
):
    rows, block, width = layer_input.shape
    span = rel_table.shape[0] // 2
    x = layer_input[0]
    count = lax.axis_size("seq")
    up = [(i, i + 1) for i in range(count - 1)]
    down = [(i + 1, i) for i in range(count - 1)]
    before = lax.ppermute(x[block - span :], "seq", up)
    after = lax.ppermute(x[:span], "seq", down)
    rel_flip = dot(anti(2 * span), rel_table).astype(BF)

    def project(rows_in, weight, bias):
        return (dot(rows_in, weight) + bias).astype(BF)

    q = project(x, w_query, b_query)
    rk = project(rel_flip, w_key, b_key)
    rq = project(rel_flip, w_query, b_query)
    x_ext = jnp.concatenate([before, x, after], axis=0)
    k = project(x_ext, w_key, b_key)
    v = project(x_ext, w_value, b_value)
    start = lax.axis_index("seq") * block
    padded = jnp.pad(segment_ids[0], (span, span), constant_values=-1)
    kid = lax.dynamic_slice_in_dim(padded, start, block + 2 * span, 0)
    qid = kid[span : span + block]
    context, probs = attn_fwd(span, q, k, v, rk, rq, qid[:, None], kid[None])

    residual_one = x.astype(F32) + dot(context, w_out) + b_out
    normed_one, inv_one = norm_rows(residual_one)
    hidden = normed_one * gain_attn + shift_attn
    hidden_low = hidden.astype(BF)
    pre_act = dot(hidden_low, w_in) + b_in
    phi = 0.5 * (1.0 + lax.erf(pre_act * (0.5**0.5)))
    act_low = (pre_act * phi).astype(BF)
    slope = phi + pre_act * (jnp.exp(-0.5 * pre_act * pre_act) * ((2.0 * math.pi) ** -0.5))
    residual_two = hidden + dot(act_low, w_down) + b_down
    normed_two, inv_two = norm_rows(residual_two)
    output = (normed_two * gain_ffn + shift_ffn).astype(BF)

    grad_out = cotangent[0].astype(F32)
    gain_ffn_grad = jnp.sum(grad_out * normed_two, axis=0)
    shift_ffn_grad = jnp.sum(grad_out, axis=0)
    grad_two = norm_back(grad_out * gain_ffn, normed_two, inv_two)
    grad_branch = grad_two.astype(BF)
    down_grad = dot(act_low, grad_branch, TN)
    down_bias_grad = jnp.sum(grad_branch.astype(F32), axis=0)
    grad_pre = (dot(grad_branch, w_down, NT) * slope).astype(BF)
    in_grad = dot(hidden_low, grad_pre, TN)
    in_bias_grad = jnp.sum(grad_pre.astype(F32), axis=0)
    grad_hidden = grad_two + dot(grad_pre, w_in, NT)
    gain_attn_grad = jnp.sum(grad_hidden * normed_one, axis=0)
    shift_attn_grad = jnp.sum(grad_hidden, axis=0)
    grad_one = norm_back(grad_hidden * gain_attn, normed_one, inv_one)
    grad_attn = grad_one.astype(BF)
    out_grad = dot(context, grad_attn, TN)
    out_bias_grad = jnp.sum(grad_attn.astype(F32), axis=0)
    grad_context = dot(grad_attn, w_out, NT).astype(BF)

    share, lanes = lax.axis_size("batch"), lax.axis_size("seq")
    rel_rows = 2 * span // (share * lanes)
    order = jnp.arange(2 * span).reshape(lanes, share, rel_rows).transpose(1, 0, 2).reshape(-1)
    picks = ((2 * span - 1 - order)[:, None] == jnp.arange(2 * span)[None]).astype(BF)
    small = [out_bias_grad, gain_attn_grad, shift_attn_grad, down_bias_grad, gain_ffn_grad, shift_ffn_grad, in_bias_grad]
    small = jnp.concatenate([vec.reshape(-1, width) for vec in small], axis=0)
    small = jnp.pad(small, ((0, 16 - small.shape[0]), (0, 0))).astype(BF)
    layout, outs = attn_bwd(
        span, q, k, v, grad_context, rk, rq, probs, w_key, w_query, w_value, grad_one, x_ext, rel_flip, picks, small,
        down_grad.astype(BF), in_grad.astype(BF), out_grad.astype(BF),
    )
    input_grad, down_sum, in_sum, *near, far = outs
    fold = layout.fold
    down_sum = jnp.concatenate([down_sum[:, n * width : (n + 1) * width] for n in range(fold)], axis=0).astype(F32)
    in_sum = in_sum[:, : layout.hidden].astype(F32)
    out_sum = jnp.concatenate([side[:, 768 : 768 + layout.third] for side in near], axis=1).astype(F32)
    query_sum, key_sum, value_sum = [layout.pairs_of(near, far, n).astype(F32) for n in range(3)]
    rel_sum = layout.rel_of(far)
    rel_sum = lax.dynamic_slice_in_dim(rel_sum, lax.axis_index("seq") * rel_rows, rel_rows, 0).astype(F32)
    vectors = layout.vectors_of(far).astype(F32)
    mine = lax.axis_index("batch") * layout.rows
    cut = lambda n: lax.dynamic_slice_in_dim(vectors[n], mine, layout.rows, 0)
    ob, ga, sa, db, gf, sf = [cut(n) for n in range(6)]
    wide = layout.hidden // share
    ib = lax.dynamic_slice_in_dim(vectors[6:10].reshape(-1), lax.axis_index("batch") * wide, wide, 0)
    qb, kb, vb = [cut(n) for n in range(10, 13)]
    return (
        output[None], input_grad[None], query_sum, qb, key_sum, kb, value_sum, vb, out_sum, ob,
        ga, sa, in_sum, ib, down_sum, db, gf, sf, rel_sum,
    )


def solution(mesh):
    tokens = P("batch", "seq", None)
    in_specs = (tokens,) + (P(),) * 17 + (P("batch", None), tokens)
    matrix, vector = P("batch", None), P("batch")
    out_specs = (
        (tokens, tokens)
        + (matrix, vector) * 4
        + (vector, vector)
        + (matrix, vector) * 2
        + (vector, vector, P(("seq", "batch"), None))
    )
    return jax.shard_map(local, mesh=mesh, in_specs=in_specs, out_specs=out_specs, check_vma=False)
```

time: 608 us -> 251 us (0.41)
  waiting for transfers between devices: 304 us -> 9.35 us
  Pallas kernels: 100 us -> 157 us
  matrix products: 83.7 us -> 38.7 us
  blocking collectives: 37 us -> 0 us
  between operations: 15.1 us -> 1.41 us
  local copies, waits for them, and re-layouts: 31.6 us -> 22.8 us
  starting transfers between devices: 12.3 us -> 4.83 us
    reduce_scatter x6 -> x0, waiting for transfers between devices: 228 us -> none  [the longest x5 195 us: reduced(): lax.psum_scatter(grad.astype(BF), 'batch', scatter_dimension=0, tiled=True)]
    psum x1 -> x0, waiting for transfers between devices: 68.4 us -> none  [reduced(): return lax.psum(part, 'seq').astype(F32)]
    pallas_call x2, Pallas kernels: 100 us -> 157 us  [the longest x1 127 us: attn_bwd(): pl.pallas_call(functools.partial(bwd_kernel, span, scale, layout), grid=(...]
    dot_general x25 -> x15, matrix products: 83.7 us -> 38.7 us  [dot(): return lax.dot_general(a, b, dims, preferred_element_type=F32)]
    unnamed x1 -> x0, blocking collectives: 25.8 us -> none
    psum x1 -> x0, blocking collectives: 11.2 us -> none  [reduced(): return lax.psum(part, 'seq').astype(F32)]
    reshape x8, local copies, waits for them, and re-layouts: 8.03 us -> 0.05 us  [the longest x7 0.04 us: local(): small = jnp.concatenate([vec.reshape(-1, width) for vec in small], axis=0)]
    unnamed x107 -> x81, local copies, waits for them, and re-layouts: 12.5 us -> 8.4 us
  transfers between devices with their start and end apart: 12 -> 2, of which waited for: 8 -> 1; matrix products, arithmetic and copies ran while one was open for 13% -> 3% of each run, Pallas kernels for 0% -> 0%
where the time goes in v2:
time: 251 us; the launch traced here: 248 us
  Pallas kernels  157 us (63%)
  matrix products  38.7 us (15%)
  local copies, waits for them, and re-layouts  22.8 us (9%)
  other arithmetic  13.7 us (5%)
  waiting for transfers between devices  9.35 us (4%)
  starting transfers between devices  4.83 us (2%)
    pallas_call x1, Pallas kernels, attn_bwd(): pl.pallas_call(functools.partial(bwd_kernel, span, scale, layout), grid=(...  127 us
    dot_general x15, matrix products, dot(): return lax.dot_general(a, b, dims, preferred_element_type=F32)  38.7 us
    pallas_call x1, Pallas kernels, attn_fwd(): pl.pallas_call(functools.partial(fwd_kernel, span, scale), grid=(HEADS //...  30 us
    ppermute x1, waiting for transfers between devices, local(): after = lax.ppermute(x[:span], 'seq', down)  9.34 us
    unnamed x81, local copies, waits for them, and re-layouts  8.4 us
    dynamic_slice x9, local copies, waits for them, and re-layouts, local(): cut = lambda n: lax.dynamic_slice_in_dim(vectors[n], mine, layout.rows, 0)  5.24 us
  transfers between devices with their start and end apart: 2, of which 1 were waited for; matrix products, arithmetic and copies ran while one was open for 3% of the time, Pallas kernels for 0%

profile of v2, /device:TPU:8, one launch (start us, length us, event | category | flops | bytes accessed | tf_op | source)
XLA Modules:
  0.0 247.5 jit_solution(6501650909860558659)
XLA Ops:
  0.7 2.2 slice_bitcast_fusion.1
  2.9 3.5 %collective-permute-start = (bf16[256,768]{1,0:T(8,128)(2,1)}, bf16[256,768]{1,0:T(8,128)(2,1)S(1)}, u32[]{:S(2)}, u32[]{:S(2)}) collective-permute-start(bf16[256,768]{1,0:T(8,128)(2,1)} %get-tuple-element.49), channel_id=1, source_target_pairs={{0,8},{8,16},{16,24},{1,9},{9,17},{17,25},{2,10},{10,18},{18,26},{... | collective-permute-start | bytes 1179656 | tf_op jit(solution)/shard_map/ppermute | solution.py:793
  6.4 1.3 collective-permute-start.1
  10.8 1.0 fusion.14.picks_ref
  12.3 1.3 reduce.3
  13.6 2.4 add_convert_fusion.4.rk_ref
  16.1 9.3 %collective-permute-done.1 = bf16[256,768]{1,0:T(8,128)(2,1)} collective-permute-done((bf16[256,768]{1,0:T(8,128)(2,1)}, bf16[256,768]{1,0:T(8,128)(2,1)}, u32[]{:S(2)}, u32[]{:S(2)}) %collective-permute-start.1) | collective-permute-done | bytes 393248 | tf_op jit(solution)/shard_map/ppermute | solution.py:794
  25.4 2.5 %add_convert_fusion.1.k_ref = bf16[1024,768]{1,0:T(8,128)(2,1)S(1)} fusion(bf16[768,768]{1,0:T(8,128)(2,1)S(1)} %copy-done.27, f32[768]{0:T(1024)S(1)} %convert_element_type.136, bf16[256,768]{1,0:T(8,128)(2,1)} %collective-permute-done.1, bf16[512,768]{1,0:T(8,128)(2,1)S(1)} %bitcast.63, bf16[256,768]{1,0:T(8,128)(2,1)S(1)} %collective-permute-done), kind=kOutput, calls=%fused_computation.12 | convolution fusion | flops 1214251008 | bytes 4328448 | tf_op jit(solution)/shard_map/dot_general | solution.py:20
  28.0 4.0 %add_convert_fusion.v_ref = bf16[1024,768]{1,0:T(8,128)(2,1)} fusion(bf16[768,768]{1,0:T(8,128)(2,1)S(1)} %copy-done.28, f32[768]{0:T(1024)S(1)} %convert_element_type.138, bf16[256,768]{1,0:T(8,128)(2,1)} %collective-permute-done.1, bf16[512,768]{1,0:T(8,128)(2,1)S(1)} %bitcast.64, bf16[256,768]{1,0:T(8,128)(2,1)S(1)} %collective-permute-done), kind=kOutput, calls=%fused_computation.11 | convolution fusion | flops 1214251008 | bytes 4328448 | tf_op jit(solution)/shard_map/dot_general | solution.py:20
  32.0 30.0 %attn_fwd.1 = (bf16[512,768]{1,0:T(8,128)(2,1)S(1)}, bf16[12,512,512]{2,1,0:T(8,128)(2,1)}) custom-call(bf16[512,768]{1,0:T(8,128)(2,1)S(1)} %add_convert_fusion.5.q_ref, bf16[1024,768]{1,0:T(8,128)(2,1)S(1)} %add_convert_fusion.1.k_ref, bf16[1024,768]{1,0:T(8,128)(2,1)} %add_convert_fusion.v_ref, bf16[512,768]{1,0:T(8,128)(2,1)S(1)} %add_convert_fusion.4.rk_ref, ...), custom_call_target="tpu_custom_call" | custom-call | flops 20000000000 | bytes 10485760 | tf_op jit(solution)/shard_map/attn_fwd/pallas_call | solution.py:103
  62.0 0.9 fusion.46
  63.2 3.3 %multiply_convert_fusion = (bf16[512,3072]{1,0:T(8,128)(2,1)S(1)}, f32[512,3072]{1,0:T(8,128)S(1)}) fusion(f32[3072]{0:T(1024)S(1)} %convert_element_type.148, bf16[768,3072]{1,0:T(8,128)(2,1)S(1)} %bitcast.73, f32[512,768]{1,0:T(8,128)S(1)} %get-tuple-element.85, f32[768]{0:T(1024)S(1)} %convert_element_type.146, f32[768]{0:T(1024)S(1)} %convert_element_type.145, ...), kind=kOutput, calls=%fused_computation.7 | convolution fusion | flops 2427322368 | bytes 15751168 | tf_op jit(solution)/shard_map/dot_general | solution.py:20
  66.6 2.8 %fusion.47 = (f32[512]{0:T(512)S(1)}, f32[512,768]{1,0:T(8,128)S(1)}) fusion(f32[768]{0:T(1024)S(1)} %convert_element_type.150, bf16[512,3072]{1,0:T(8,128)(2,1)S(1)} %get-tuple-element.86, bf16[3072,768]{1,0:T(8,128)(2,1)S(1)} %bitcast.71, f32[768]{0:T(1024)S(1)} %convert_element_type.146, f32[768]{0:T(1024)S(1)} %convert_element_type.145, ...), kind=kOutput, calls=%fused_computation.128 | convolution fusion | flops 2418671104 | bytes 11025408 | tf_op jit(solution)/shard_map/dot_general | solution.py:20
  69.7 0.8 copy-done.6
  70.5 1.5 fusion.12
  72.6 4.9 %fusion.48 = (bf16[3072]{0:T(1024)(128)(2,1)S(1)}, bf16[512,3072]{1,0:T(8,128)(2,1)S(1)}) fusion(f32[512,3072]{1,0:T(8,128)S(1)} %get-tuple-element.87, f32[3072]{0:T(1024)S(1)} %convert_element_type.148, bf16[3072,768]{1,0:T(8,128)(2,1)S(1)} %bitcast.71, f32[512,768]{1,0:T(8,128)S(1)} %get-tuple-element.45), kind=kOutput, calls=%fused_computation.129 | convolution fusion | flops 2435183616 | bytes 15747072 | tf_op jit(solution)/shard_map/dot_general | solution.py:20
  77.5 3.1 %multiply_reduce_fusion = (bf16[768]{0:T(1024)(128)(2,1)S(1)}, f32[512]{0:T(512)S(1)}, f32[512]{0:T(512)S(1)}, bf16[768]{0:T(1024)(128)(2,1)S(1)}, f32[512,768]{1,0:T(8,128)S(1)}) fusion(f32[512,768]{1,0:T(8,128)S(1)} %get-tuple-element.85, f32[512]{0:T(512)S(1)} %add_rsqrt_fusion.1, f32[512]{0:T(512)S(1)} %broadcast_multiply_fusion.5, ...), kind=kOutput, calls=%fused_computation.23 | convolution fusion | flops 2419848704 | bytes 12597248 | tf_op jit(solution)/shard_map/dot_general | solution.py:20
  80.6 4.8 %convolution_convert_fusion = bf16[768,3072]{1,0:T(8,128)(2,1)} fusion(bf16[512,3072]{1,0:T(8,128)(2,1)S(1)} %get-tuple-element.92, f32[512,768]{1,0:T(8,128)S(1)} %get-tuple-element.85, f32[768]{0:T(1024)S(1)} %convert_element_type.146, f32[768]{0:T(1024)S(1)} %convert_element_type.145, f32[512]{0:T(512)S(1)} %add_rsqrt_fusion.1, ...), kind=kOutput, calls=%fused_computation.9 | convolution fusion | flops 2420244480 | bytes 9447424 | tf_op jit(solution)/shard_map/dot_general | solution.py:20
  85.4 4.4 %convolution_convert_fusion.1 = bf16[3072,768]{1,0:T(8,128)(2,1)} fusion(bf16[512,3072]{1,0:T(8,128)(2,1)S(1)} %get-tuple-element.86, f32[512,768]{1,0:T(8,128)S(1)} %get-tuple-element.45), kind=kOutput, calls=%fused_computation.10 | convolution fusion | flops 2418671616 | bytes 9437184 | tf_op jit(solution)/shard_map/dot_general | solution.py:20
  90.3 1.8 convolution_convert_fusion.2
  92.1 1.7 convolution_convert_fusion.3.g_ref
  94.7 2.3 pad_maximum_fusion.x_ref
  97.0 126.8 %attn_bwd_reduce.1 = (f32[512,768]{1,0:T(8,128)}, bf16[96,3072]{1,0:T(8,128)(2,1)}, bf16[96,3072]{1,0:T(8,128)(2,1)}, bf16[96,1024]{1,0:T(8,128)(2,1)}, bf16[96,...) custom-call(bf16[512,768]{1,0:T(8,128)(2,1)} %copy-done.2, bf16[1024,768]{1,0:T(8,128)(2,1)} %copy-done.5, ...), custom_call_target="tpu_custom_call" | custom-call | flops 49999998976 | bytes 20971520 | tf_op jit(solution)/shard_map/attn_bwd_reduce/pallas_call | solution.py:714
  223.7 0.9 slice.193
  229.4 0.8 slice.179
  230.2 0.8 constant_dynamic-update-slice_fusion.23
  231.0 1.2 fusion.43
  237.5 0.8 constant_dynamic-update-slice_fusion.22
  238.4 0.8 constant_dynamic-update-slice_fusion.18
  241.4 1.1 convert_element_type.172
  244.6 1.1 maximum_convert_fusion
  245.7 1.1 copy.61
  (140 shorter events, 20.9 us)
Async XLA Ops:
  0.7 61.3 %copy-start = (bf16[768,768]{1,0:T(8,128)(2,1)S(1)}, bf16[768,768]{1,0:T(8,128)(2,1)}, u32[]{:S(2)}) copy-start(bf16[768,768]{1,0:T(8,128)(2,1)} %param.27) | copy-start | bytes 3538948
  0.7 7.1 %copy-start.29 = (bf16[512,768]{1,0:T(8,128)(2,1)S(1)}, bf16[512,768]{1,0:T(8,128)(2,1)}, u32[]{:S(2)}) copy-start(bf16[512,768]{1,0:T(8,128)(2,1)} %param.37) | copy-start | bytes 2359300
  2.9 5.5 %copy-start.17 = (bf16[768]{0:T(1024)(128)(2,1)S(1)}, bf16[768]{0:T(1024)(128)(2,1)}, u32[]{:S(2)}) copy-start(bf16[768]{0:T(1024)(128)(2,1)} %param.22) | copy-start | bytes 4612
  2.9 5.5 %copy-start.8 = (bf16[1,512,768]{2,1,0:T(8,128)(2,1)S(1)}, bf16[1,512,768]{2,1,0:T(8,128)(2,1)}, u32[]{:S(2)}) copy-start(bf16[1,512,768]{2,1,0:T(8,128)(2,1)} %param.20) | copy-start | bytes 2359300
  2.9 13.2 %collective-permute-start = (bf16[256,768]{1,0:T(8,128)(2,1)}, bf16[256,768]{1,0:T(8,128)(2,1)S(1)}, u32[]{:S(2)}, u32[]{:S(2)}) collective-permute-start(bf16[256,768]{1,0:T(8,128)(2,1)} %get-tuple-element.49), channel_id=1, source_target_pairs={{0,8},{8,16},{16,24},{1,9},{9,17},{17,25},{2,10},{10,18},{18,26},{... | collective-permute-start | bytes 1179656 | tf_op jit(solution)/shard_map/ppermute | solution.py:793
  6.4 19.0 %collective-permute-start.1 = (bf16[256,768]{1,0:T(8,128)(2,1)}, bf16[256,768]{1,0:T(8,128)(2,1)}, u32[]{:S(2)}, u32[]{:S(2)}) collective-permute-start(bf16[256,768]{1,0:T(8,128)(2,1)} %get-tuple-element.50), channel_id=1, source_target_pairs={{8,0},{16,8},{24,16},{9,1},{17,9},{25,17},{10,2},{18,10},{26,18},{... | collective-permute-start | bytes 1179656 | tf_op jit(solution)/shard_map/ppermute | solution.py:794
  9.8 22.1 %copy-start.2 = (bf16[512,768]{1,0:T(8,128)(2,1)}, bf16[512,768]{1,0:T(8,128)(2,1)S(1)}, u32[]{:S(2)}) copy-start(bf16[512,768]{1,0:T(8,128)(2,1)S(1)} %add_convert_fusion.5.q_ref) | copy-start | bytes 2359300
  9.8 2.0 copy-start.15
  9.8 2.3 copy-start.18
  9.9 2.3 copy-start.19
  9.9 2.3 copy-start.20
  9.9 2.3 copy-start.21
  9.9 2.3 copy-start.22
  9.9 2.3 copy-start.16
  9.9 2.3 copy-start.23
  9.9 2.3 copy-start.24
  9.9 2.4 copy-start.25
  10.7 21.2 %copy-start.3 = (bf16[512,768]{1,0:T(8,128)(2,1)}, bf16[512,768]{1,0:T(8,128)(2,1)S(1)}, u32[]{:S(2)}) copy-start(bf16[512,768]{1,0:T(8,128)(2,1)S(1)} %add_convert_fusion.3.rq_ref) | copy-start | bytes 2359300
  13.6 11.8 %copy-start.9 = (bf16[1,512,768]{2,1,0:T(8,128)(2,1)S(1)}, bf16[1,512,768]{2,1,0:T(8,128)(2,1)}, u32[]{:S(2)}) copy-start(bf16[1,512,768]{2,1,0:T(8,128)(2,1)} %param.20) | copy-start | bytes 2359300
  13.6 11.8 %copy-start.27 = (bf16[768,768]{1,0:T(8,128)(2,1)S(1)}, bf16[768,768]{1,0:T(8,128)(2,1)}, u32[]{:S(2)}) copy-start(bf16[768,768]{1,0:T(8,128)(2,1)} %wk_ref.1) | copy-start | bytes 3538948
  16.1 15.9 %copy-start.4 = (bf16[512,768]{1,0:T(8,128)(2,1)}, bf16[512,768]{1,0:T(8,128)(2,1)S(1)}, u32[]{:S(2)}) copy-start(bf16[512,768]{1,0:T(8,128)(2,1)S(1)} %add_convert_fusion.4.rk_ref) | copy-start | bytes 2359300
  25.4 2.5 %copy-start.28 = (bf16[768,768]{1,0:T(8,128)(2,1)S(1)}, bf16[768,768]{1,0:T(8,128)(2,1)}, u32[]{:S(2)}) copy-start(bf16[768,768]{1,0:T(8,128)(2,1)} %wv_ref.1) | copy-start | bytes 3538948
  27.9 4.0 %copy-start.5 = (bf16[1024,768]{1,0:T(8,128)(2,1)}, bf16[1024,768]{1,0:T(8,128)(2,1)S(1)}, u32[]{:S(2)}) copy-start(bf16[1024,768]{1,0:T(8,128)(2,1)S(1)} %add_convert_fusion.1.k_ref) | copy-start | bytes 4718596
  28.0 35.2 %slice-start.2 = ((s8[4718592]{0:T(1024)(128)(4,1)}), s8[4194304]{0:T(1024)(128)(4,1)S(1)}, s32[]{:S(2)}) async-start(s8[4718592]{0:T(1024)(128)(4,1)} %bitcast.72), calls=%async_computation.2 | async-start | bytes 8388608
  32.0 31.2 %slice-start.3 = ((s8[4718592]{0:T(1024)(128)(4,1)}), s8[524288]{0:T(1024)(128)(4,1)S(1)}, s32[]{:S(2)}) async-start(s8[4718592]{0:T(1024)(128)(4,1)} %bitcast.72), calls=%async_computation.3 | async-start | bytes 1048576
  62.9 3.7 %slice-start = ((s8[4718592]{0:T(1024)(128)(4,1)}), s8[4194304]{0:T(1024)(128)(4,1)S(1)}, s32[]{:S(2)}) async-start(s8[4718592]{0:T(1024)(128)(4,1)} %bitcast.70), calls=%async_computation | async-start | bytes 8388608
  63.2 3.3 %slice-start.1 = ((s8[4718592]{0:T(1024)(128)(4,1)}), s8[524288]{0:T(1024)(128)(4,1)S(1)}, s32[]{:S(2)}) async-start(s8[4718592]{0:T(1024)(128)(4,1)} %bitcast.70), calls=%async_computation.1 | async-start | bytes 1048576
  92.1 2.6 %copy-start.10 = (bf16[1,512,768]{2,1,0:T(8,128)(2,1)S(1)}, bf16[1,512,768]{2,1,0:T(8,128)(2,1)}, u32[]{:S(2)}) copy-start(bf16[1,512,768]{2,1,0:T(8,128)(2,1)} %param.20) | copy-start | bytes 2359300
  223.7 8.5 %copy-start.13 = (bf16[96,1024]{1,0:T(8,128)(2,1)S(1)}, bf16[96,1024]{1,0:T(8,128)(2,1)}, u32[]{:S(2)}) copy-start(bf16[96,1024]{1,0:T(8,128)(2,1)} %get-tuple-element.32) | copy-start | bytes 589828
  223.7 8.5 %copy-start.14 = (bf16[96,1024]{1,0:T(8,128)(2,1)S(1)}, bf16[96,1024]{1,0:T(8,128)(2,1)}, u32[]{:S(2)}) copy-start(bf16[96,1024]{1,0:T(8,128)(2,1)} %get-tuple-element.33) | copy-start | bytes 589828
  231.0 10.5 %copy-start.12 = (bf16[96,3072]{1,0:T(8,128)(2,1)S(1)}, bf16[96,3072]{1,0:T(8,128)(2,1)}, u32[]{:S(2)}) copy-start(bf16[96,3072]{1,0:T(8,128)(2,1)} %get-tuple-element.35) | copy-start | bytes 1769476
  242.5 3.2 %copy-start.11 = (f32[512,768]{1,0:T(8,128)S(1)}, f32[512,768]{1,0:T(8,128)}, u32[]{:S(2)}) copy-start(f32[512,768]{1,0:T(8,128)} %get-tuple-element.30) | copy-start | bytes 4718596
  (5 other events, 7.5 us)

commit v3 on v2

--- a/solution.py
+++ b/solution.py
@@ -3,17 +3,26 @@
 
 import jax
 import jax.numpy as jnp
+import numpy as np
 from jax import lax
 from jax.experimental import pallas as pl
 from jax.experimental.pallas import tpu as pltpu
 from jax.sharding import PartitionSpec as P
 
-HEADS = 12
 F32 = jnp.float32
 BF = jnp.bfloat16
 NN = (((1,), (0,)), ((), ()))
 NT = (((1,), (1,)), ((), ()))
 TN = (((0,), (0,)), ((), ()))
+MESH = pl.DeviceIdType.MESH
+
+
+def toggled(value, mask):
+    out = value
+    for bit in range(mask.bit_length()):
+        if mask >> bit & 1:
+            out = out + (1 - 2 * ((value // (1 << bit)) % 2)) * (1 << bit)
+    return out
 
 
 def dot(a, b, dims=NN):
@@ -44,80 +53,204 @@
     return pltpu.roll(x, shift, 1, stride=1, stride_axis=0)
 
 
-def fwd_kernel(n, scale, q_ref, k_ref, v_ref, rk_ref, rq_ref, qid_ref, kid_ref, ctx_ref, p_ref, bias_ref, mask_ref, rqm_ref):
-    nq = q_ref.shape[0] // n
+def fwd_tile(n, scale, pair, qt, q_ref, k_ref, v_ref, rk_ref, rqm_ref, bias_ref, mask_ref, p_ref):
     factor = scale * math.log2(math.e)
     row, lane = grid_of(n)
-    right = lane > row
-
-    @pl.when(pl.program_id(0) == 0)
+    right, upper = lane > row, row + lane >= n - 1
+    lanes = pl.ds(pl.multiple_of(pair * 128, 128), 128)
+    at = lambda m: (pl.ds(pl.multiple_of((qt + m) * n, n), n), lanes)
+    qb = q_ref[at(0)]
+    rk_low, rk_high = rk_ref[0:n, lanes], rk_ref[n:, lanes]
+    outs = []
+    for hh in range(2):
+        qm = head_lanes(qb, hh)
+        low, high = rqm_ref[hh, 0:n, lanes], rqm_ref[hh, n:, lanes]
+        to_low = sheared(dot(qm, rk_low, NT), 1)
+        to_high = sheared(dot(qm, rk_high, NT), 1)
+        side = jnp.where(right, dot(qm, k_ref[at(0)], NT) + to_low, dot(qm, k_ref[at(2)], NT) + to_high)
+        middle = dot(qm, k_ref[at(1)], NT) + jnp.where(right, to_high, to_low)
+        key_side = jnp.where(upper, dot(k_ref[at(0)], high, NT), dot(k_ref[at(2)], low, NT))
+        key_middle = jnp.where(upper, dot(k_ref[at(1)], low, NT), dot(k_ref[at(1)], high, NT))
+        side = (side + sheared(key_side, 1).T) * factor + bias_ref[:, 0:n]
+        middle = (middle + sheared(key_middle, 1).T) * factor + bias_ref[:, n:]
+        top = jnp.max(jnp.maximum(side, middle), axis=-1, keepdims=True)
+        side, middle = jnp.exp2(side - top), jnp.exp2(middle - top)
+        inverse = 1.0 / jnp.sum(side + middle, axis=-1, keepdims=True)
+        side, middle = (side * inverse).astype(BF), (middle * inverse).astype(BF)
+        p_ref[hh, :, 0:n] = side
+        p_ref[hh, :, n:] = middle
+        out = dot(side * mask_ref[0], v_ref[at(0)]) + dot(middle, v_ref[at(1)])
+        outs.append(out + dot(side * mask_ref[1], v_ref[at(2)]))
+    return both_heads(*outs).astype(BF)
+
+
+class Halo:
+    def __init__(self, span, block, ext_ref, sems):
+        self.span, self.block, self.ext_ref, self.sems = span, block, ext_ref, sems
+        self.s, self.b, self.ns = lax.axis_index("seq"), lax.axis_index("batch"), lax.axis_size("seq")
+
+    def greet(self):
+        barrier = pltpu.get_barrier_semaphore()
+        for step in range(1, self.ns):
+            peer = {"seq": toggled(self.s, step), "batch": self.b}
+            pl.semaphore_signal(barrier, inc=1, device_id=peer, device_id_type=MESH)
+        pl.semaphore_wait(barrier, self.ns - 1)
+
+    def copy(self, up):
+        span, block = self.span, self.block
+        src, dst = (block, 0) if up else (span, span + block)
+        return pltpu.make_async_remote_copy(
+            src_ref=self.ext_ref.at[pl.ds(src, span)],
+            dst_ref=self.ext_ref.at[pl.ds(dst, span)],
+            send_sem=self.sems.at[0, int(up)],
+            recv_sem=self.sems.at[1, int(up)],
+            device_id={"seq": self.s + (1 if up else -1), "batch": self.b},
+            device_id_type=MESH,
+        )
+
+    def sends(self, up):
+        return self.s < self.ns - 1 if up else self.s > 0
+
+    def gets(self, up):
+        return self.s > 0 if up else self.s < self.ns - 1
+
+    def start(self, up):
+        pl.when(self.sends(up))(lambda: self.copy(up).start())
+
+    def wait(self, up):
+        at = pl.ds(0 if up else self.span + self.block, self.span)
+        pl.when(self.gets(up))(lambda: self.copy(up).wait_recv())
+
+        @pl.when(jnp.logical_not(self.gets(up)))
+        def _():
+            self.ext_ref[at] = jnp.zeros((self.span, self.ext_ref.shape[1]), BF)
+
+    def finish(self):
+        for up in (True, False):
+            pl.when(self.sends(up))(lambda up=up: self.copy(up).wait_send())
+
+
+def fwd_kernel(n, scale, x_hbm, rel_hbm, wk_hbm, wq_hbm, wv_hbm, bq_ref, bk_ref, bv_ref, qid_ref, kid_ref,
+               ctx_ref, p_ref, q_out, k_out, v_out, rk_out, rq_out, xt_out,
+               q_ref, k_ref, v_ref, rk_ref, rq_ref, xt_ref, ext_ref, rel_ref, flip_ref, wk_ref, wq_ref, wv_ref,
+               rqm_ref, bias_ref, mask_ref, halo_sem, in_sem, out_sem):
+    block = x_hbm.shape[0]
+    ext = block + 2 * n
+    qt, pair = pl.program_id(0), pl.program_id(1)
+    last = (qt == pl.num_programs(0) - 1) & (pair == pl.num_programs(1) - 1)
+    halo = Halo(n, block, ext_ref, halo_sem)
+    row, lane = grid_of(n)
+    bias_of = lambda ref: ref[...].astype(F32)[None]
+    own = slice(n, n + block)
+    kept = ((q_ref, q_out), (rk_ref, rk_out), (rq_ref, rq_out), (k_ref, k_out), (v_ref, v_out), (xt_ref, xt_out))
+    loads = ((x_hbm, ext_ref.at[pl.ds(n, block)]), (rel_hbm, rel_ref), (wk_hbm, wk_ref), (wq_hbm, wq_ref), (wv_hbm, wv_ref))
+
+    def load(m):
+        return pltpu.make_async_copy(*loads[m], in_sem.at[m])
+
+    def keep(first, end):
+        for m in range(first, end):
+            yield pltpu.make_async_copy(*kept[m], out_sem.at[m])
+
+    def keys(rows):
+        k_ref[rows] = (dot(ext_ref[rows], wk_ref[...]) + bias_of(bk_ref)).astype(BF)
+        v_ref[rows] = (dot(ext_ref[rows], wv_ref[...]) + bias_of(bv_ref)).astype(BF)
+
+    def turn(ref, first, size, at):
+        for m in range(0, size, 128):
+            xt_ref[:, at + m : at + m + 128] = ref[first + m : first + m + 128, :].astype(F32).T.astype(BF)
+
+    def get_after():
+        halo.wait(False)
+        keys(slice(n + block, ext))
+        turn(ext_ref, n + block, n, n + block)
+        for copy in keep(3, 6):
+            copy.start()
+
+    @pl.when((qt == 0) & (pair == 0))
     def _():
-        for qt in range(nq):
-            qid = qid_ref[qt * n : (qt + 1) * n, :]
-            first, middle, third = [kid_ref[:, (qt + m) * n : (qt + m + 1) * n] for m in range(3)]
-            side = (right & (qid == first)) | ((lane < row) & (qid == third))
-            bias_ref[qt, :, 0:n] = jnp.where(side, 0.0, -1e30)
-            bias_ref[qt, :, n:] = jnp.where(qid == middle, 0.0, -1e30)
-        mask_ref[0] = jnp.where(right, 1.0, 0.0).astype(BF)
-        mask_ref[1] = jnp.where(right, 0.0, 1.0).astype(BF)
-
-    for hh in range(2):
-        rqm_ref[hh] = head_lanes(rq_ref[...], hh)
-
-    def tile(qt, carry):
+        for m in range(5):
+            load(m).start()
+        halo.greet()
+        load(0).wait()
+        halo.start(True)
+        load(1).wait()
+        flip_ref[...] = dot(anti(2 * n), rel_ref[...]).astype(BF)
+        load(2).wait()
+        rk_ref[...] = (dot(flip_ref[...], wk_ref[...]) + bias_of(bk_ref)).astype(BF)
+        load(3).wait()
+        rq_ref[...] = (dot(flip_ref[...], wq_ref[...]) + bias_of(bq_ref)).astype(BF)
+        q_ref[...] = (dot(ext_ref[own], wq_ref[...]) + bias_of(bq_ref)).astype(BF)
+        for copy in keep(0, 3):
+            copy.start()
+        load(4).wait()
+        keys(own)
+        head = (lax.broadcasted_iota(jnp.int32, rq_ref.shape, 1) // 64) % 2
+        for hh in range(2):
+            rqm_ref[hh] = jnp.where(head == hh, rq_ref[...].astype(F32), 0.0).astype(BF)
+        mask_ref[0] = jnp.where(lane > row, 1.0, 0.0).astype(BF)
+        mask_ref[1] = jnp.where(lane > row, 0.0, 1.0).astype(BF)
+        turn(ext_ref, n, block, n)
+        turn(flip_ref, 0, 2 * n, ext)
+        halo.wait(True)
+        halo.start(False)
+        keys(slice(0, n))
+        turn(ext_ref, 0, n, 0)
+        if block == n:
+            get_after()
+
+    if block > n:
+        pl.when((qt == 1) & (pair == 0))(get_after)
+
+    @pl.when(pair == 0)
+    def _():
         at = lambda m: pl.ds(pl.multiple_of((qt + m) * n, n), n)
-        qb = q_ref[at(0), :]
-        outs = []
-        for hh in range(2):
-            qm = head_lanes(qb, hh)
-            low, high = rqm_ref[hh, 0:n], rqm_ref[hh, n:]
-            to_low = sheared(dot(qm, rk_ref[0:n], NT), 1)
-            to_high = sheared(dot(qm, rk_ref[n:], NT), 1)
-            side = jnp.where(right, dot(qm, k_ref[at(0), :], NT) + to_low, dot(qm, k_ref[at(2), :], NT) + to_high)
-            middle = dot(qm, k_ref[at(1), :], NT) + jnp.where(right, to_high, to_low)
-            upper = row + lane >= n - 1
-            key_side = jnp.where(upper, dot(k_ref[at(0), :], high, NT), dot(k_ref[at(2), :], low, NT))
-            key_middle = jnp.where(upper, dot(k_ref[at(1), :], low, NT), dot(k_ref[at(1), :], high, NT))
-            side = (side + sheared(key_side, 1).T) * factor + bias_ref[qt, :, 0:n]
-            middle = (middle + sheared(key_middle, 1).T) * factor + bias_ref[qt, :, n:]
-            top = jnp.max(jnp.maximum(side, middle), axis=-1, keepdims=True)
-            side, middle = jnp.exp2(side - top), jnp.exp2(middle - top)
-            inverse = 1.0 / jnp.sum(side + middle, axis=-1, keepdims=True)
-            side, middle = (side * inverse).astype(BF), (middle * inverse).astype(BF)
-            p_ref[hh, at(0), 0:n] = side
-            p_ref[hh, at(0), n:] = middle
-            out = dot(side * mask_ref[0], v_ref[at(0), :]) + dot(middle, v_ref[at(1), :])
-            outs.append(out + dot(side * mask_ref[1], v_ref[at(2), :]))
-        ctx_ref[at(0), :] = both_heads(*outs).astype(BF)
-        return carry
-
-    lax.fori_loop(0, nq, tile, 0)
-
-
-def attn_fwd(span, q, k, v, rk, rq, qid, kid):
-    block, width = q.shape
-    ext = k.shape[0]
+        qid = qid_ref[at(0), :]
+        first, middle, third = [kid_ref[:, at(m)] for m in range(3)]
+        side = ((lane > row) & (qid == first)) | ((lane < row) & (qid == third))
+        bias_ref[:, 0:n] = jnp.where(side, 0.0, -1e30)
+        bias_ref[:, n:] = jnp.where(qid == middle, 0.0, -1e30)
+
+    ctx_ref[...] = fwd_tile(n, scale, pair, qt, q_ref, k_ref, v_ref, rk_ref, rqm_ref, bias_ref, mask_ref, p_ref)
+
+    @pl.when(last)
+    def _():
+        halo.finish()
+        for copy in keep(0, 6):
+            copy.wait()
+
+
+def attn_fwd(span, x, rel_table, w_query, w_key, w_value, b_query, b_key, b_value, qid, kid):
+    block, width = x.shape
+    ext, table = block + 2 * span, 2 * span
     scale = (3.0 * 64) ** -0.5
-    col = lambda rows: pl.BlockSpec((rows, 128), lambda h: (0, h))
-    whole = lambda shape: pl.BlockSpec(shape, lambda h: (0, 0))
+    heads = width // 64
+    whole = lambda shape: pl.BlockSpec(shape, lambda t, h: (0,) * len(shape), pipeline_mode=pl.Buffered(1))
+    far = pl.BlockSpec(memory_space=pltpu.HBM)
+    small = [b_query, b_key, b_value, qid, kid]
+    kept = [(rows, width) for rows in (block, ext, ext, table, table)] + [(width, ext + table)]
+    more = [(ext, width), (table, width), (table, width)] + [(width, width)] * 3
     return pl.pallas_call(
         functools.partial(fwd_kernel, span, scale),
-        grid=(HEADS // 2,),
-        out_shape=(
-            jax.ShapeDtypeStruct((block, width), BF),
-            jax.ShapeDtypeStruct((HEADS, block, 2 * span), BF),
-        ),
-        in_specs=[col(block), col(ext), col(ext), col(2 * span), col(2 * span), whole((block, 1)), whole((1, ext))],
-        out_specs=(col(block), pl.BlockSpec((2, block, 2 * span), lambda h: (h, 0, 0))),
-        scratch_shapes=[
-            pltpu.VMEM((block // span, span, 2 * span), F32),
+        grid=(block // span, width // 128),
+        out_shape=[jax.ShapeDtypeStruct((block, width), BF), jax.ShapeDtypeStruct((heads, block, table), BF)]
+        + [pltpu.HBM(shape, BF) for shape in kept],
+        in_specs=[far] * 5 + [whole(arg.shape) for arg in small],
+        out_specs=[pl.BlockSpec((span, 128), lambda t, h: (t, h)), pl.BlockSpec((2, span, table), lambda t, h: (h, t, 0))]
+        + [far] * 6,
+        scratch_shapes=[pltpu.VMEM(shape, BF) for shape in kept + more]
+        + [
+            pltpu.VMEM((2, table, width), BF),
+            pltpu.VMEM((span, table), F32),
             pltpu.VMEM((2, span, span), BF),
-            pltpu.VMEM((2, 2 * span, 128), BF),
+            pltpu.SemaphoreType.DMA((2, 2)),
+            pltpu.SemaphoreType.DMA((5,)),
+            pltpu.SemaphoreType.DMA((6,)),
         ],
-        compiler_params=pltpu.CompilerParams(vmem_limit_bytes=48 << 20),
-        cost_estimate=pl.CostEstimate(flops=20_000_000_000, bytes_accessed=10 << 20, transcendentals=HEADS * block * 2 * span),
+        compiler_params=pltpu.CompilerParams(collective_id=1, has_side_effects=True, vmem_limit_bytes=44 << 20),
+        cost_estimate=pl.CostEstimate(flops=20_000_000_000, bytes_accessed=20 << 20, transcendentals=heads * block * table),
         name="attn_fwd",
-    )(q, k, v, rk, rq, qid, kid)
+    )(*[pltpu.with_memory_space_constraint(arg, pltpu.HBM) for arg in (x, rel_table, w_key, w_query, w_value)], *small)
 
 
 def bwd_tile(n, scale, qt, q_ref, k_ref, v_ref, g_ref, rk_ref, rq_ref, p_ref, mask_ref, kjt_ref, dk_acc, dvt_acc, drkt_acc, drqt_acc):
@@ -177,17 +310,6 @@
         mask_ref[m] = jnp.where(keep, 1.0, 0.0).astype(BF)
 
 
-MESH = pl.DeviceIdType.MESH
-
-
-def toggled(value, mask):
-    out = value
-    for bit in range(mask.bit_length()):
-        if mask >> bit & 1:
-            out = out + (1 - 2 * ((value // (1 << bit)) % 2)) * (1 << bit)
-    return out
-
-
 class Mesh:
     def __init__(self, ns, nb):
         self.ns, self.nb, self.nz = ns, nb, nb // 2
@@ -231,7 +353,7 @@
         dma = pltpu.SemaphoreType.DMA
         moves = len(self.moves)
         shapes += [] if self.box else [dma((moves,))]
-        shapes += [dma((2, moves)), dma((2, 2, mesh.bits)), dma((2, 2, mesh.nz - 1)), dma((2, 2, mesh.ns - 1))]
+        shapes += [dma((2, moves)), dma((2, 2, mesh.bits)), dma((2, 2, mesh.nz - 1)), dma((2, 2, mesh.bits))]
         return shapes
 
     def bind(self, refs):
@@ -318,13 +440,17 @@
                 other * 2 + mesh.c,
             )
 
-    def out_copies(self, half):
-        kept, unused, size = self.region(self.mesh.bits, half)
-        for step in range(1, self.mesh.ns):
-            lanes = self.span(kept, size)
-            yield self.copy(
-                self.final.at[:, lanes], self.final.at[:, lanes], self.out_sem, (half, step - 1), toggled(self.mesh.s, step), self.mesh.b
-            )
+    def out_copy(self, level, half):
+        kept, unused, size = self.region(level + 1, half)
+        lanes = self.span(kept, size)
+        return self.copy(
+            self.final.at[:, lanes],
+            self.final.at[:, lanes],
+            self.out_sem,
+            (half, level),
+            toggled(self.mesh.s, 1 << self.order(half, level)),
+            self.mesh.b,
+        )
 
     def start_core(self):
         for copy in self.core_copies():
@@ -392,10 +518,9 @@
             else:
                 self.final[:, lanes] = total.astype(BF)
 
-    def start_out(self):
+    def start_out(self, level):
         for half in range(self.mesh.ways):
-            for copy in self.out_copies(half):
-                copy.start()
+            self.out_copy(level, half).start()
 
     def core(self):
         self.start_core()
@@ -423,12 +548,19 @@
             self.end_seq()
         else:
             self.add_z()
-        self.start_out()
+        self.start_out(self.mesh.bits - 1)
+
+    def out2(self):
+        for level in reversed(range(self.mesh.bits - 1)):
+            for half in range(self.mesh.ways):
+                self.out_copy(level + 1, half).wait_recv()
+            self.start_out(level)
 
     def finish(self):
         for half in range(self.mesh.ways):
-            for copy in self.out_copies(half):
-                copy.wait()
+            self.out_copy(0, half).wait()
+            for level in range(1, self.mesh.bits):
+                self.out_copy(level, half).wait_send()
             for copy in self.z_copies(half):
                 copy.wait_send()
             for level in range(self.mesh.bits):
@@ -450,49 +582,63 @@
         self.small_at = 384 + 512
         self.stack = rows // 16
         small_lanes = -(-self.pairs // self.stack) * 128
-        down = [
-            (lambda c, n=n: self.down_ref.at[:, c, pl.ds(n * rows, rows), :], n * width, width) for n in range(self.fold)
-        ]
-        into = [(lambda c: self.in_ref.at[:, c], 0, hidden)]
-        self.down = Chunk(mesh, rows, self.fold * width, down)
-        self.into = Chunk(mesh, rows, hidden, into)
+        self.split = split = hidden // 3
+        whole = lambda name, lanes: self.boxed(lambda c: getattr(self, name).at[:, c], lanes)
+        self.down = whole("down_ref", self.fold * width)
+        self.into = whole("into_ref", hidden - split)
+        self.rest = whole("rest_ref", split)
         lanes = Chunk(mesh, rows, 768 + self.third, []).lanes
-        self.near = []
-        for n in range(3):
-            box = lambda c, n=n: self.near_ref.at[n, :, c]
-            self.near.append(Chunk(mesh, rows, lanes, [(box, 0, lanes)], box, early_z=n < 0))
-        lanes = Chunk(mesh, rows, self.small_at + small_lanes, []).lanes
-        far = lambda c: self.far_ref.at[:, c]
-        self.far = Chunk(mesh, rows, lanes, [(far, 0, lanes)], far)
-        self.chunks = [self.down, self.into, *self.near, self.far]
+        self.near = [self.boxed(lambda c, n=n: self.near_ref.at[n, :, c], lanes) for n in range(3)]
+        self.far = whole("far_ref", self.small_at + small_lanes)
+        self.chunks = [self.down, self.into, self.rest, *self.near, self.far]
+
+    def boxed(self, box, lanes):
+        chunk = Chunk(self.mesh, self.rows, lanes, [])
+        chunk.box, chunk.moves = box, [(box, 0, chunk.lanes)]
+        return chunk
+
+    def starts(self):
+        at = 0
+        for chunk in self.chunks:
+            yield at
+            at += chunk.lanes
 
     def scratch(self):
         mesh = self.mesh
-        shapes = [
-            pltpu.VMEM((3, mesh.nz, 2, self.rows, self.near[0].lanes), BF),
-            pltpu.VMEM((mesh.nz, 2, self.rows, self.far.lanes), BF),
-            pltpu.SemaphoreType.DMA((3,)),
-        ]
+        box = lambda lanes: pltpu.VMEM((mesh.nz, 2, self.rows, lanes), BF)
+        shapes = [box(chunk.lanes) for chunk in (self.down, self.into, self.rest, self.far)]
+        shapes.append(pltpu.VMEM((3, mesh.nz, 2, self.rows, self.near[0].lanes), BF))
         for chunk in self.chunks:
             shapes += chunk.scratch()
         return shapes
 
-    def bind(self, down_ref, in_ref, out_ref, refs):
+    def bind(self, refs):
         self.mesh.locate()
-        self.down_ref, self.in_ref, self.out_ref = down_ref, in_ref, out_ref
-        self.near_ref, self.far_ref, self.out_sem = refs[:3]
-        refs = refs[3:]
+        self.down_ref, self.into_ref, self.rest_ref, self.far_ref, self.near_ref = refs[:5]
+        refs = refs[5:]
         for chunk in self.chunks:
             refs = chunk.bind(refs)
         return refs
 
-    def out_copies(self):
-        for n in range(3):
-            yield pltpu.make_async_copy(
-                self.out_ref.at[:, :, :, pl.ds(n * self.third, self.third)],
-                self.near_ref.at[n, :, :, :, pl.ds(768, self.third)],
-                self.out_sem.at[n],
-            )
+    def store_down(self, m, grads):
+        rows, share = self.rows, self.rows * self.fold
+        for n in range(self.width // rows):
+            b, part = divmod(m * self.width + n * rows, share)
+            lanes = slice(part // rows * self.width, (part // rows + 1) * self.width)
+            self.down_ref[b // 2, b % 2, :, lanes] = grads[n * rows : (n + 1) * rows]
+
+    def store_into(self, m, grads):
+        rows, split = self.rows, self.split
+        ref, lanes = (self.rest_ref, slice(0, split)) if m == 0 else (self.into_ref, slice((m - 1) * split, m * split))
+        for b in range(self.mesh.nb):
+            ref[b // 2, b % 2, :, lanes] = grads[b * rows : (b + 1) * rows]
+
+    def store_out(self, grads):
+        rows, third = self.rows, self.third
+        for b in range(self.mesh.nb):
+            for n in range(3):
+                part = grads[b * rows : (b + 1) * rows, n * third : (n + 1) * third]
+                self.near_ref[n, b // 2, b % 2, :, 768 : 768 + third] = part
 
     def store_pair(self, pair, grads):
         rows = self.rows
@@ -521,51 +667,45 @@
                 row, lane = (n % self.stack) * 16, self.small_at + (n // self.stack) * 128
                 put[row : row + 16, lane : lane + 128] = vectors[:, n * 128 : (n + 1) * 128]
 
-    def rel_of(self, far):
-        take, at, half = self.rel_rows, self.rel_at, self.rel_rows // 2
-        low = [far[take : take + half, at : at + 256], far[take : take + half, at + 256 : at + 512]]
-        return jnp.concatenate([far[0:take, at : at + 512], jnp.concatenate(low, axis=0)], axis=1)
-
-    def vectors_of(self, far):
-        parts = []
-        for n in range(self.pairs):
-            row, lane = (n % self.stack) * 16, self.small_at + (n // self.stack) * 128
-            parts.append(far[row : row + 16, lane : lane + 128])
-        return jnp.concatenate(parts, axis=1)
-
-    def pairs_of(self, near, far, n):
-        blocks = [side[:, m * 384 + n * 128 : m * 384 + (n + 1) * 128] for side in near for m in range(2)][: self.pairs - 1]
-        return jnp.concatenate(blocks + [far[:, n * 128 : (n + 1) * 128]], axis=1)
-
     def schedule(self, edges):
-        down, into, one, two, three, far = self.chunks
-
-        def open_all():
-            self.mesh.greet()
-            for copy in self.out_copies():
-                copy.start()
-            down.core()
-            into.core()
-
-        def open_near():
-            for copy in self.out_copies():
-                copy.wait()
-            one.core()
+        down, into, rest, one, two, three, far = self.chunks
 
         steps = {
-            0: [open_all],
+            0: [],
             1: [down.s0],
-            2: [into.s0],
-            4: [down.s1, open_near],
-            5: [one.s0],
-            6: [into.s1],
-            7: [down.z],
-            8: [one.s1, two.core],
-            9: [into.z, two.s0],
-            10: [down.out, three.core, one.z],
-            11: [three.s0, two.s1],
+            3: [into.s0, rest.s0],
+            6: [down.s1, one.core],
+            7: [one.s0],
+            9: [into.s1, rest.s1],
+            10: [down.z],
+            12: [one.s1, two.core],
+            13: [into.z, rest.z, two.s0],
+            15: [down.out, three.core, one.z],
+            16: [three.s0, two.s1],
         }
-        last = [far.core, into.out, one.out, two.z, three.s1, far.s0, edges.start, two.out, three.z, far.s1, three.out, far.z, far.out]
+        last = [
+            far.core,
+            down.out2,
+            into.out,
+            rest.out,
+            one.out,
+            two.z,
+            three.s1,
+            far.s0,
+            edges.start,
+            into.out2,
+            rest.out2,
+            one.out2,
+            two.out,
+            three.z,
+            far.s1,
+            two.out2,
+            three.out,
+            far.z,
+            three.out2,
+            far.out,
+            far.out2,
+        ]
         last += [chunk.finish for chunk in self.chunks]
         return steps, last
 
@@ -604,10 +744,12 @@
 
 
 def bwd_kernel(tq, scale, layout, q_ref, k_ref, v_ref, g_ref, rk_ref, rq_ref, p_ref, wk_ref, wq_ref, wv_ref,
-               g_one_ref, x_ref, rel_ref, picks_ref, small_ref, down_ref, in_ref, out_ref,
-               dx_ref, down_out, in_out, near0_out, near1_out, near2_out, far_out,
+               act_hbm, branch_ref, hidden_ref, pre_hbm, ctx_hbm, attn_hbm, g_one_hbm, xt_hbm, picks_ref, *rest):
+    small_refs, rest = rest[:7], rest[7:]
+    (dx_ref, packed_hbm,
                mask_ref, kjt_ref, dk_acc, dvt_acc, drkt_acc, drqt_acc,
-               xt_ref, d_ref, rel_acc, vec_ref, dx_acc, sent_ref, got_ref, edge_sem, *refs):
+               xt_ref, d_ref, rel_acc, vec_ref, dx_acc, sent_ref, got_ref, edge_sem,
+     load_ref, load_sem, side_sem, packed_sem, *refs) = rest
     block = q_ref.shape[0]
     nq = block // tq
     ext = k_ref.shape[0]
@@ -617,7 +759,7 @@
     pair = pl.program_id(0)
     pairs = layout.pairs
     flip = anti(tq)
-    layout.bind(down_ref, in_ref, out_ref, refs)
+    layout.bind(refs)
     edges = Edges(layout.mesh, (sent_ref, got_ref, edge_sem))
     steps, last = layout.schedule(edges)
 
@@ -627,18 +769,57 @@
                 action()
         return all_of
 
+    loads = [act_hbm.at[:, pl.ds(m * layout.width, layout.width)] for m in range(layout.fold)]
+    loads += [pre_hbm.at[:, pl.ds(m * layout.split, layout.split)] for m in range(3)]
+    loads += [ctx_hbm, attn_hbm]
+
+    def load(m):
+        size = loads[m].shape
+        return pltpu.make_async_copy(loads[m], load_ref.at[m % 3, pl.ds(0, size[0]), pl.ds(0, size[1])], load_sem.at[m % 3])
+
+    def loaded(m):
+        size = loads[m].shape
+        load(m).wait()
+        return load_ref[m % 3, 0 : size[0], 0 : size[1]]
+
+    def dx_copy():
+        return pltpu.make_async_copy(g_one_hbm, dx_ref, side_sem.at[0])
+
+    def xt_copy():
+        return pltpu.make_async_copy(xt_hbm, xt_ref, side_sem.at[1])
+
     @pl.when(pair == 0)
     def _():
+        for m in range(2):
+            load(m).start()
+        layout.mesh.greet()
+        m = 0
+        for n in range(layout.fold):
+            load(m + 2).start()
+            layout.store_down(n, dot(loaded(m), branch_ref[...], TN).astype(BF))
+            m += 1
+        layout.down.core()
+        for n in range(3):
+            if m + 2 < len(loads):
+                load(m + 2).start()
+            layout.store_into(n, dot(hidden_ref[...], loaded(m), TN).astype(BF))
+            if n == 0:
+                layout.rest.core()
+            m += 1
+        xt_copy().start()
+        dx_copy().start()
+        layout.into.core()
         run(steps[0])()
+        layout.store_out(dot(loaded(m), loaded(m + 1), TN).astype(BF))
         bwd_masks(tq, mask_ref)
-        for n in range(ext // 128):
-            xt_ref[:, n * 128 : (n + 1) * 128] = x_ref[n * 128 : (n + 1) * 128, :].astype(F32).T.astype(BF)
-        for n in range(table // 128):
-            xt_ref[:, ext + n * 128 : ext + (n + 1) * 128] = rel_ref[n * 128 : (n + 1) * 128, :].astype(F32).T.astype(BF)
         d_ref[...] = jnp.zeros_like(d_ref)
         rel_acc[...] = jnp.zeros_like(rel_acc)
         dx_acc[...] = jnp.zeros_like(dx_acc)
-        vec_ref[...] = small_ref[...].astype(F32)
+        vec_ref[...] = jnp.zeros_like(vec_ref)
+        for n, ref in enumerate(small_refs[:6]):
+            vec_ref[n : n + 1, :] = ref[...][None]
+        for n in range(layout.fold):
+            vec_ref[6 + n : 7 + n, :] = small_refs[6][n * layout.width : (n + 1) * layout.width][None]
 
     for kt in range(nk):
         kjt_ref[kt] = dot(k_ref[kt * tq : (kt + 1) * tq, :], flip, TN).astype(BF)
@@ -649,8 +830,8 @@
 
     def tile(qt, carry):
         for step, actions in steps.items():
-            if step:
-                pl.when(pair * nq + qt == step * pairs * nq // 12)(run(actions))
+            if step and step % 3 < min(nq, 2):
+                pl.when((pair == step // 3) & (qt == step % 3))(run(actions))
         row = pl.multiple_of(qt * tq, tq)
         dq = bwd_tile(
             tq, scale, qt, q_ref, k_ref, v_ref, g_ref, rk_ref, rq_ref, p_ref, mask_ref, kjt_ref, dk_acc, dvt_acc, drkt_acc, drqt_acc
@@ -659,6 +840,9 @@
         return carry
 
     lax.fori_loop(0, nq, tile, 0)
+    for step, actions in steps.items():
+        if step % 3 >= min(nq, 2):
+            pl.when(pair == step // 3)(run(actions))
     for kt in range(nk):
         here = slice(kt * tq, (kt + 1) * tq)
         dk = dot(flip, dk_acc[kt].astype(BF)).astype(BF)
@@ -670,6 +854,7 @@
         d_ref[here, 0:128] = drqt_acc[:, st * 128 : (st + 1) * 128].T.astype(BF)
         d_ref[here, 128:256] = drkt_acc[:, st * 128 : (st + 1) * 128].T.astype(BF)
 
+    pl.when(pair == 0)(lambda: xt_copy().wait())
     grads = dot(xt_ref[...], d_ref[...]).astype(BF)
     layout.store_pair(pair, grads)
     weights = jnp.concatenate([wq_ref[...], wk_ref[...], wv_ref[...]], axis=1)
@@ -686,43 +871,47 @@
         sent_ref[0] = dx_acc[0:span].astype(BF)
         sent_ref[1] = dx_acc[ext - span :].astype(BF)
         run(last[:1])()
-        dx_ref[...] = g_one_ref[...] + dx_acc[span : span + block]
+        dx_copy().wait()
+        dx_ref[...] += dx_acc[span : span + block]
         run(last[1:])()
+
+        packed_copies = []
+        for n, (at, chunk) in enumerate(zip(layout.starts(), layout.chunks)):
+            packed_copies.append(pltpu.make_async_copy(chunk.final, packed_hbm.at[:, pl.ds(at, chunk.lanes)], packed_sem.at[n]))
+            packed_copies[-1].start()
 
         def take(side, rows):
             here = slice(0, span) if side == 0 else slice(block - span, block)
             dx_ref[here] += rows.astype(F32)
 
         edges.finish(take)
-        outs = (down_out, in_out, near0_out, near1_out, near2_out, far_out)
-        for out, chunk in zip(outs, layout.chunks):
-            out[...] = chunk.final[...]
-
-
-def attn_bwd(span, q, k, v, g, rk, rq, probs, w_key, w_query, w_value, grad_one, x_ext, rel_flip, picks, small, down_grad, in_grad, out_grad):
+        for copy in packed_copies:
+            copy.wait()
+
+
+def attn_bwd(span, q, k, v, g, rk, rq, probs, w_key, w_query, w_value, act, branch, hidden, pre, context, g_attn, g_one, xt, picks, small):
     block, width = q.shape
     ext = k.shape[0]
     table = 2 * span
     scale = (3.0 * 64) ** -0.5
     ns, nb = lax.axis_size("seq"), lax.axis_size("batch")
-    layout = Layout(ns, nb, width, in_grad.shape[1], table)
+    layout = Layout(ns, nb, width, act.shape[1], table)
     col = lambda rows: pl.BlockSpec((rows, 128), lambda h: (0, h))
     whole = lambda shape: pl.BlockSpec(shape, lambda h: (0, 0), pipeline_mode=pl.Buffered(1))
-    any_spec = pl.BlockSpec(memory_space=pl.ANY)
-    by_share = lambda grad: grad.reshape(nb // 2, 2, grad.shape[0] // nb, grad.shape[1])
-    packed = [jax.ShapeDtypeStruct((layout.rows, chunk.lanes), BF) for chunk in layout.chunks]
+    any_spec = pl.BlockSpec(memory_space=pltpu.HBM)
+    packed = jax.ShapeDtypeStruct((layout.rows, sum(chunk.lanes for chunk in layout.chunks)), BF)
     outs = pl.pallas_call(
         functools.partial(bwd_kernel, span, scale, layout),
         grid=(width // 128,),
         out_shape=(
             jax.ShapeDtypeStruct((block, width), F32),
-            *packed,
+            packed,
         ),
         in_specs=[col(block), col(ext), col(ext), col(block), col(rk.shape[0]), col(rq.shape[0]),
                   pl.BlockSpec((2, block, table), lambda h: (h, 0, 0)), col(width), col(width), col(width),
-                  whole(grad_one.shape), whole(x_ext.shape), whole(rel_flip.shape), whole(picks.shape), whole(small.shape),
-                  any_spec, any_spec, any_spec],
-        out_specs=(whole((block, width)),) + tuple(whole(part.shape) for part in packed),
+                  any_spec, whole(branch.shape), whole(hidden.shape), any_spec, any_spec, any_spec, any_spec, any_spec,
+                  whole(picks.shape)] + [pl.BlockSpec(part.shape, lambda h: (0,)) for part in small],
+        out_specs=(whole((block, width)), any_spec),
         scratch_shapes=[
             pltpu.VMEM((4, span, span), BF),
             pltpu.VMEM((ext // span, 128, span), BF),
@@ -738,13 +927,66 @@
             pltpu.VMEM((2, span, width), BF),
             pltpu.VMEM((2, span, width), BF),
             pltpu.SemaphoreType.DMA((2, 2)),
+            pltpu.VMEM((3, block, layout.split), BF),
+            pltpu.SemaphoreType.DMA((3,)),
+            pltpu.SemaphoreType.DMA((2,)),
+            pltpu.SemaphoreType.DMA((len(layout.chunks),)),
         ] + layout.scratch(),
         compiler_params=pltpu.CompilerParams(collective_id=0, has_side_effects=True, vmem_limit_bytes=60 << 20),
         cost_estimate=pl.CostEstimate(flops=50_000_000_000, bytes_accessed=20 << 20, transcendentals=0),
         name="attn_bwd_reduce",
-    )(q, k, v, g, rk, rq, probs, w_key, w_query, w_value, grad_one, x_ext, rel_flip, picks, small,
-      by_share(down_grad), by_share(in_grad), by_share(out_grad))
+    )(*[pltpu.with_memory_space_constraint(arg, pltpu.HBM) for arg in (q, k, v)], g, *[pltpu.with_memory_space_constraint(arg, pltpu.HBM) for arg in (rk, rq, probs)], w_key, w_query, w_value, act, branch, hidden, pre, context, g_attn, g_one, pltpu.with_memory_space_constraint(xt, pltpu.HBM), picks, *small)
     return layout, outs
+
+
+def unpack_kernel(layout, packed_ref,
+                  down_out, into_out, out_out, query_out, key_out, value_out, rel_out, *refs):
+    vec_outs, wide_out, (rel_ref, vec_ref) = refs[:-3], refs[-3], refs[-2:]
+    rows, width, pairs = layout.rows, layout.width, layout.pairs
+    parts = [packed_ref.at[:, at : at + chunk.lanes] for at, chunk in zip(layout.starts(), layout.chunks)]
+    down_ref, into_ref, rest_ref, *near, far_ref = parts
+    split = layout.hidden // 3
+    into_out[:, :split] = rest_ref[:, :split].astype(F32)
+    into_out[:, split:] = into_ref[:, : layout.hidden - split].astype(F32)
+    for n in range(layout.fold):
+        down_out[n * rows : (n + 1) * rows, :] = down_ref[:, n * width : (n + 1) * width].astype(F32)
+    for n, side in enumerate(near):
+        out_out[:, n * layout.third : (n + 1) * layout.third] = side[:, 768 : 768 + layout.third].astype(F32)
+    for m in range(pairs):
+        side, at = (far_ref, 0) if m == pairs - 1 else (near[m // 2], m % 2 * 384)
+        for n, out in enumerate((query_out, key_out, value_out)):
+            out[:, m * 128 : (m + 1) * 128] = side[:, at + n * 128 : at + (n + 1) * 128].astype(F32)
+    take, at, half = layout.rel_rows, layout.rel_at, layout.rel_rows // 2
+    rel_ref[:, 0:512] = far_ref[0:take, at : at + 512].astype(F32)
+    for n in range(2):
+        rel_ref[n * half : (n + 1) * half, 512:768] = far_ref[take : take + half, at + n * 256 : at + (n + 1) * 256].astype(F32)
+    own = take // layout.mesh.ns
+    rel_out[...] = pltpu.roll(rel_ref[...], take - lax.axis_index("seq") * own, 0)[:own]
+    for n in range(pairs):
+        row, lane = (n % layout.stack) * 16, layout.small_at + (n // layout.stack) * 128
+        vec_ref[:, n * 128 : (n + 1) * 128] = far_ref[row : row + 16, lane : lane + 128].astype(F32)
+    b = lax.axis_index("batch")
+    mine = pltpu.roll(vec_ref[...], width - b * rows, 1)
+    for out, n in zip(vec_outs, (0, 1, 2, 3, 4, 5, 10, 11, 12)):
+        out[...] = mine[n, :rows]
+    wide = wide_out.shape[0]
+    fit = width // wide
+    line = pltpu.roll(pltpu.roll(vec_ref[...], width - (b % fit) * wide, 1), 10 - b // fit, 0)
+    wide_out[...] = line[0, :wide]
+
+
+def unpack(layout, packed):
+    rows, width = layout.rows, layout.width
+    shape = lambda *dims: jax.ShapeDtypeStruct(dims, F32)
+    shapes = [shape(layout.fold * rows, width), shape(rows, layout.hidden)] + [shape(rows, width)] * 4
+    shapes += [shape(layout.rel_rows // layout.mesh.ns, width)] + [shape(rows)] * 9 + [shape(layout.fold * rows)]
+    return pl.pallas_call(
+        functools.partial(unpack_kernel, layout),
+        out_shape=shapes,
+        scratch_shapes=[pltpu.VMEM((layout.rel_rows, width), F32), pltpu.VMEM((16, width), F32)],
+        compiler_params=pltpu.CompilerParams(vmem_limit_bytes=32 << 20),
+        name="unpack",
+    )(packed)
 
 
 NORM_EPS = 1e-07
@@ -787,27 +1029,13 @@
     rows, block, width = layer_input.shape
     span = rel_table.shape[0] // 2
     x = layer_input[0]
-    count = lax.axis_size("seq")
-    up = [(i, i + 1) for i in range(count - 1)]
-    down = [(i + 1, i) for i in range(count - 1)]
-    before = lax.ppermute(x[block - span :], "seq", up)
-    after = lax.ppermute(x[:span], "seq", down)
-    rel_flip = dot(anti(2 * span), rel_table).astype(BF)
-
-    def project(rows_in, weight, bias):
-        return (dot(rows_in, weight) + bias).astype(BF)
-
-    q = project(x, w_query, b_query)
-    rk = project(rel_flip, w_key, b_key)
-    rq = project(rel_flip, w_query, b_query)
-    x_ext = jnp.concatenate([before, x, after], axis=0)
-    k = project(x_ext, w_key, b_key)
-    v = project(x_ext, w_value, b_value)
     start = lax.axis_index("seq") * block
     padded = jnp.pad(segment_ids[0], (span, span), constant_values=-1)
     kid = lax.dynamic_slice_in_dim(padded, start, block + 2 * span, 0)
     qid = kid[span : span + block]
-    context, probs = attn_fwd(span, q, k, v, rk, rq, qid[:, None], kid[None])
+    context, probs, q, k, v, rk, rq, xt = attn_fwd(
+        span, x, rel_table, w_query, w_key, w_value, b_query, b_key, b_value, qid[:, None], kid[None]
+    )
 
     residual_one = x.astype(F32) + dot(context, w_out) + b_out
     normed_one, inv_one = norm_rows(residual_one)
@@ -826,46 +1054,29 @@
     shift_ffn_grad = jnp.sum(grad_out, axis=0)
     grad_two = norm_back(grad_out * gain_ffn, normed_two, inv_two)
     grad_branch = grad_two.astype(BF)
-    down_grad = dot(act_low, grad_branch, TN)
     down_bias_grad = jnp.sum(grad_branch.astype(F32), axis=0)
     grad_pre = (dot(grad_branch, w_down, NT) * slope).astype(BF)
-    in_grad = dot(hidden_low, grad_pre, TN)
     in_bias_grad = jnp.sum(grad_pre.astype(F32), axis=0)
     grad_hidden = grad_two + dot(grad_pre, w_in, NT)
     gain_attn_grad = jnp.sum(grad_hidden * normed_one, axis=0)
     shift_attn_grad = jnp.sum(grad_hidden, axis=0)
     grad_one = norm_back(grad_hidden * gain_attn, normed_one, inv_one)
     grad_attn = grad_one.astype(BF)
-    out_grad = dot(context, grad_attn, TN)
     out_bias_grad = jnp.sum(grad_attn.astype(F32), axis=0)
     grad_context = dot(grad_attn, w_out, NT).astype(BF)
 
     share, lanes = lax.axis_size("batch"), lax.axis_size("seq")
     rel_rows = 2 * span // (share * lanes)
-    order = jnp.arange(2 * span).reshape(lanes, share, rel_rows).transpose(1, 0, 2).reshape(-1)
-    picks = ((2 * span - 1 - order)[:, None] == jnp.arange(2 * span)[None]).astype(BF)
+    order = np.arange(2 * span).reshape(lanes, share, rel_rows).transpose(1, 0, 2).reshape(-1)
+    picks = jnp.asarray((2 * span - 1 - order)[:, None] == np.arange(2 * span)[None], BF)
     small = [out_bias_grad, gain_attn_grad, shift_attn_grad, down_bias_grad, gain_ffn_grad, shift_ffn_grad, in_bias_grad]
-    small = jnp.concatenate([vec.reshape(-1, width) for vec in small], axis=0)
-    small = jnp.pad(small, ((0, 16 - small.shape[0]), (0, 0))).astype(BF)
     layout, outs = attn_bwd(
-        span, q, k, v, grad_context, rk, rq, probs, w_key, w_query, w_value, grad_one, x_ext, rel_flip, picks, small,
-        down_grad.astype(BF), in_grad.astype(BF), out_grad.astype(BF),
+        span, q, k, v, grad_context, rk, rq, probs, w_key, w_query, w_value, act_low, grad_branch, hidden_low, grad_pre,
+        context, grad_attn, grad_one, xt, picks, small,
     )
-    input_grad, down_sum, in_sum, *near, far = outs
-    fold = layout.fold
-    down_sum = jnp.concatenate([down_sum[:, n * width : (n + 1) * width] for n in range(fold)], axis=0).astype(F32)
-    in_sum = in_sum[:, : layout.hidden].astype(F32)
-    out_sum = jnp.concatenate([side[:, 768 : 768 + layout.third] for side in near], axis=1).astype(F32)
-    query_sum, key_sum, value_sum = [layout.pairs_of(near, far, n).astype(F32) for n in range(3)]
-    rel_sum = layout.rel_of(far)
-    rel_sum = lax.dynamic_slice_in_dim(rel_sum, lax.axis_index("seq") * rel_rows, rel_rows, 0).astype(F32)
-    vectors = layout.vectors_of(far).astype(F32)
-    mine = lax.axis_index("batch") * layout.rows
-    cut = lambda n: lax.dynamic_slice_in_dim(vectors[n], mine, layout.rows, 0)
-    ob, ga, sa, db, gf, sf = [cut(n) for n in range(6)]
-    wide = layout.hidden // share
-    ib = lax.dynamic_slice_in_dim(vectors[6:10].reshape(-1), lax.axis_index("batch") * wide, wide, 0)
-    qb, kb, vb = [cut(n) for n in range(10, 13)]
+    input_grad, packed = outs
+    down_sum, in_sum, out_sum, query_sum, key_sum, value_sum, rel_sum, *vectors = unpack(layout, packed)
+    ob, ga, sa, db, gf, sf, qb, kb, vb, ib = vectors
     return (
         output[None], input_grad[None], query_sum, qb, key_sum, kb, value_sum, vb, out_sum, ob,
         ga, sa, in_sum, ib, down_sum, db, gf, sf, rel_sum,

time: 251 us -> 216 us (0.86)
  matrix products: 38.7 us -> 18.4 us
  Pallas kernels: 157 us -> 176 us
  local copies, waits for them, and re-layouts: 22.8 us -> 10.9 us
  waiting for transfers between devices: 9.35 us -> 0 us
  other arithmetic: 13.7 us -> 7.4 us
  starting transfers between devices: 4.83 us -> 0 us
    dot_general x15 -> x6, matrix products: 38.7 us -> 18.4 us  [dot(): return lax.dot_general(a, b, dims, preferred_element_type=F32)]
    pallas_call x1, Pallas kernels: 127 us -> 137 us  [attn_bwd(): pl.pallas_call(functools.partial(bwd_kernel, span, scale, layout), grid=(...]
    ppermute x2 -> x0, waiting for transfers between devices: 9.35 us -> none  [the longest x1 9.34 us: local(): after = lax.ppermute(x[:span], 'seq', down)]
    pallas_call x1 -> x2, Pallas kernels: 30 us -> 38.8 us  [the longest x1 36.9 us: attn_fwd(): pl.pallas_call(functools.partial(fwd_kernel, span, scale), grid=(block //...]
    convert_element_type x11 -> x1, other arithmetic: 6.86 us -> 0.31 us  [local(): hidden_low = hidden.astype(BF)]
    slice x9 -> x0, local copies, waits for them, and re-layouts: 5.89 us -> none  [the longest x1 2.18 us: local(): before = lax.ppermute(x[block - span:], 'seq', up)]
    dynamic_slice x10 -> x0, local copies, waits for them, and re-layouts: 5.89 us -> none  [the longest x9 5.24 us: local(): cut = lambda n: lax.dynamic_slice_in_dim(vectors[n], mine, layout.rows, 0)]
    ppermute x2 -> x0, starting transfers between devices: 4.83 us -> none  [the longest x1 3.54 us: local(): before = lax.ppermute(x[block - span:], 'seq', up)]
  transfers between devices with their start and end apart: 2 -> 0, of which waited for: 1 -> 0; matrix products, arithmetic and copies ran while one was open for 3% -> 0% of each run, Pallas kernels for 0% -> 0%
where the time goes in v3:
time: 216 us; the launch traced here: 214 us
  Pallas kernels  176 us (81%)
  matrix products  18.4 us (9%)
  local copies, waits for them, and re-layouts  10.9 us (5%)
  other arithmetic  7.4 us (3%)
    pallas_call x1, Pallas kernels, attn_bwd(): pl.pallas_call(functools.partial(bwd_kernel, span, scale, layout), grid=(...  137 us
    pallas_call x1, Pallas kernels, attn_fwd(): pl.pallas_call(functools.partial(fwd_kernel, span, scale), grid=(block //...  36.9 us
    dot_general x6, matrix products, dot(): return lax.dot_general(a, b, dims, preferred_element_type=F32)  18.4 us
    unnamed x51, local copies, waits for them, and re-layouts  9.83 us

profile of v3, /device:TPU:8, one launch (start us, length us, event | category | flops | bytes accessed | tf_op | source)
XLA Modules:
  0.0 213.6 jit_solution(9496948854014182529)
XLA Ops:
  0.7 0.0 copy-start
  0.7 0.9 pad_dynamic-slice_fusion
  1.6 0.1 copy.40.qid_ref
  1.7 0.7 copy-done.2
  2.4 0.7 copy-done.3
  3.1 0.7 copy-done.4
  3.8 36.9 %attn_fwd.1 = (bf16[512,768]{1,0:T(8,128)(2,1)S(1)}, bf16[12,512,512]{2,1,0:T(8,128)(2,1)S(1)}, bf16[512,768]{1,0:T(8,128)(2,1)}, bf16[1024,768]{1,0:T(8,128)(2,...) custom-call(bf16[512,768]{1,0:T(8,128)(2,1)} %bitcast.51, ...), custom_call_target="tpu_custom_call" | custom-call | flops 20000000000 | bytes 20971520 | tf_op jit(solution)/shard_map/attn_fwd/pallas_call | solution.py:233
  40.7 2.7 %copy-done.6 = bf16[12,512,512]{2,1,0:T(8,128)(2,1)} copy-done((bf16[12,512,512]{2,1,0:T(8,128)(2,1)}, bf16[12,512,512]{2,1,0:T(8,128)(2,1)S(1)}, u32[]{:S(2)}) %copy-start.6) | copy-done | bytes 6291480
  43.4 0.9 fusion.19
  44.3 0.0 copy-done.5
  44.4 0.3 multiply_reduce_fusion.3
  44.7 1.1 copy-done.14
  45.8 0.0 copy-done.15
  45.8 0.3 fusion.15.hidden_ref
  46.2 0.0 slice-start.1
  46.2 3.8 %multiply_convert_fusion = (bf16[512,3072]{1,0:T(8,128)(2,1)S(1)}, f32[512,3072]{1,0:T(8,128)S(1)}) fusion(f32[3072]{0:T(1024)S(1)} %convert_element_type.67, bf16[512,768]{1,0:T(8,128)(2,1)S(1)} %fusion.15.hidden_ref, bf16[768,3072]{1,0:T(8,128)(2,1)S(1)} %copy-done.19), kind=kOutput, calls=%fused_computation.8 | convolution fusion | flops 2425356288 | bytes 14954496 | tf_op jit(solution)/shard_map/dot_general | solution.py:29
  50.1 2.8 %fusion.20 = (f32[512]{0:T(512)S(1)}, f32[512,768]{1,0:T(8,128)S(1)}) fusion(f32[768]{0:T(1024)S(1)} %convert_element_type.69, bf16[512,3072]{1,0:T(8,128)(2,1)S(1)} %get-tuple-element.88.act_hbm, bf16[3072,768]{1,0:T(8,128)(2,1)S(1)} %bitcast.50, f32[768]{0:T(1024)S(1)} %convert_element_type.65, f32[768]{0:T(1024)S(1)} %convert_element_type.64, ...), kind=kOutput, calls=%fused_computation.50 | convolution fusion | flops 2418671104 | bytes 11025408 | tf_op jit(solution)/shard_map/dot_general | solution.py:29
  52.9 0.3 multiply_reduce_fusion.2
  53.3 0.3 copy-done.17
  53.6 0.5 copy-done.7
  54.1 1.3 fusion.14
  55.4 2.1 %convert_reduce_fusion.2 = (f32[768]{0:T(1024)}, bf16[512,768]{1,0:T(8,128)(2,1)S(1)}, bf16[1,512,768]{2,1,0:T(8,128)(2,1)}) fusion(f32[512]{0:T(512)S(1)} %get-tuple-element.95, f32[512,768]{1,0:T(8,128)S(1)} %get-tuple-element.91, f32[512]{0:T(512)S(1)} %broadcast_multiply_fusion.4, f32[512]{0:T(512)S(1)} %get-tuple-element.96, ...), kind=kLoop, calls=%fused_computation.21 | loop fusion | flops 5504256 | bytes 3949568 | tf_op jit(solution)/shard_map/reduce_sum | solution.py:1057
  57.5 5.2 %convert_reduce_fusion = (f32[3072]{0:T(1024)}, bf16[512,3072]{1,0:T(8,128)(2,1)S(1)}) fusion(f32[512,3072]{1,0:T(8,128)S(1)} %get-tuple-element.89, f32[3072]{0:T(1024)S(1)} %convert_element_type.67, bf16[512,768]{1,0:T(8,128)(2,1)S(1)} %get-tuple-element.81.branch_ref, bf16[3072,768]{1,0:T(8,128)(2,1)S(1)} %bitcast.50), kind=kOutput, calls=%fused_computation.7 | convolution fusion | flops 2436363264 | bytes 14966784 | tf_op jit(solution)/shard_map/dot_general | solution.py:29
  62.8 3.9 %multiply_reduce_fusion = (f32[768]{0:T(1024)}, f32[512]{0:T(512)S(1)}, f32[512]{0:T(512)S(1)}, f32[768]{0:T(1024)}, f32[512,768]{1,0:T(8,128)S(1)}) fusion(f32[512,768]{1,0:T(8,128)S(1)} %get-tuple-element.87, f32[512]{0:T(512)S(1)} %add_rsqrt_fusion.1, f32[512]{0:T(512)S(1)} %broadcast_multiply_fusion.5, f32[768]{0:T(1024)S(1)} %convert_element_type.64, ...), kind=kOutput, calls=%fused_computation.22 | convolution fusion | flops 2422994432 | bytes 13398016 | tf_op jit(solution)/shard_map/dot_general | solution.py:29
  66.7 2.3 %convert_reduce_fusion.3 = (f32[768]{0:T(1024)}, bf16[512,768]{1,0:T(8,128)(2,1)S(1)}, f32[512,768]{1,0:T(8,128)}) fusion(f32[512]{0:T(512)S(1)} %broadcast_multiply_fusion, f32[512,768]{1,0:T(8,128)S(1)} %get-tuple-element.87, f32[512]{0:T(512)S(1)} %broadcast_multiply_fusion.5, f32[512]{0:T(512)S(1)} %broadcast_multiply_fusion.1, ...), kind=kLoop, calls=%fused_computation.23 | loop fusion | flops 3931392 | bytes 5519360 | tf_op jit(solution)/shard_map/reduce_sum | solution.py:1065
  68.9 1.7 convolution_convert_fusion.g_ref
  70.6 0.7 convert_reduce_fusion.1.rest_5_
  71.4 137.2 %attn_bwd_reduce.1 = (f32[512,768]{1,0:T(8,128)}, bf16[96,10240]{1,0:T(8,128)(2,1)}) custom-call(bf16[512,768]{1,0:T(8,128)(2,1)} %get-tuple-element.47.q_ref, bf16[1024,768]{1,0:T(8,128)(2,1)} %get-tuple-element.48.k_ref, bf16[1024,768]{1,0:T(8,128)(2,1)} %get-tuple-element.49.v_ref, bf16[512,768]{1,0:T(8,128)(2,1)} %convolution_convert_fusion.g_ref, ...), custom_call_target="tpu_custom_call" | custom-call | flops 49999998976 | bytes 20971520 | tf_op jit(solution)/shard_map/attn_bwd_reduce/pallas_call | solution.py:903
  208.6 1.5 copy-done.1
  210.1 1.9 unpack.1
  212.0 0.4 copy-done.8
  212.5 1.1 copy.42
  (53 shorter events, 0.1 us)
Async XLA Ops:
  0.7 42.7 %copy-start = (bf16[768,768]{1,0:T(8,128)(2,1)S(1)}, bf16[768,768]{1,0:T(8,128)(2,1)}, u32[]{:S(2)}) copy-start(bf16[768,768]{1,0:T(8,128)(2,1)} %param.28) | copy-start | bytes 3538948
  1.7 0.7 copy-start.2
  2.4 0.7 copy-start.3
  3.1 0.7 copy-start.4
  3.8 39.6 %copy-start.13 = (bf16[768]{0:T(1024)(128)(2,1)S(1)}, bf16[768]{0:T(1024)(128)(2,1)}, u32[]{:S(2)}) copy-start(bf16[768]{0:T(1024)(128)(2,1)} %param.29) | copy-start | bytes 4612
  3.8 39.6 %copy-start.20 = (bf16[1,512,768]{2,1,0:T(8,128)(2,1)S(1)}, bf16[1,512,768]{2,1,0:T(8,128)(2,1)}, u32[]{:S(2)}) copy-start(bf16[1,512,768]{2,1,0:T(8,128)(2,1)} %param.21) | copy-start | bytes 2359300
  40.7 2.7 %copy-start.6 = (bf16[12,512,512]{2,1,0:T(8,128)(2,1)}, bf16[12,512,512]{2,1,0:T(8,128)(2,1)S(1)}, u32[]{:S(2)}) copy-start(bf16[12,512,512]{2,1,0:T(8,128)(2,1)S(1)} %get-tuple-element.52.p_ref) | copy-start | bytes 18874372
  43.4 1.0 copy-start.5
  43.4 2.7 %copy-start.19 = (bf16[768,3072]{1,0:T(8,128)(2,1)S(1)}, bf16[768,3072]{1,0:T(8,128)(2,1)}, u32[]{:S(2)}) copy-start(bf16[768,3072]{1,0:T(8,128)(2,1)} %param.32) | copy-start | bytes 14155780
  44.3 1.4 copy-start.14
  44.3 1.4 copy-start.15
  44.7 1.5 copy-start.12
  45.8 4.3 %slice-start = ((s8[4718592]{0:T(1024)(128)(4,1)}), s8[4194304]{0:T(1024)(128)(4,1)S(1)}, s32[]{:S(2)}) async-start(s8[4718592]{0:T(1024)(128)(4,1)} %bitcast.49), calls=%async_computation | async-start | bytes 8388608
  46.1 3.9 %copy-start.9 = (bf16[512,768]{1,0:T(8,128)(2,1)}, bf16[512,768]{1,0:T(8,128)(2,1)S(1)}, u32[]{:S(2)}) copy-start(bf16[512,768]{1,0:T(8,128)(2,1)S(1)} %fusion.15.hidden_ref) | copy-start | bytes 2359300
  46.2 3.9 %copy-start.16 = (bf16[768]{0:T(1024)(128)(2,1)S(1)}, bf16[768]{0:T(1024)(128)(2,1)}, u32[]{:S(2)}) copy-start(bf16[768]{0:T(1024)(128)(2,1)} %param.35) | copy-start | bytes 4612
  46.2 3.9 %slice-start.1 = ((s8[4718592]{0:T(1024)(128)(4,1)}), s8[524288]{0:T(1024)(128)(4,1)S(1)}, s32[]{:S(2)}) async-start(s8[4718592]{0:T(1024)(128)(4,1)} %bitcast.49), calls=%async_computation.1 | async-start | bytes 1048576
  50.0 2.9 %copy-start.21 = (bf16[512,3072]{1,0:T(8,128)(2,1)}, bf16[512,3072]{1,0:T(8,128)(2,1)S(1)}, u32[]{:S(2)}) copy-start(bf16[512,3072]{1,0:T(8,128)(2,1)S(1)} %get-tuple-element.88.act_hbm) | copy-start | bytes 9437188
  52.9 0.7 copy-start.17
  52.9 1.1 copy-start.7
  53.2 2.1 copy-start.18
  57.5 5.2 %copy-start.10 = (bf16[512,768]{1,0:T(8,128)(2,1)}, bf16[512,768]{1,0:T(8,128)(2,1)S(1)}, u32[]{:S(2)}) copy-start(bf16[512,768]{1,0:T(8,128)(2,1)S(1)} %get-tuple-element.81.branch_ref) | copy-start | bytes 2359300
  62.8 3.9 %copy-start.22 = (bf16[512,3072]{1,0:T(8,128)(2,1)}, bf16[512,3072]{1,0:T(8,128)(2,1)S(1)}, u32[]{:S(2)}) copy-start(bf16[512,3072]{1,0:T(8,128)(2,1)S(1)} %get-tuple-element.94.pre_hbm) | copy-start | bytes 9437188
  68.9 1.7 copy-start.11
  208.6 1.5 copy-start.1
  210.1 2.3 %copy-start.8 = (f32[512,768]{1,0:T(8,128)S(1)}, f32[512,768]{1,0:T(8,128)}, u32[]{:S(2)}) copy-start(f32[512,768]{1,0:T(8,128)} %get-tuple-element.54) | copy-start | bytes 4718596

commit v4 on v3

--- a/solution.py
+++ b/solution.py
@@ -583,17 +583,17 @@
         self.stack = rows // 16
         small_lanes = -(-self.pairs // self.stack) * 128
         self.split = split = hidden // 3
-        whole = lambda name, lanes: self.boxed(lambda c: getattr(self, name).at[:, c], lanes)
+        whole = lambda name, lanes, early=False: self.boxed(lambda c: getattr(self, name).at[:, c], lanes, early)
         self.down = whole("down_ref", self.fold * width)
         self.into = whole("into_ref", hidden - split)
-        self.rest = whole("rest_ref", split)
+        self.rest = whole("rest_ref", split, False)
         lanes = Chunk(mesh, rows, 768 + self.third, []).lanes
-        self.near = [self.boxed(lambda c, n=n: self.near_ref.at[n, :, c], lanes) for n in range(3)]
+        self.near = [self.boxed(lambda c, n=n: self.near_ref.at[n, :, c], lanes, n in (2,)) for n in range(3)]
         self.far = whole("far_ref", self.small_at + small_lanes)
         self.chunks = [self.down, self.into, self.rest, *self.near, self.far]
 
-    def boxed(self, box, lanes):
-        chunk = Chunk(self.mesh, self.rows, lanes, [])
+    def boxed(self, box, lanes, early=False):
+        chunk = Chunk(self.mesh, self.rows, lanes, [], early_z=early)
         chunk.box, chunk.moves = box, [(box, 0, chunk.lanes)]
         return chunk
 
@@ -667,43 +667,42 @@
                 row, lane = (n % self.stack) * 16, self.small_at + (n // self.stack) * 128
                 put[row : row + 16, lane : lane + 128] = vectors[:, n * 128 : (n + 1) * 128]
 
-    def schedule(self, edges):
+    def schedule(self):
         down, into, rest, one, two, three, far = self.chunks
 
         steps = {
-            0: [],
-            1: [down.s0],
-            3: [into.s0, rest.s0],
-            6: [down.s1, one.core],
-            7: [one.s0],
-            9: [into.s1, rest.s1],
-            10: [down.z],
-            12: [one.s1, two.core],
-            13: [into.z, rest.z, two.s0],
-            15: [down.out, three.core, one.z],
-            16: [three.s0, two.s1],
+            1: [rest.s0],
+            2: [into.s0],
+            3: [down.s0],
+            7: [one.core],
+            8: [into.s1],
+            9: [down.s1, rest.s1],
+            11: [into.z],
+            12: [one.s0, two.core],
+            13: [rest.z, two.s0],
+            14: [down.z, into.out, one.s1],
+            15: [two.s1],
+            16: [into.out2, rest.out, three.core, one.z],
+            17: [two.z],
         }
         last = [
             far.core,
+            three.z,
+            far.s0,
+            down.out,
+            two.out,
+            far.s1,
+            one.out,
+            three.s0,
             down.out2,
-            into.out,
-            rest.out,
-            one.out,
-            two.z,
+            far.z,
             three.s1,
-            far.s0,
-            edges.start,
-            into.out2,
+            two.out2,
+            one.out2,
+            three.out,
+            far.out,
             rest.out2,
-            one.out2,
-            two.out,
-            three.z,
-            far.s1,
-            two.out2,
-            three.out,
-            far.z,
             three.out2,
-            far.out,
             far.out2,
         ]
         last += [chunk.finish for chunk in self.chunks]
@@ -761,7 +760,7 @@
     flip = anti(tq)
     layout.bind(refs)
     edges = Edges(layout.mesh, (sent_ref, got_ref, edge_sem))
-    steps, last = layout.schedule(edges)
+    steps, last = layout.schedule()
 
     def run(actions):
         def all_of():
@@ -809,7 +808,7 @@
         xt_copy().start()
         dx_copy().start()
         layout.into.core()
-        run(steps[0])()
+        run(steps.get(0, []))()
         layout.store_out(dot(loaded(m), loaded(m + 1), TN).astype(BF))
         bwd_masks(tq, mask_ref)
         d_ref[...] = jnp.zeros_like(d_ref)
@@ -854,11 +853,18 @@
         d_ref[here, 0:128] = drqt_acc[:, st * 128 : (st + 1) * 128].T.astype(BF)
         d_ref[here, 128:256] = drkt_acc[:, st * 128 : (st + 1) * 128].T.astype(BF)
 
+    weights = jnp.concatenate([wq_ref[...], wk_ref[...], wv_ref[...]], axis=1)
+    dx_acc[...] += dot(d_ref[0:ext], weights, NT)
+
+    @pl.when(pair == pairs - 1)
+    def _():
+        sent_ref[0] = dx_acc[0:span].astype(BF)
+        sent_ref[1] = dx_acc[ext - span :].astype(BF)
+        edges.start()
+
     pl.when(pair == 0)(lambda: xt_copy().wait())
     grads = dot(xt_ref[...], d_ref[...]).astype(BF)
     layout.store_pair(pair, grads)
-    weights = jnp.concatenate([wq_ref[...], wk_ref[...], wv_ref[...]], axis=1)
-    dx_acc[...] += dot(d_ref[0:ext], weights, NT)
     rel_acc[...] += dot(d_ref[ext:, 0:128], wq_ref[...], NT) + dot(d_ref[ext:, 128:256], wk_ref[...], NT)
     sums = dot(jnp.ones((8, ext + table), BF), d_ref[...])[0:1]
     for n in range(3):
@@ -868,8 +874,6 @@
     def _():
         rel = dot(picks_ref[...], rel_acc[...].astype(BF)).astype(BF)
         layout.store_rest(rel, vec_ref[...].astype(BF))
-        sent_ref[0] = dx_acc[0:span].astype(BF)
-        sent_ref[1] = dx_acc[ext - span :].astype(BF)
         run(last[:1])()
         dx_copy().wait()
         dx_ref[...] += dx_acc[span : span + block]
@@ -939,9 +943,14 @@
     return layout, outs
 
 
-def unpack_kernel(layout, packed_ref,
-                  down_out, into_out, out_out, query_out, key_out, value_out, rel_out, *refs):
-    vec_outs, wide_out, (rel_ref, vec_ref) = refs[:-3], refs[-3], refs[-2:]
+def unpack_kernel(layout, packed_hbm, dx_hbm,
+                  dx_out, down_out, into_out, out_out, query_out, key_out, value_out, rel_out, *refs):
+    vec_outs, wide_out, (packed_ref, rel_ref, vec_ref, sems) = refs[:-5], refs[-5], refs[-4:]
+    packed_copy = pltpu.make_async_copy(packed_hbm, packed_ref, sems.at[0])
+    dx_copy = pltpu.make_async_copy(dx_hbm, dx_out, sems.at[1])
+    packed_copy.start()
+    dx_copy.start()
+    packed_copy.wait()
     rows, width, pairs = layout.rows, layout.width, layout.pairs
     parts = [packed_ref.at[:, at : at + chunk.lanes] for at, chunk in zip(layout.starts(), layout.chunks)]
     down_ref, into_ref, rest_ref, *near, far_ref = parts
@@ -973,20 +982,29 @@
     fit = width // wide
     line = pltpu.roll(pltpu.roll(vec_ref[...], width - (b % fit) * wide, 1), 10 - b // fit, 0)
     wide_out[...] = line[0, :wide]
-
-
-def unpack(layout, packed):
+    dx_copy.wait()
+
+
+def unpack(layout, packed, dx):
     rows, width = layout.rows, layout.width
     shape = lambda *dims: jax.ShapeDtypeStruct(dims, F32)
-    shapes = [shape(layout.fold * rows, width), shape(rows, layout.hidden)] + [shape(rows, width)] * 4
+    shapes = [shape(*dx.shape), shape(layout.fold * rows, width), shape(rows, layout.hidden)] + [shape(rows, width)] * 4
     shapes += [shape(layout.rel_rows // layout.mesh.ns, width)] + [shape(rows)] * 9 + [shape(layout.fold * rows)]
+    vmem, far = pl.BlockSpec(memory_space=pltpu.VMEM), pl.BlockSpec(memory_space=pltpu.HBM)
     return pl.pallas_call(
         functools.partial(unpack_kernel, layout),
         out_shape=shapes,
-        scratch_shapes=[pltpu.VMEM((layout.rel_rows, width), F32), pltpu.VMEM((16, width), F32)],
+        in_specs=[far, far],
+        out_specs=[vmem] * len(shapes),
+        scratch_shapes=[
+            pltpu.VMEM(packed.shape, BF),
+            pltpu.VMEM((layout.rel_rows, width), F32),
+            pltpu.VMEM((16, width), F32),
+            pltpu.SemaphoreType.DMA((2,)),
+        ],
         compiler_params=pltpu.CompilerParams(vmem_limit_bytes=32 << 20),
         name="unpack",
-    )(packed)
+    )(*[pltpu.with_memory_space_constraint(arg, pltpu.HBM) for arg in (packed, dx)])
 
 
 NORM_EPS = 1e-07
@@ -1075,7 +1093,7 @@
         context, grad_attn, grad_one, xt, picks, small,
     )
     input_grad, packed = outs
-    down_sum, in_sum, out_sum, query_sum, key_sum, value_sum, rel_sum, *vectors = unpack(layout, packed)
+    input_grad, down_sum, in_sum, out_sum, query_sum, key_sum, value_sum, rel_sum, *vectors = unpack(layout, packed, input_grad)
     ob, ga, sa, db, gf, sf, qb, kb, vb, ib = vectors
     return (
         output[None], input_grad[None], query_sum, qb, key_sum, kb, value_sum, vb, out_sum, ob,

time: 216 us -> 202 us (0.935); the launches traced: 214 us -> 202 us
  Pallas kernels: 176 us -> 167 us
  local copies, waits for them, and re-layouts: 10.9 us -> 7.75 us
    pallas_call x1, Pallas kernels: 137 us -> 126 us  [attn_bwd(): pl.pallas_call(functools.partial(bwd_kernel, span, scale, layout), grid=(...]
    unnamed x51 -> x46, local copies, waits for them, and re-layouts: 9.83 us -> 6.72 us
    pallas_call x1, Pallas kernels: 1.9 us -> 4.37 us  [unpack(): pl.pallas_call(functools.partial(unpack_kernel, layout), out_shape=shapes...]
where the time goes in v4:
time: 202 us
  Pallas kernels  167 us (83%)
  matrix products  18.4 us (9%)
  local copies, waits for them, and re-layouts  7.75 us (4%)
  other arithmetic  7.4 us (4%)
    pallas_call x1, Pallas kernels, attn_bwd(): pl.pallas_call(functools.partial(bwd_kernel, span, scale, layout), grid=(...  126 us
    pallas_call x1, Pallas kernels, attn_fwd(): pl.pallas_call(functools.partial(fwd_kernel, span, scale), grid=(block //...  36.9 us
    dot_general x6, matrix products, dot(): return lax.dot_general(a, b, dims, preferred_element_type=F32)  18.4 us
    unnamed x46, local copies, waits for them, and re-layouts  6.72 us
    pallas_call x1, Pallas kernels, unpack(): pl.pallas_call(functools.partial(unpack_kernel, layout), out_shape=shapes...  4.37 us

profile of v4, /device:TPU:8, one launch (start us, length us, event | category | flops | bytes accessed | tf_op | source)
XLA Modules:
  0.0 201.8 jit_solution(2000292196401740796)
XLA Ops:
  0.7 0.0 copy-start
  0.7 0.9 pad_dynamic-slice_fusion
  1.6 0.1 copy.40.qid_ref
  1.7 0.0 copy-start.1
  1.7 0.7 copy-done.1
  2.4 0.7 copy-done.2
  3.1 0.7 copy-done.3
  3.8 36.9 %attn_fwd.1 = (bf16[512,768]{1,0:T(8,128)(2,1)S(1)}, bf16[12,512,512]{2,1,0:T(8,128)(2,1)S(1)}, bf16[512,768]{1,0:T(8,128)(2,1)}, bf16[1024,768]{1,0:T(8,128)(2,...) custom-call(bf16[512,768]{1,0:T(8,128)(2,1)} %bitcast.51, ...), custom_call_target="tpu_custom_call" | custom-call | flops 20000000000 | bytes 20971520 | tf_op jit(solution)/shard_map/attn_fwd/pallas_call | solution.py:233
  40.7 2.7 %copy-done.5 = bf16[12,512,512]{2,1,0:T(8,128)(2,1)} copy-done((bf16[12,512,512]{2,1,0:T(8,128)(2,1)}, bf16[12,512,512]{2,1,0:T(8,128)(2,1)S(1)}, u32[]{:S(2)}) %copy-start.5) | copy-done | bytes 6291480
  43.4 0.0 copy-start.17
  43.4 0.9 fusion.19
  44.3 0.0 copy-done.4
  44.4 0.3 multiply_reduce_fusion.3
  44.7 1.1 copy-done.12
  45.8 0.0 copy-done.13
  45.8 0.3 fusion.15.hidden_ref
  46.2 0.0 copy-start.14
  46.2 0.0 slice-start.1
  46.2 3.8 %multiply_convert_fusion = (bf16[512,3072]{1,0:T(8,128)(2,1)S(1)}, f32[512,3072]{1,0:T(8,128)S(1)}) fusion(f32[3072]{0:T(1024)S(1)} %convert_element_type.67, bf16[512,768]{1,0:T(8,128)(2,1)S(1)} %fusion.15.hidden_ref, bf16[768,3072]{1,0:T(8,128)(2,1)S(1)} %copy-done.17), kind=kOutput, calls=%fused_computation.8 | convolution fusion | flops 2425356288 | bytes 14954496 | tf_op jit(solution)/shard_map/dot_general | solution.py:29
  50.1 2.8 %fusion.20 = (f32[512]{0:T(512)S(1)}, f32[512,768]{1,0:T(8,128)S(1)}) fusion(f32[768]{0:T(1024)S(1)} %convert_element_type.69, bf16[512,3072]{1,0:T(8,128)(2,1)S(1)} %get-tuple-element.90.act_hbm, bf16[3072,768]{1,0:T(8,128)(2,1)S(1)} %bitcast.49, f32[768]{0:T(1024)S(1)} %convert_element_type.65, f32[768]{0:T(1024)S(1)} %convert_element_type.64, ...), kind=kOutput, calls=%fused_computation.50 | convolution fusion | flops 2418671104 | bytes 11025408 | tf_op jit(solution)/shard_map/dot_general | solution.py:29
  52.9 0.3 multiply_reduce_fusion.2
  53.3 0.3 copy-done.15
  53.6 0.5 copy-done.6
  54.1 1.3 fusion.14
  55.4 2.1 %convert_reduce_fusion.2 = (f32[768]{0:T(1024)}, bf16[512,768]{1,0:T(8,128)(2,1)S(1)}, bf16[1,512,768]{2,1,0:T(8,128)(2,1)}) fusion(f32[512]{0:T(512)S(1)} %get-tuple-element.97, f32[512,768]{1,0:T(8,128)S(1)} %get-tuple-element.93, f32[512]{0:T(512)S(1)} %broadcast_multiply_fusion.4, f32[512]{0:T(512)S(1)} %get-tuple-element.98, ...), kind=kLoop, calls=%fused_computation.21 | loop fusion | flops 5504256 | bytes 3949568 | tf_op jit(solution)/shard_map/reduce_sum | solution.py:1075
  57.5 5.2 %convert_reduce_fusion = (f32[3072]{0:T(1024)}, bf16[512,3072]{1,0:T(8,128)(2,1)S(1)}) fusion(f32[512,3072]{1,0:T(8,128)S(1)} %get-tuple-element.91, f32[3072]{0:T(1024)S(1)} %convert_element_type.67, bf16[512,768]{1,0:T(8,128)(2,1)S(1)} %get-tuple-element.83.branch_ref, bf16[3072,768]{1,0:T(8,128)(2,1)S(1)} %bitcast.49), kind=kOutput, calls=%fused_computation.7 | convolution fusion | flops 2436363264 | bytes 14966784 | tf_op jit(solution)/shard_map/dot_general | solution.py:29
  62.8 3.9 %multiply_reduce_fusion = (f32[768]{0:T(1024)}, f32[512]{0:T(512)S(1)}, f32[512]{0:T(512)S(1)}, f32[768]{0:T(1024)}, f32[512,768]{1,0:T(8,128)S(1)}) fusion(f32[512,768]{1,0:T(8,128)S(1)} %get-tuple-element.89, f32[512]{0:T(512)S(1)} %add_rsqrt_fusion.1, f32[512]{0:T(512)S(1)} %broadcast_multiply_fusion.5, f32[768]{0:T(1024)S(1)} %convert_element_type.64, ...), kind=kOutput, calls=%fused_computation.22 | convolution fusion | flops 2422994432 | bytes 13398016 | tf_op jit(solution)/shard_map/dot_general | solution.py:29
  66.7 2.3 %convert_reduce_fusion.3 = (f32[768]{0:T(1024)}, bf16[512,768]{1,0:T(8,128)(2,1)S(1)}, f32[512,768]{1,0:T(8,128)}) fusion(f32[512]{0:T(512)S(1)} %broadcast_multiply_fusion, f32[512,768]{1,0:T(8,128)S(1)} %get-tuple-element.89, f32[512]{0:T(512)S(1)} %broadcast_multiply_fusion.5, f32[512]{0:T(512)S(1)} %broadcast_multiply_fusion.1, ...), kind=kLoop, calls=%fused_computation.23 | loop fusion | flops 3931392 | bytes 5519360 | tf_op jit(solution)/shard_map/reduce_sum | solution.py:1083
  68.9 1.7 convolution_convert_fusion.g_ref
  70.6 0.7 convert_reduce_fusion.1.rest_5_
  71.4 125.9 %attn_bwd_reduce.1 = (f32[512,768]{1,0:T(8,128)}, bf16[96,10240]{1,0:T(8,128)(2,1)}) custom-call(bf16[512,768]{1,0:T(8,128)(2,1)} %get-tuple-element.48.q_ref, bf16[1024,768]{1,0:T(8,128)(2,1)} %get-tuple-element.49.k_ref, bf16[1024,768]{1,0:T(8,128)(2,1)} %get-tuple-element.50.v_ref, bf16[512,768]{1,0:T(8,128)(2,1)} %convolution_convert_fusion.g_ref, ...), custom_call_target="tpu_custom_call" | custom-call | flops 49999998976 | bytes 20971520 | tf_op jit(solution)/shard_map/attn_bwd_reduce/pallas_call | solution.py:907
  197.3 4.4 %unpack.1 = (f32[512,768]{1,0:T(8,128)}, f32[384,768]{1,0:T(8,128)}, f32[96,3072]{1,0:T(8,128)}, f32[96,768]{1,0:T(8,128)}, f32[96,768]{1,0:T(8,128)}, /*index=5...) custom-call(bf16[96,10240]{1,0:T(8,128)(2,1)} %get-tuple-element.55., ...), custom_call_target="tpu_custom_call" | custom-call | tf_op jit(solution)/shard_map/unpack/pallas_call | solution.py:994
  (48 shorter events, 0.1 us)
Async XLA Ops:
  0.7 42.7 %copy-start = (bf16[768,768]{1,0:T(8,128)(2,1)S(1)}, bf16[768,768]{1,0:T(8,128)(2,1)}, u32[]{:S(2)}) copy-start(bf16[768,768]{1,0:T(8,128)(2,1)} %param.28) | copy-start | bytes 3538948
  1.7 0.7 copy-start.1
  2.4 0.7 copy-start.2
  3.1 0.7 copy-start.3
  3.8 39.6 %copy-start.11 = (bf16[768]{0:T(1024)(128)(2,1)S(1)}, bf16[768]{0:T(1024)(128)(2,1)}, u32[]{:S(2)}) copy-start(bf16[768]{0:T(1024)(128)(2,1)} %param.29) | copy-start | bytes 4612
  3.8 39.6 %copy-start.18 = (bf16[1,512,768]{2,1,0:T(8,128)(2,1)S(1)}, bf16[1,512,768]{2,1,0:T(8,128)(2,1)}, u32[]{:S(2)}) copy-start(bf16[1,512,768]{2,1,0:T(8,128)(2,1)} %param.21) | copy-start | bytes 2359300
  40.7 2.7 %copy-start.5 = (bf16[12,512,512]{2,1,0:T(8,128)(2,1)}, bf16[12,512,512]{2,1,0:T(8,128)(2,1)S(1)}, u32[]{:S(2)}) copy-start(bf16[12,512,512]{2,1,0:T(8,128)(2,1)S(1)} %get-tuple-element.53.p_ref) | copy-start | bytes 18874372
  43.4 1.0 copy-start.4
  43.4 2.7 %copy-start.17 = (bf16[768,3072]{1,0:T(8,128)(2,1)S(1)}, bf16[768,3072]{1,0:T(8,128)(2,1)}, u32[]{:S(2)}) copy-start(bf16[768,3072]{1,0:T(8,128)(2,1)} %param.32) | copy-start | bytes 14155780
  44.3 1.4 copy-start.12
  44.3 1.4 copy-start.13
  44.7 1.5 copy-start.10
  45.8 4.3 %slice-start = ((s8[4718592]{0:T(1024)(128)(4,1)}), s8[4194304]{0:T(1024)(128)(4,1)S(1)}, s32[]{:S(2)}) async-start(s8[4718592]{0:T(1024)(128)(4,1)} %bitcast.48), calls=%async_computation | async-start | bytes 8388608
  46.1 3.9 %copy-start.7 = (bf16[512,768]{1,0:T(8,128)(2,1)}, bf16[512,768]{1,0:T(8,128)(2,1)S(1)}, u32[]{:S(2)}) copy-start(bf16[512,768]{1,0:T(8,128)(2,1)S(1)} %fusion.15.hidden_ref) | copy-start | bytes 2359300
  46.2 3.9 %copy-start.14 = (bf16[768]{0:T(1024)(128)(2,1)S(1)}, bf16[768]{0:T(1024)(128)(2,1)}, u32[]{:S(2)}) copy-start(bf16[768]{0:T(1024)(128)(2,1)} %param.35) | copy-start | bytes 4612
  46.2 3.9 %slice-start.1 = ((s8[4718592]{0:T(1024)(128)(4,1)}), s8[524288]{0:T(1024)(128)(4,1)S(1)}, s32[]{:S(2)}) async-start(s8[4718592]{0:T(1024)(128)(4,1)} %bitcast.48), calls=%async_computation.1 | async-start | bytes 1048576
  50.0 2.9 %copy-start.19 = (bf16[512,3072]{1,0:T(8,128)(2,1)}, bf16[512,3072]{1,0:T(8,128)(2,1)S(1)}, u32[]{:S(2)}) copy-start(bf16[512,3072]{1,0:T(8,128)(2,1)S(1)} %get-tuple-element.90.act_hbm) | copy-start | bytes 9437188
  52.9 0.7 copy-start.15
  52.9 1.1 copy-start.6
  53.2 2.1 %copy-start.16 = (bf16[768]{0:T(1024)(128)(2,1)S(1)}, bf16[768]{0:T(1024)(128)(2,1)}, u32[]{:S(2)}) copy-start(bf16[768]{0:T(1024)(128)(2,1)} %param.37) | copy-start | bytes 4612
  57.5 5.2 %copy-start.8 = (bf16[512,768]{1,0:T(8,128)(2,1)}, bf16[512,768]{1,0:T(8,128)(2,1)S(1)}, u32[]{:S(2)}) copy-start(bf16[512,768]{1,0:T(8,128)(2,1)S(1)} %get-tuple-element.83.branch_ref) | copy-start | bytes 2359300
  62.8 3.9 %copy-start.20 = (bf16[512,3072]{1,0:T(8,128)(2,1)}, bf16[512,3072]{1,0:T(8,128)(2,1)S(1)}, u32[]{:S(2)}) copy-start(bf16[512,3072]{1,0:T(8,128)(2,1)S(1)} %get-tuple-element.96.pre_hbm) | copy-start | bytes 9437188
  68.9 1.7 copy-start.9

commit v5 on v4

--- a/solution.py
+++ b/solution.py
@@ -233,7 +233,7 @@
     return pl.pallas_call(
         functools.partial(fwd_kernel, span, scale),
         grid=(block // span, width // 128),
-        out_shape=[jax.ShapeDtypeStruct((block, width), BF), jax.ShapeDtypeStruct((heads, block, table), BF)]
+        out_shape=[pltpu.HBM((block, width), BF), pltpu.HBM((heads, block, table), BF)]
         + [pltpu.HBM(shape, BF) for shape in kept],
         in_specs=[far] * 5 + [whole(arg.shape) for arg in small],
         out_specs=[pl.BlockSpec((span, 128), lambda t, h: (t, h)), pl.BlockSpec((2, span, table), lambda t, h: (h, t, 0))]
@@ -743,8 +743,7 @@
 
 
 def bwd_kernel(tq, scale, layout, q_ref, k_ref, v_ref, g_ref, rk_ref, rq_ref, p_ref, wk_ref, wq_ref, wv_ref,
-               act_hbm, branch_ref, hidden_ref, pre_hbm, ctx_hbm, attn_hbm, g_one_hbm, xt_hbm, picks_ref, *rest):
-    small_refs, rest = rest[:7], rest[7:]
+               act_hbm, branch_ref, hidden_ref, pre_hbm, ctx_hbm, attn_hbm, g_one_hbm, xt_hbm, picks_ref, small_ref, *rest):
     (dx_ref, packed_hbm,
                mask_ref, kjt_ref, dk_acc, dvt_acc, drkt_acc, drqt_acc,
                xt_ref, d_ref, rel_acc, vec_ref, dx_acc, sent_ref, got_ref, edge_sem,
@@ -814,11 +813,7 @@
         d_ref[...] = jnp.zeros_like(d_ref)
         rel_acc[...] = jnp.zeros_like(rel_acc)
         dx_acc[...] = jnp.zeros_like(dx_acc)
-        vec_ref[...] = jnp.zeros_like(vec_ref)
-        for n, ref in enumerate(small_refs[:6]):
-            vec_ref[n : n + 1, :] = ref[...][None]
-        for n in range(layout.fold):
-            vec_ref[6 + n : 7 + n, :] = small_refs[6][n * layout.width : (n + 1) * layout.width][None]
+        vec_ref[...] = small_ref[...]
 
     for kt in range(nk):
         kjt_ref[kt] = dot(k_ref[kt * tq : (kt + 1) * tq, :], flip, TN).astype(BF)
@@ -914,7 +909,7 @@
         in_specs=[col(block), col(ext), col(ext), col(block), col(rk.shape[0]), col(rq.shape[0]),
                   pl.BlockSpec((2, block, table), lambda h: (h, 0, 0)), col(width), col(width), col(width),
                   any_spec, whole(branch.shape), whole(hidden.shape), any_spec, any_spec, any_spec, any_spec, any_spec,
-                  whole(picks.shape)] + [pl.BlockSpec(part.shape, lambda h: (0,)) for part in small],
+                  whole(picks.shape), whole(small.shape)],
         out_specs=(whole((block, width)), any_spec),
         scratch_shapes=[
             pltpu.VMEM((4, span, span), BF),
@@ -939,7 +934,7 @@
         compiler_params=pltpu.CompilerParams(collective_id=0, has_side_effects=True, vmem_limit_bytes=60 << 20),
         cost_estimate=pl.CostEstimate(flops=50_000_000_000, bytes_accessed=20 << 20, transcendentals=0),
         name="attn_bwd_reduce",
-    )(*[pltpu.with_memory_space_constraint(arg, pltpu.HBM) for arg in (q, k, v)], g, *[pltpu.with_memory_space_constraint(arg, pltpu.HBM) for arg in (rk, rq, probs)], w_key, w_query, w_value, act, branch, hidden, pre, context, g_attn, g_one, pltpu.with_memory_space_constraint(xt, pltpu.HBM), picks, *small)
+    )(*[pltpu.with_memory_space_constraint(arg, pltpu.HBM) for arg in (q, k, v)], g, *[pltpu.with_memory_space_constraint(arg, pltpu.HBM) for arg in (rk, rq, probs)], w_key, w_query, w_value, act, branch, hidden, pre, context, g_attn, g_one, pltpu.with_memory_space_constraint(xt, pltpu.HBM), picks, small)
     return layout, outs
 
 
@@ -1008,18 +1003,136 @@
 
 
 NORM_EPS = 1e-07
-
-
-def norm_rows(values):
-    centred = values - jnp.mean(values, axis=-1, keepdims=True)
-    inv_std = lax.rsqrt(jnp.mean(centred * centred, axis=-1, keepdims=True) + NORM_EPS)
-    return centred * inv_std, inv_std
-
-
-def norm_back(grads, normed, inv_std):
-    first_mean = jnp.mean(grads, axis=-1, keepdims=True)
-    second_mean = jnp.mean(grads * normed, axis=-1, keepdims=True)
-    return inv_std * (grads - first_mean - normed * second_mean)
+STEP = 1536
+
+
+def mid_kernel(ctx_ref, x_ref, cot_ref, b_out, gain_attn, shift_attn, b_in, b_down, gain_ffn, shift_ffn, w_out_hbm, w_in_hbm, w_down_hbm,
+               out_ref, branch_ref, hidden_ref, gone_ref, gattn_ref, gctx_ref, vec_ref, act_hbm, pre_hbm,
+               w_out_ref, w_in_ref, w_down_ref, act_ref, pre_ref, slope_ref, full_ref, normed_ref, inv_ref, acc_ref, line_ref, in_sem, out_sem):
+    block, width = x_ref.shape
+    wide = w_in_ref.shape[1]
+    parts = wide // width
+    loads = [(w_out_hbm, w_out_ref)]
+    for n in range(parts):
+        loads.append((w_in_hbm.at[:, pl.ds(n * width, width)], w_in_ref.at[:, pl.ds(n * width, width)]))
+    loads.append((w_down_hbm, w_down_ref))
+    row_of = lambda ref: ref[...].astype(F32)[None]
+    total = lambda values: jnp.sum(values, axis=0, keepdims=True)
+    mean = lambda values: jnp.mean(values, axis=-1, keepdims=True)
+
+    def load(n):
+        return pltpu.make_async_copy(*loads[n], in_sem.at[n])
+
+    def norm(values):
+        centred = values - mean(values)
+        inv = lax.rsqrt(mean(centred * centred) + NORM_EPS)
+        return centred * inv, inv
+
+    def norm_back(grads, normed, inv):
+        return inv * (grads - mean(grads) - normed * mean(grads * normed))
+
+    for n in range(len(loads)):
+        load(n).start()
+    blocks = [slice(n, n + 128) for n in range(0, block, 128)]
+    load(0).wait()
+    for rows in blocks:
+        normed, inv = norm(x_ref[rows].astype(F32) + dot(ctx_ref[rows], w_out_ref[...]) + row_of(b_out))
+        normed_ref[rows], inv_ref[rows] = normed, inv
+        hidden = normed * row_of(gain_attn) + row_of(shift_attn)
+        full_ref[rows] = hidden
+        hidden_ref[rows] = hidden.astype(BF)
+    for n in range(1, len(loads)):
+        load(n).wait()
+    acc_ref[...] = full_ref[...] + row_of(b_down)
+
+    def up(n, carry):
+        cols = pl.ds(pl.multiple_of(n * STEP, STEP), STEP)
+        pre = dot(hidden_ref[...], w_in_ref[:, cols]) + b_in[cols].astype(F32)[None]
+        phi = 0.5 + 0.5 * lax.erf(pre * (0.5**0.5))
+        act = (pre * phi).astype(BF)
+        act_ref[:, cols] = act
+        slope_ref[:, cols] = phi + pre * (jnp.exp(-0.5 * pre * pre) * ((2.0 * math.pi) ** -0.5))
+        acc_ref[...] += dot(act, w_down_ref[cols, :])
+        return carry
+
+    lax.fori_loop(0, wide // STEP, up, 0, unroll=1)
+    act_copy = pltpu.make_async_copy(act_ref, act_hbm, out_sem.at[0])
+    act_copy.start()
+    gain, shift, bias = 0.0, 0.0, 0.0
+    for rows in blocks:
+        normed, inv = norm(acc_ref[rows])
+        out_ref[rows] = (normed * row_of(gain_ffn) + row_of(shift_ffn)).astype(BF)
+        grads = cot_ref[rows].astype(F32)
+        gain, shift = gain + total(grads * normed), shift + total(grads)
+        grad_two = norm_back(grads * row_of(gain_ffn), normed, inv)
+        acc_ref[rows] = grad_two
+        branch = grad_two.astype(BF)
+        branch_ref[rows] = branch
+        bias = bias + total(branch.astype(F32))
+    vec_ref[...] = jnp.zeros_like(vec_ref)
+    vec_ref[3:4], vec_ref[4:5], vec_ref[5:6] = bias, gain, shift
+
+    def down(n, carry):
+        cols = pl.ds(pl.multiple_of(n * STEP, STEP), STEP)
+        pre = (dot(branch_ref[...], w_down_ref[cols, :], NT) * slope_ref[:, cols]).astype(BF)
+        pre_ref[:, cols] = pre
+        line_ref[0:1, cols] = total(pre.astype(F32))
+        acc_ref[...] += dot(pre, w_in_ref[:, cols], NT)
+        return carry
+
+    lax.fori_loop(0, wide // STEP, down, 0, unroll=1)
+    pre_copy = pltpu.make_async_copy(pre_ref, pre_hbm, out_sem.at[1])
+    pre_copy.start()
+    for n in range(parts):
+        vec_ref[6 + n : 7 + n] = line_ref[0:1, n * width : (n + 1) * width]
+    gain, shift, bias = 0.0, 0.0, 0.0
+    for rows in blocks:
+        grads, normed = acc_ref[rows], normed_ref[rows]
+        gain, shift = gain + total(grads * normed), shift + total(grads)
+        grad_one = norm_back(grads * row_of(gain_attn), normed, inv_ref[rows])
+        gone_ref[rows] = grad_one
+        grad_attn = grad_one.astype(BF)
+        gattn_ref[rows] = grad_attn
+        bias = bias + total(grad_attn.astype(F32))
+        gctx_ref[rows] = dot(grad_attn, w_out_ref[...], NT).astype(BF)
+    vec_ref[0:1], vec_ref[1:2], vec_ref[2:3] = bias, gain, shift
+    act_copy.wait()
+    pre_copy.wait()
+
+
+def middle(context, x, cotangent, small, w_out, w_in, w_down):
+    block, width = x.shape
+    wide = w_in.shape[1]
+    far = pl.BlockSpec(memory_space=pltpu.HBM)
+    whole = lambda arg: pl.BlockSpec(arg.shape, lambda t: (0,) * len(arg.shape), pipeline_mode=pl.Buffered(1))
+    tall = (block, width)
+    args = [context, x, cotangent, *small]
+    outs = [jax.ShapeDtypeStruct(tall, BF)]
+    outs += [pltpu.HBM(dims, kind) for dims, kind in ((tall, BF), (tall, BF), (tall, F32), (tall, BF), (tall, BF), ((16, width), F32))]
+    return pl.pallas_call(
+        mid_kernel,
+        grid=(1,),
+        out_shape=outs + [pltpu.HBM((block, wide), BF)] * 2,
+        in_specs=[whole(arg) for arg in args] + [far] * 3,
+        out_specs=[whole(out) for out in outs] + [far] * 2,
+        scratch_shapes=[
+            pltpu.VMEM((width, width), BF),
+            pltpu.VMEM((width, wide), BF),
+            pltpu.VMEM((wide, width), BF),
+            pltpu.VMEM((block, wide), BF),
+            pltpu.VMEM((block, wide), BF),
+            pltpu.VMEM((block, wide), F32),
+            pltpu.VMEM(tall, F32),
+            pltpu.VMEM(tall, F32),
+            pltpu.VMEM((block, 1), F32),
+            pltpu.VMEM(tall, F32),
+            pltpu.VMEM((8, wide), F32),
+            pltpu.SemaphoreType.DMA((2 + wide // width,)),
+            pltpu.SemaphoreType.DMA((2,)),
+        ],
+        compiler_params=pltpu.CompilerParams(vmem_limit_bytes=56 << 20),
+        name="middle",
+    )(*args, *[pltpu.with_memory_space_constraint(arg, pltpu.HBM) for arg in (w_out, w_in, w_down)])
 
 
 def local(
@@ -1055,39 +1168,13 @@
         span, x, rel_table, w_query, w_key, w_value, b_query, b_key, b_value, qid[:, None], kid[None]
     )
 
-    residual_one = x.astype(F32) + dot(context, w_out) + b_out
-    normed_one, inv_one = norm_rows(residual_one)
-    hidden = normed_one * gain_attn + shift_attn
-    hidden_low = hidden.astype(BF)
-    pre_act = dot(hidden_low, w_in) + b_in
-    phi = 0.5 * (1.0 + lax.erf(pre_act * (0.5**0.5)))
-    act_low = (pre_act * phi).astype(BF)
-    slope = phi + pre_act * (jnp.exp(-0.5 * pre_act * pre_act) * ((2.0 * math.pi) ** -0.5))
-    residual_two = hidden + dot(act_low, w_down) + b_down
-    normed_two, inv_two = norm_rows(residual_two)
-    output = (normed_two * gain_ffn + shift_ffn).astype(BF)
-
-    grad_out = cotangent[0].astype(F32)
-    gain_ffn_grad = jnp.sum(grad_out * normed_two, axis=0)
-    shift_ffn_grad = jnp.sum(grad_out, axis=0)
-    grad_two = norm_back(grad_out * gain_ffn, normed_two, inv_two)
-    grad_branch = grad_two.astype(BF)
-    down_bias_grad = jnp.sum(grad_branch.astype(F32), axis=0)
-    grad_pre = (dot(grad_branch, w_down, NT) * slope).astype(BF)
-    in_bias_grad = jnp.sum(grad_pre.astype(F32), axis=0)
-    grad_hidden = grad_two + dot(grad_pre, w_in, NT)
-    gain_attn_grad = jnp.sum(grad_hidden * normed_one, axis=0)
-    shift_attn_grad = jnp.sum(grad_hidden, axis=0)
-    grad_one = norm_back(grad_hidden * gain_attn, normed_one, inv_one)
-    grad_attn = grad_one.astype(BF)
-    out_bias_grad = jnp.sum(grad_attn.astype(F32), axis=0)
-    grad_context = dot(grad_attn, w_out, NT).astype(BF)
-
+    output, grad_branch, hidden_low, grad_one, grad_attn, grad_context, small, act_low, grad_pre = middle(
+        context, x, cotangent[0], [b_out, gain_attn, shift_attn, b_in, b_down, gain_ffn, shift_ffn], w_out, w_in, w_down
+    )
     share, lanes = lax.axis_size("batch"), lax.axis_size("seq")
     rel_rows = 2 * span // (share * lanes)
     order = np.arange(2 * span).reshape(lanes, share, rel_rows).transpose(1, 0, 2).reshape(-1)
     picks = jnp.asarray((2 * span - 1 - order)[:, None] == np.arange(2 * span)[None], BF)
-    small = [out_bias_grad, gain_attn_grad, shift_attn_grad, down_bias_grad, gain_ffn_grad, shift_ffn_grad, in_bias_grad]
     layout, outs = attn_bwd(
         span, q, k, v, grad_context, rk, rq, probs, w_key, w_query, w_value, act_low, grad_branch, hidden_low, grad_pre,
         context, grad_attn, grad_one, xt, picks, small,

time: 202 us -> 195 us (0.965)
  Pallas kernels: 167 us -> 191 us
  matrix products: 18.4 us -> 0 us
  other arithmetic: 7.4 us -> 0 us
  local copies, waits for them, and re-layouts: 7.75 us -> 2.98 us
    pallas_call x0 -> x1, Pallas kernels: none -> 23.6 us  [middle(): pl.pallas_call(mid_kernel, grid=(1,), out_shape=outs + [pltpu.HBM((block,...]
    dot_general x6 -> x0, matrix products: 18.4 us -> none  [dot(): return lax.dot_general(a, b, dims, preferred_element_type=F32)]
    reduce_sum x6 -> x0, other arithmetic: 7.04 us -> none  [the longest x1 2.26 us: local(): out_bias_grad = jnp.sum(grad_attn.astype(F32), axis=0)]
    unnamed x46 -> x6, local copies, waits for them, and re-layouts: 6.72 us -> 2.04 us
where the time goes in v5:
time: 195 us
  Pallas kernels  191 us (98%)
  local copies, waits for them, and re-layouts  2.98 us (2%)
    pallas_call x1, Pallas kernels, attn_bwd(): pl.pallas_call(functools.partial(bwd_kernel, span, scale, layout), grid=(...  126 us
    pallas_call x1, Pallas kernels, attn_fwd(): pl.pallas_call(functools.partial(fwd_kernel, span, scale), grid=(block //...  37.2 us
    pallas_call x1, Pallas kernels, middle(): pl.pallas_call(mid_kernel, grid=(1,), out_shape=outs + [pltpu.HBM((block,...  23.6 us
    pallas_call x1, Pallas kernels, unpack(): pl.pallas_call(functools.partial(unpack_kernel, layout), out_shape=shapes...  4.37 us

profile of v5, /device:TPU:8, one launch (start us, length us, event | category | flops | bytes accessed | tf_op | source)
XLA Modules:
  0.0 194.6 jit_solution(4286135797577106564)
XLA Ops:
  0.7 0.8 pad_dynamic-slice_fusion
  1.4 0.1 copy.40.qid_ref
  1.6 0.0 copy-start
  1.6 0.7 copy-done
  2.3 0.0 copy-start.1
  2.3 0.7 copy-done.1
  3.0 0.0 copy-start.2
  3.0 0.7 copy-done.2
  3.7 37.2 %attn_fwd.1 = (bf16[512,768]{1,0:T(8,128)(2,1)}, bf16[12,512,512]{2,1,0:T(8,128)(2,1)}, bf16[512,768]{1,0:T(8,128)(2,1)}, bf16[1024,768]{1,0:T(8,128)(2,1)}, bf1...) custom-call(bf16[512,768]{1,0:T(8,128)(2,1)} %bitcast.8, ...), custom_call_target="tpu_custom_call" | custom-call | flops 20000000000 | bytes 20971520 | tf_op jit(solution)/shard_map/attn_fwd/pallas_call | solution.py:233
  40.9 23.6 %middle.1 = (bf16[512,768]{1,0:T(8,128)(2,1)}, bf16[512,768]{1,0:T(8,128)(2,1)}, bf16[512,768]{1,0:T(8,128)(2,1)}, f32[512,768]{1,0:T(8,128)}, bf16[512,768]{1,0...) custom-call(bf16[512,768]{1,0:T(8,128)(2,1)} %get-tuple-element.56.c, ...), custom_call_target="tpu_custom_call" | custom-call | tf_op jit(solution)/shard_map/middle/pallas_call | solution.py:1112
  64.5 125.6 %attn_bwd_reduce.1 = (f32[512,768]{1,0:T(8,128)}, bf16[96,10240]{1,0:T(8,128)(2,1)}) custom-call(bf16[512,768]{1,0:T(8,128)(2,1)} %get-tuple-element.58.q_ref, bf16[1024,768]{1,0:T(8,128)(2,1)} %get-tuple-element.59.k_ref, bf16[1024,768]{1,0:T(8,128)(2,1)} %get-tuple-element.60.v_ref, bf16[512,768]{1,0:T(8,128)(2,1)} %get-tuple-element.61.g_ref, ...), custom_call_target="tpu_custom_call" | custom-call | flops 49999998976 | bytes 20971520 | tf_op jit(solution)/shard_map/attn_bwd_reduce/pallas_call | solution.py:902
  190.1 4.4 %unpack.1 = (f32[512,768]{1,0:T(8,128)}, f32[384,768]{1,0:T(8,128)}, f32[96,3072]{1,0:T(8,128)}, f32[96,768]{1,0:T(8,128)}, f32[96,768]{1,0:T(8,128)}, /*index=5...) custom-call(bf16[96,10240]{1,0:T(8,128)(2,1)} %get-tuple-element.73., ...), custom_call_target="tpu_custom_call" | custom-call | tf_op jit(solution)/shard_map/unpack/pallas_call | solution.py:989
  (1 shorter events, 0.0 us)
Async XLA Ops:
  1.6 0.7 copy-start
  2.3 0.7 copy-start.1
  3.0 0.7 copy-start.2

commit v6 on v5

--- a/solution.py
+++ b/solution.py
@@ -250,7 +250,7 @@
         compiler_params=pltpu.CompilerParams(collective_id=1, has_side_effects=True, vmem_limit_bytes=44 << 20),
         cost_estimate=pl.CostEstimate(flops=20_000_000_000, bytes_accessed=20 << 20, transcendentals=heads * block * table),
         name="attn_fwd",
-    )(*[pltpu.with_memory_space_constraint(arg, pltpu.HBM) for arg in (x, rel_table, w_key, w_query, w_value)], *small)
+    )(*[pltpu.with_memory_space_constraint(arg, pltpu.HBM) for arg in (x, rel_table, w_key, w_query, w_value, b_query, b_key, b_value)], qid, kid)
 
 
 def bwd_tile(n, scale, qt, q_ref, k_ref, v_ref, g_ref, rk_ref, rq_ref, p_ref, mask_ref, kjt_ref, dk_acc, dvt_acc, drkt_acc, drqt_acc):
@@ -673,35 +673,36 @@
         steps = {
             1: [rest.s0],
             2: [into.s0],
-            3: [down.s0],
-            7: [one.core],
+            4: [down.s0],
             8: [into.s1],
-            9: [down.s1, rest.s1],
+            9: [rest.s1],
+            10: [down.s1, one.core],
             11: [into.z],
-            12: [one.s0, two.core],
-            13: [rest.z, two.s0],
-            14: [down.z, into.out, one.s1],
-            15: [two.s1],
-            16: [into.out2, rest.out, three.core, one.z],
-            17: [two.z],
+            12: [rest.z, one.s0, two.core],
+            13: [two.s0, down.z],
+            14: [one.s1],
+            15: [three.core, into.out],
+            16: [three.z, into.out2, two.s1],
+            17: [rest.out],
         }
         last = [
             far.core,
-            three.z,
             far.s0,
+            three.s0,
+            one.z,
             down.out,
-            two.out,
             far.s1,
+            two.z,
             one.out,
-            three.s0,
+            three.s1,
             down.out2,
             far.z,
-            three.s1,
+            rest.out2,
+            three.out,
+            two.out,
+            one.out2,
+            far.out,
             two.out2,
-            one.out2,
-            three.out,
-            far.out,
-            rest.out2,
             three.out2,
             far.out2,
         ]

time: 195 us -> 193 us (0.990); the launches traced: 195 us -> 191 us
  local copies, waits for them, and re-layouts: 2.98 us -> 0.93 us
  Pallas kernels: 191 us -> 189 us
    pallas_call x1, Pallas kernels: 126 us -> 123 us  [attn_bwd(): pl.pallas_call(functools.partial(bwd_kernel, span, scale, layout), grid=(...]
    unnamed x6 -> x0, local copies, waits for them, and re-layouts: 2.04 us -> none
where the time goes in v6:
time: 193 us; the launch traced here: 191 us
  Pallas kernels  189 us (98%)
    pallas_call x1, Pallas kernels, attn_bwd(): pl.pallas_call(functools.partial(bwd_kernel, span, scale, layout), grid=(...  123 us
    pallas_call x1, Pallas kernels, attn_fwd(): pl.pallas_call(functools.partial(fwd_kernel, span, scale), grid=(block //...  38.1 us
    pallas_call x1, Pallas kernels, middle(): pl.pallas_call(mid_kernel, grid=(1,), out_shape=outs + [pltpu.HBM((block,...  23.6 us
    pallas_call x1, Pallas kernels, unpack(): pl.pallas_call(functools.partial(unpack_kernel, layout), out_shape=shapes...  4.37 us

profile of v6, /device:TPU:8, one launch (start us, length us, event | category | flops | bytes accessed | tf_op | source)
XLA Modules:
  0.0 190.5 jit_solution(8465414180196263680)
XLA Ops:
  0.7 0.8 pad_dynamic-slice_fusion
  1.4 0.1 copy.40.qid_ref
  1.6 38.1 %attn_fwd.1 = (bf16[512,768]{1,0:T(8,128)(2,1)}, bf16[12,512,512]{2,1,0:T(8,128)(2,1)}, bf16[512,768]{1,0:T(8,128)(2,1)}, bf16[1024,768]{1,0:T(8,128)(2,1)}, bf1...) custom-call(bf16[512,768]{1,0:T(8,128)(2,1)} %bitcast.8, ...), custom_call_target="tpu_custom_call" | custom-call | flops 20000000000 | bytes 20971520 | tf_op jit(solution)/shard_map/attn_fwd/pallas_call | solution.py:233
  39.7 23.6 %middle.1 = (bf16[512,768]{1,0:T(8,128)(2,1)}, bf16[512,768]{1,0:T(8,128)(2,1)}, bf16[512,768]{1,0:T(8,128)(2,1)}, f32[512,768]{1,0:T(8,128)}, bf16[512,768]{1,0...) custom-call(bf16[512,768]{1,0:T(8,128)(2,1)} %get-tuple-element.56.c, ...), custom_call_target="tpu_custom_call" | custom-call | tf_op jit(solution)/shard_map/middle/pallas_call | solution.py:1113
  63.3 122.7 %attn_bwd_reduce.1 = (f32[512,768]{1,0:T(8,128)}, bf16[96,10240]{1,0:T(8,128)(2,1)}) custom-call(bf16[512,768]{1,0:T(8,128)(2,1)} %get-tuple-element.58.q_ref, bf16[1024,768]{1,0:T(8,128)(2,1)} %get-tuple-element.59.k_ref, bf16[1024,768]{1,0:T(8,128)(2,1)} %get-tuple-element.60.v_ref, bf16[512,768]{1,0:T(8,128)(2,1)} %get-tuple-element.61.g_ref, ...), custom_call_target="tpu_custom_call" | custom-call | flops 49999998976 | bytes 20971520 | tf_op jit(solution)/shard_map/attn_bwd_reduce/pallas_call | solution.py:903
  186.0 4.4 %unpack.1 = (f32[512,768]{1,0:T(8,128)}, f32[384,768]{1,0:T(8,128)}, f32[96,3072]{1,0:T(8,128)}, f32[96,768]{1,0:T(8,128)}, f32[96,768]{1,0:T(8,128)}, /*index=5...) custom-call(bf16[96,10240]{1,0:T(8,128)(2,1)} %get-tuple-element.73., ...), custom_call_target="tpu_custom_call" | custom-call | tf_op jit(solution)/shard_map/unpack/pallas_call | solution.py:990
  (1 shorter events, 0.0 us)

commit v7 on v6

--- a/solution.py
+++ b/solution.py
@@ -331,7 +331,10 @@
         peers += [self.at(toggled(self.s, step), self.b) for step in range(1, self.ns)]
         for peer in peers:
             pl.semaphore_signal(barrier, inc=1, device_id=peer, device_id_type=MESH)
-        pl.semaphore_wait(barrier, len(peers))
+        self.greeted = len(peers)
+
+    def meet(self):
+        pl.semaphore_wait(pltpu.get_barrier_semaphore(), self.greeted)
 
 
 class Chunk:
@@ -789,14 +792,15 @@
 
     @pl.when(pair == 0)
     def _():
+        layout.mesh.greet()
         for m in range(2):
             load(m).start()
-        layout.mesh.greet()
         m = 0
         for n in range(layout.fold):
             load(m + 2).start()
             layout.store_down(n, dot(loaded(m), branch_ref[...], TN).astype(BF))
             m += 1
+        layout.mesh.meet()
         layout.down.core()
         for n in range(3):
             if m + 2 < len(loads):

time: 193 us -> 193 us (level)
  no operation moved by 1% of the time
where the time goes in v7:
time: 193 us; the launch traced here: 190 us
  Pallas kernels  189 us (98%)
    pallas_call x1, Pallas kernels, attn_bwd(): pl.pallas_call(functools.partial(bwd_kernel, span, scale, layout), grid=(...  122 us
    pallas_call x1, Pallas kernels, attn_fwd(): pl.pallas_call(functools.partial(fwd_kernel, span, scale), grid=(block //...  38.1 us
    pallas_call x1, Pallas kernels, middle(): pl.pallas_call(mid_kernel, grid=(1,), out_shape=outs + [pltpu.HBM((block,...  23.6 us
    pallas_call x1, Pallas kernels, unpack(): pl.pallas_call(functools.partial(unpack_kernel, layout), out_shape=shapes...  4.37 us

profile of v7, /device:TPU:8, one launch (start us, length us, event | category | flops | bytes accessed | tf_op | source)
XLA Modules:
  0.0 190.3 jit_solution(14476438532797290692)
XLA Ops:
  0.7 0.8 pad_dynamic-slice_fusion
  1.4 0.1 copy.40.qid_ref
  1.6 38.1 %attn_fwd.1 = (bf16[512,768]{1,0:T(8,128)(2,1)}, bf16[12,512,512]{2,1,0:T(8,128)(2,1)}, bf16[512,768]{1,0:T(8,128)(2,1)}, bf16[1024,768]{1,0:T(8,128)(2,1)}, bf1...) custom-call(bf16[512,768]{1,0:T(8,128)(2,1)} %bitcast.8, ...), custom_call_target="tpu_custom_call" | custom-call | flops 20000000000 | bytes 20971520 | tf_op jit(solution)/shard_map/attn_fwd/pallas_call | solution.py:233
  39.7 23.6 %middle.1 = (bf16[512,768]{1,0:T(8,128)(2,1)}, bf16[512,768]{1,0:T(8,128)(2,1)}, bf16[512,768]{1,0:T(8,128)(2,1)}, f32[512,768]{1,0:T(8,128)}, bf16[512,768]{1,0...) custom-call(bf16[512,768]{1,0:T(8,128)(2,1)} %get-tuple-element.56.c, ...), custom_call_target="tpu_custom_call" | custom-call | tf_op jit(solution)/shard_map/middle/pallas_call | solution.py:1117
  63.3 122.5 %attn_bwd_reduce.1 = (f32[512,768]{1,0:T(8,128)}, bf16[96,10240]{1,0:T(8,128)(2,1)}) custom-call(bf16[512,768]{1,0:T(8,128)(2,1)} %get-tuple-element.58.q_ref, bf16[1024,768]{1,0:T(8,128)(2,1)} %get-tuple-element.59.k_ref, bf16[1024,768]{1,0:T(8,128)(2,1)} %get-tuple-element.60.v_ref, bf16[512,768]{1,0:T(8,128)(2,1)} %get-tuple-element.61.g_ref, ...), custom_call_target="tpu_custom_call" | custom-call | flops 49999998976 | bytes 20971520 | tf_op jit(solution)/shard_map/attn_bwd_reduce/pallas_call | solution.py:907
  185.8 4.4 %unpack.1 = (f32[512,768]{1,0:T(8,128)}, f32[384,768]{1,0:T(8,128)}, f32[96,3072]{1,0:T(8,128)}, f32[96,768]{1,0:T(8,128)}, f32[96,768]{1,0:T(8,128)}, /*index=5...) custom-call(bf16[96,10240]{1,0:T(8,128)(2,1)} %get-tuple-element.73., ...), custom_call_target="tpu_custom_call" | custom-call | tf_op jit(solution)/shard_map/unpack/pallas_call | solution.py:994
  (1 shorter events, 0.0 us)
